TPU v7x, 32 devices: a whole 2x2x4 slice. The times are simulated.
32 devices in a mesh: layer: 2 (over core), prow: 4 (over z), pcol: 4 (over y, x).
Axes of the slice: x: 2, y: 2, z: 4, core: 2. Of those that a mesh axis runs over, the one named last changes fastest.
Arguments:
- diag_inverse: float32 [2, 3, 2048, 2048], P('layer', None, 'prow', 'pcol'), may hold values from -1 to 1, as said below
- root_inverse: float32 [2048, 2048], P('prow', 'pcol'), may hold values from -1 to 1, as said below
- coupling: float32 [2, 5, 2048, 2048], P('layer', None, 'prow', 'pcol'), may hold values from -0.0625 to 0.0625
- tile_mask: int32 [2, 5, 16, 16], P('layer'), may hold values 0 or 1
- sketch: float32 [2, 3, 2048, 256], P('layer', None, 'prow'), may hold values from -6 to 6
- root_sketch: float32 [2048, 256], P('prow'), may hold values from -6 to 6
Outputs:
- solution: float32 [2, 3, 2048, 256], P('layer', None, 'prow')
- root_solution: float32 [2048, 256], P('prow')
Inputs may be any that keep to these rules, and one draw needn't show every extreme that they name: `diag_inverse`: lower triangular. `root_inverse`: lower triangular.
All inputs are finite; a program needn't handle non-finite values. No bound on the sum of `tile_mask` on one device may be relied on, other than what follows from the above.
Results may differ from a plain program's by a relative error of at most 0.0001.
Values sent between devices are 32-bit elements; how exact they have to be, the bound alone decides.
No kernel may reach another device: no remote copies, remote signals or barrier semaphores. Data moves between devices by JAX's collectives and lax.ppermute only.
A program may use at most 64 MiB of HBM per device.

v0:
```python
import jax
import jax.numpy as jnp
from jax import lax
from jax.sharding import PartitionSpec as P

TILE = 128


def broadcast(block, axis, owner):
    block = jnp.where(lax.axis_index(axis) == owner, block, jnp.zeros_like(block))
    return lax.psum(block, axis)


def forward_product(matrix, vector):
    return jnp.einsum("nij,njk->nik", matrix, vector, precision=lax.Precision.HIGHEST)


def transpose_product(matrix, vector):
    return jnp.einsum("nij,nik->njk", matrix, vector, precision=lax.Precision.HIGHEST)


def column_panel(vector):
    group_ratio = lax.axis_size("pcol") // lax.axis_size("prow")
    col_index = lax.axis_index("pcol")
    received = broadcast(vector, "prow", col_index // group_ratio)
    col_width = vector.shape[1] // group_ratio
    return lax.dynamic_slice_in_dim(received, col_index % group_ratio * col_width, col_width, 1)


def column_total(partial_value):
    return lax.psum(partial_value, "pcol")


def regroup(column_rows):
    group_ratio = lax.axis_size("pcol") // lax.axis_size("prow")
    row_index = lax.axis_index("prow")
    col_width = column_rows.shape[1]
    complete = lax.all_gather(column_rows, "pcol", axis=1, tiled=True)
    return lax.dynamic_slice_in_dim(
        complete, row_index * (col_width * group_ratio), col_width * group_ratio, 1
    )


def row_total(partial_value):
    return regroup(lax.psum(partial_value, "prow"))


def local_mask(tile_mask, rows_here, cols_here):
    row_tiles = (lax.axis_index("prow") * rows_here + lax.iota(jnp.int32, rows_here)) // TILE
    col_tiles = (lax.axis_index("pcol") * cols_here + lax.iota(jnp.int32, cols_here)) // TILE
    table = jnp.take(tile_mask[0], row_tiles, axis=1)
    table = jnp.take(table, col_tiles, axis=2)
    return table.astype(jnp.float32)


def per_device(diag_inverse, root_inverse, coupling, tile_mask, sketch, root_sketch):
    layer_inverse = diag_inverse[0]
    rows_here = coupling.shape[2]
    cols_here = coupling.shape[3]
    blocks = coupling[0] * local_mask(tile_mask, rows_here, cols_here)
    rhs_local = sketch[0]
    leaves = column_total(forward_product(layer_inverse[0:2], column_panel(rhs_local[0:2])))
    fed_leaves = column_panel(leaves)
    mid_part = forward_product(blocks[0:2], fed_leaves)
    root_part = forward_product(blocks[2:4], fed_leaves)
    mid_rhs = rhs_local[2] - column_total(mid_part[0] + mid_part[1])
    middle = column_total(forward_product(layer_inverse[2:3], column_panel(mid_rhs[None])))[0]
    upper_part = forward_product(blocks[4:5], column_panel(middle[None]))[0]
    update = lax.psum(root_part[0] + root_part[1] + upper_part, ("layer", "pcol"))
    root_forward = column_total(
        forward_product(root_inverse[None], column_panel((root_sketch - update)[None]))
    )[0]
    root_solution = row_total(transpose_product(root_inverse[None], root_forward[None]))[0]
    spread_root = jnp.broadcast_to(root_solution, (3,) + root_solution.shape)
    back_terms = row_total(transpose_product(blocks[2:5], spread_root))
    mid_back = middle - back_terms[2]
    mid_solution = row_total(transpose_product(layer_inverse[2:3], mid_back[None]))[0]
    spread_mid = jnp.broadcast_to(mid_solution, (2,) + mid_solution.shape)
    leaf_terms = row_total(transpose_product(blocks[0:2], spread_mid))
    leaf_back = leaves - leaf_terms - back_terms[0:2]
    leaf_solution = row_total(transpose_product(layer_inverse[0:2], leaf_back))
    solution = jnp.concatenate([leaf_solution, mid_solution[None]], axis=0)[None]
    return (solution, root_solution)


def solution(mesh):
    in_specs = (
        P("layer", None, "prow", "pcol"),
        P("prow", "pcol"),
        P("layer", None, "prow", "pcol"),
        P("layer", None, None, None),
        P("layer", None, "prow", None),
        P("prow", None),
    )
    out_specs = (P("layer", None, "prow", None), P("prow", None))
    return jax.shard_map(
        per_device, mesh=mesh, in_specs=in_specs, out_specs=out_specs, check_vma=False
    )
```

profile of v0, /device:TPU:0, one launch (start us, length us, event | category | flops | bytes accessed | tf_op | source)
XLA Modules:
  0.0 1045.1 jit_solution(8067346142498596732)
XLA Ops:
  10.1 55.4 %all-reduce.16.cloned.1.call-done = f32[2,512,256]{1,2,0:T(8,128)} async-done(((f32[2,512,256]{1,2,0:T(8,128)}), f32[2,512,256]{1,2,0:T(8,128)}) %all-reduce.16.cloned.1.call-update) | async-done | bytes 1048592 | tf_op jit(solution)/shard_map/psum | solution.py:11
  65.5 4.8 fusion.6
  73.2 49.2 %all-reduce.18.cloned.1.call-done = f32[2,512,256]{1,2,0:T(8,128)} async-done(((f32[2,512,256]{1,2,0:T(8,128)}), f32[2,512,256]{1,2,0:T(8,128)}) %all-reduce.18.cloned.1.call-update) | async-done | bytes 1048592 | tf_op jit(solution)/shard_map/psum | solution.py:31
  124.8 3.4 select_bitcast_fusion
  129.0 4.4 gather_fusion.1
  133.4 8.8 copy.17
  142.2 7.9 bitcast_multiply_fusion
  150.1 27.3 %all-reduce.20.cloned.1.call-done = f32[2,512,256]{1,2,0:T(8,128)} async-done(((f32[2,512,256]{1,2,0:T(8,128)}), f32[2,512,256]{1,2,0:T(8,128)}) %all-reduce.20.cloned.1.call-update) | async-done | bytes 1048592 | tf_op jit(solution)/shard_map/psum | solution.py:11
  177.4 3.8 fusion.35
  182.2 44.8 %all-reduce.22.cloned.1.call-done = f32[512,256]{1,0:T(8,128)} async-done(((f32[512,256]{1,0:T(8,128)}), f32[512,256]{1,0:T(8,128)}) %all-reduce.22.cloned.1.call-update) | async-done | bytes 524304 | tf_op jit(solution)/shard_map/psum | solution.py:31
  229.1 39.0 %all-reduce.24.cloned.1.call-done = f32[512,256]{1,0:T(8,128)} async-done(((f32[512,256]{1,0:T(8,128)}), f32[512,256]{1,0:T(8,128)}) %all-reduce.24.cloned.1.call-update) | async-done | bytes 524304 | tf_op jit(solution)/shard_map/psum | solution.py:11
  268.1 4.0 convolution_bitcast_fusion.3
  272.2 45.4 %all-reduce.26.cloned.1.call-done = f32[1,512,256]{1,2,0:T(8,128)} async-done(((f32[1,512,256]{1,2,0:T(8,128)}), f32[1,512,256]{1,2,0:T(8,128)}) %all-reduce.26.cloned.1.call-update) | async-done | bytes 524304 | tf_op jit(solution)/shard_map/psum | solution.py:31
  319.8 3.6 fusion.36
  323.4 35.5 %all-reduce.28.cloned.1.call-done = f32[512,256]{0,1:T(8,128)} async-done(((f32[512,256]{0,1:T(8,128)}), f32[512,256]{0,1:T(8,128)}) %all-reduce.28.cloned.1.call-update) | async-done | bytes 524304 | tf_op jit(solution)/shard_map/psum | solution.py:11
  362.1 55.0 %all-reduce.30.cloned.1.call-done = f32[512,256]{1,0:T(8,128)} async-done(((f32[512,256]{1,0:T(8,128)}), f32[512,256]{1,0:T(8,128)}) %all-reduce.30.cloned.1.call-update) | async-done | bytes 524304 | tf_op jit(solution)/shard_map/psum | solution.py:69
  419.1 38.7 %all-reduce.32.cloned.1.call-done = f32[512,256]{1,0:T(8,128)} async-done(((f32[512,256]{1,0:T(8,128)}), f32[512,256]{1,0:T(8,128)}) %all-reduce.32.cloned.1.call-update) | async-done | bytes 524304 | tf_op jit(solution)/shard_map/psum | solution.py:11
  457.8 3.7 convolution_bitcast_fusion.2
  461.6 45.4 %all-reduce.34.cloned.1.call-done = f32[512,256]{0,1:T(8,128)} async-done(((f32[512,256]{0,1:T(8,128)}), f32[512,256]{0,1:T(8,128)}) %all-reduce.34.cloned.1.call-update) | async-done | bytes 524304 | tf_op jit(solution)/shard_map/psum | solution.py:31
  510.0 38.4 %all-reduce.36.cloned.1.call-done = f32[1,512,256]{1,2,0:T(8,128)} async-done(((f32[1,512,256]{1,2,0:T(8,128)}), f32[1,512,256]{1,2,0:T(8,128)}) %all-reduce.36.cloned.1.call-update) | async-done | bytes 524304 | tf_op jit(solution)/shard_map/psum | solution.py:45
  548.5 37.1 %all-gather.6.cloned.1.call-done = f32[1,2048,256]{1,2,0:T(8,128)} async-done(((f32[1,512,256]{1,2,0:T(8,128)}), f32[1,2048,256]{1,2,0:T(8,128)}) %all-gather.6.cloned.1.call-update) | async-done | bytes 2097168 | tf_op jit(solution)/shard_map/all_gather | solution.py:38
  586.9 6.1 fusion.18
  593.1 69.2 %all-reduce.38.cloned.1.call-done = f32[3,512,256]{1,2,0:T(8,128)} async-done(((f32[3,512,256]{1,2,0:T(8,128)}), f32[3,512,256]{1,2,0:T(8,128)}) %all-reduce.38.cloned.1.call-update) | async-done | bytes 1572880 | tf_op jit(solution)/shard_map/psum | solution.py:45
  662.4 71.0 %all-gather.8.cloned.1.call-done = f32[3,2048,256]{1,2,0:T(8,128)} async-done(((f32[3,512,256]{1,2,0:T(8,128)}), f32[3,2048,256]{1,2,0:T(8,128)}) %all-gather.8.cloned.1.call-update) | async-done | bytes 6291472 | tf_op jit(solution)/shard_map/all_gather | solution.py:38
  736.7 38.4 %all-reduce.40.cloned.1.call-done = f32[1,512,256]{1,2,0:T(8,128)} async-done(((f32[1,512,256]{1,2,0:T(8,128)}), f32[1,512,256]{1,2,0:T(8,128)}) %all-reduce.40.cloned.1.call-update) | async-done | bytes 524304 | tf_op jit(solution)/shard_map/psum | solution.py:45
  775.4 36.9 %all-gather.10.cloned.1.call-done = f32[1,2048,256]{1,2,0:T(8,128)} async-done(((f32[1,512,256]{1,2,0:T(8,128)}), f32[1,2048,256]{1,2,0:T(8,128)}) %all-gather.10.cloned.1.call-update) | async-done | bytes 2097168 | tf_op jit(solution)/shard_map/all_gather | solution.py:38
  813.6 4.7 fusion.25
  818.3 51.9 %all-reduce.42.cloned.1.call-done = f32[2,512,256]{1,2,0:T(8,128)} async-done(((f32[2,512,256]{1,2,0:T(8,128)}), f32[2,512,256]{1,2,0:T(8,128)}) %all-reduce.42.cloned.1.call-update) | async-done | bytes 1048592 | tf_op jit(solution)/shard_map/psum | solution.py:45
  870.3 53.8 %all-gather.12.cloned.1.call-done = f32[2,2048,256]{1,2,0:T(8,128)} async-done(((f32[2,512,256]{1,2,0:T(8,128)}), f32[2,2048,256]{1,2,0:T(8,128)}) %all-gather.12.cloned.1.call-update) | async-done | bytes 4194320 | tf_op jit(solution)/shard_map/all_gather | solution.py:38
  924.1 5.2 fusion.9
  929.3 51.9 %all-reduce.44.cloned.1.call-done = f32[2,512,256]{1,2,0:T(8,128)} async-done(((f32[2,512,256]{1,2,0:T(8,128)}), f32[2,512,256]{1,2,0:T(8,128)}) %all-reduce.44.cloned.1.call-update) | async-done | bytes 1048592 | tf_op jit(solution)/shard_map/psum | solution.py:45
  981.3 53.9 %all-gather.14.cloned.1.call-done = f32[2,2048,256]{1,2,0:T(8,128)} async-done(((f32[2,512,256]{1,2,0:T(8,128)}), f32[2,2048,256]{1,2,0:T(8,128)}) %all-gather.14.cloned.1.call-update) | async-done | bytes 4194320 | tf_op jit(solution)/shard_map/all_gather | solution.py:38
  (80 shorter events, 31.7 us)
Async XLA Ops:
  7.2 450.6 %copy-start = (f32[512,512]{1,0:T(8,128)S(1)}, f32[512,512]{1,0:T(8,128)}, u32[]{:S(2)}) copy-start(f32[512,512]{1,0:T(8,128)} %param.7) | copy-start | bytes 3145732
  7.2 58.3 %all-reduce.16.cloned.1.call-start = ((), (), s32[]{:S(2)}) async-start(), calls=%async_computation | async-start | bytes 2097152 | tf_op jit(solution)/shard_map/psum | solution.py:11
  10.0 60.4 %copy-start.6 = (s32[1,5,16,16]{3,2,1,0:T(8,128)S(1)}, s32[1,5,16,16]{3,2,1,0:T(8,128)}, u32[]{:S(2)}) copy-start(s32[1,5,16,16]{3,2,1,0:T(8,128)} %param.9) | copy-start | bytes 15364
  10.0 112.4 %all-reduce.18.cloned.1.call-start = ((), (), s32[]{:S(2)}) async-start(), calls=%async_computation.1 | async-start | bytes 2097152 | tf_op jit(solution)/shard_map/psum | solution.py:31
  70.4 107.0 %all-reduce.20.cloned.1.call-start = ((), (), s32[]{:S(2)}) async-start(), calls=%async_computation.2 | async-start | bytes 2097152 | tf_op jit(solution)/shard_map/psum | solution.py:11
  124.8 102.2 %all-reduce.22.cloned.1.call-start = ((), (), s32[]{:S(2)}) async-start(), calls=%async_computation.3 | async-start | bytes 1048576 | tf_op jit(solution)/shard_map/psum | solution.py:31
  182.1 137.7 %copy-start.2 = (f32[2,512,256]{1,2,0:T(8,128)S(1)}, f32[2,512,256]{1,2,0:T(8,128)}, u32[]{:S(2)}) copy-start(f32[2,512,256]{1,2,0:T(8,128)} %all-reduce.20.cloned.1.call-done) | copy-start | bytes 3145732
  182.1 86.0 %all-reduce.24.cloned.1.call-start = ((), (), s32[]{:S(2)}) async-start(), calls=%async_computation.4 | async-start | bytes 1048576 | tf_op jit(solution)/shard_map/psum | solution.py:11
  229.0 88.6 %all-reduce.26.cloned.1.call-start = ((), (), s32[]{:S(2)}) async-start(), calls=%async_computation.5 | async-start | bytes 1048576 | tf_op jit(solution)/shard_map/psum | solution.py:31
  272.1 86.7 %all-reduce.28.cloned.1.call-start = ((), (), s32[]{:S(2)}) async-start(), calls=%async_computation.6 | async-start | bytes 1048576 | tf_op jit(solution)/shard_map/psum | solution.py:11
  319.5 97.6 %all-reduce.30.cloned.1.call-start = ((), (), s32[]{:S(2)}) async-start(), calls=%async_computation.7 | async-start | bytes 1048576 | tf_op jit(solution)/shard_map/psum | solution.py:69
  323.3 93.8 %copy-start.5 = (f32[512,256]{1,0:T(8,128)S(1)}, f32[512,256]{1,0:T(8,128)}, u32[]{:S(2)}) copy-start(f32[512,256]{1,0:T(8,128)} %param.11) | copy-start | bytes 1572868
  362.1 95.7 %all-reduce.32.cloned.1.call-start = ((), (), s32[]{:S(2)}) async-start(), calls=%async_computation.8 | async-start | bytes 1048576 | tf_op jit(solution)/shard_map/psum | solution.py:11
  419.1 88.0 %all-reduce.34.cloned.1.call-start = ((), (), s32[]{:S(2)}) async-start(), calls=%async_computation.9 | async-start | bytes 1048576 | tf_op jit(solution)/shard_map/psum | solution.py:31
  461.5 86.9 %all-reduce.36.cloned.1.call-start = ((), (), s32[]{:S(2)}) async-start(), calls=%async_computation.10 | async-start | bytes 1048576 | tf_op jit(solution)/shard_map/psum | solution.py:45
  509.9 75.6 %all-gather.6.cloned.1.call-start = ((), (), s32[]{:S(2)}) async-start(), calls=%async_computation.11 | async-start | bytes 2621440 | tf_op jit(solution)/shard_map/all_gather | solution.py:38
  548.4 113.9 %all-reduce.38.cloned.1.call-start = ((), (), s32[]{:S(2)}) async-start(), calls=%async_computation.12 | async-start | bytes 3145728 | tf_op jit(solution)/shard_map/psum | solution.py:45
  586.9 6.2 copy-start.3
  593.0 140.4 %copy-start.4 = (f32[1,512,256]{1,2,0:T(8,128)S(1)}, f32[1,512,256]{1,2,0:T(8,128)}, u32[]{:S(2)}) copy-start(f32[1,512,256]{1,2,0:T(8,128)} %all-reduce.26.cloned.1.call-done) | copy-start | bytes 1572868
  593.0 140.3 %all-gather.8.cloned.1.call-start = ((), (), s32[]{:S(2)}) async-start(), calls=%async_computation.13 | async-start | bytes 7864320 | tf_op jit(solution)/shard_map/all_gather | solution.py:38
  662.3 112.8 %all-reduce.40.cloned.1.call-start = ((), (), s32[]{:S(2)}) async-start(), calls=%async_computation.14 | async-start | bytes 1048576 | tf_op jit(solution)/shard_map/psum | solution.py:45
  736.7 75.6 %all-gather.10.cloned.1.call-start = ((), (), s32[]{:S(2)}) async-start(), calls=%async_computation.15 | async-start | bytes 2621440 | tf_op jit(solution)/shard_map/all_gather | solution.py:38
  775.1 95.1 %all-reduce.42.cloned.1.call-start = ((), (), s32[]{:S(2)}) async-start(), calls=%async_computation.16 | async-start | bytes 2097152 | tf_op jit(solution)/shard_map/psum | solution.py:45
  813.6 110.5 %copy-start.1 = (f32[2,512,256]{1,2,0:T(8,128)S(1)}, f32[2,512,256]{1,2,0:T(8,128)}, u32[]{:S(2)}) copy-start(f32[2,512,256]{1,2,0:T(8,128)} %all-reduce.18.cloned.1.call-done) | copy-start | bytes 3145732
  818.3 105.8 %all-gather.12.cloned.1.call-start = ((), (), s32[]{:S(2)}) async-start(), calls=%async_computation.17 | async-start | bytes 5242880 | tf_op jit(solution)/shard_map/all_gather | solution.py:38
  870.3 111.0 %all-reduce.44.cloned.1.call-start = ((), (), s32[]{:S(2)}) async-start(), calls=%async_computation.18 | async-start | bytes 2097152 | tf_op jit(solution)/shard_map/psum | solution.py:45
  929.3 105.9 %all-gather.14.cloned.1.call-start = ((), (), s32[]{:S(2)}) async-start(), calls=%async_computation.19 | async-start | bytes 5242880 | tf_op jit(solution)/shard_map/all_gather | solution.py:38
Sparse Core Ops, SparseCore 0:
  11.0 54.5 all-reduce.15
  70.5 51.9 all-reduce.17
  125.5 51.8 all-reduce.19
  182.2 44.6 all-reduce.21
  229.7 38.2 all-reduce.23
  272.3 45.3 all-reduce.25
  320.5 38.2 all-reduce.27
  362.5 54.5 all-reduce.29
  420.2 37.5 all-reduce.31
  461.6 45.3 all-reduce.33
  510.1 38.2 all-reduce.35
  550.2 35.2 all-gather.5
  593.2 69.0 all-reduce.37
  664.1 69.1 all-gather.7
  736.8 38.2 all-reduce.39
  777.0 35.2 all-gather.9
  818.4 51.8 all-reduce.41
  872.0 52.0 all-gather.11
  929.4 51.8 all-reduce.43
  983.1 52.0 all-gather.13
where the time goes:
time: 1050 us
  waiting for transfers between devices  939 us (89%)
  matrix products  45.3 us (4%)
  local copies, waits for them, and re-layouts  23.8 us (2%)
  other arithmetic  21.5 us (2%)
  between operations  14.5 us (1%)
    all_gather x5, waiting for transfers between devices, regroup(): complete = lax.all_gather(column_rows, 'pcol', axis=1, tiled=True)  253 us
    psum x5, waiting for transfers between devices, row_total(): return regroup(lax.psum(partial_value, 'prow'))  250 us
    psum x5, waiting for transfers between devices, broadcast(): return lax.psum(block, axis)  196 us
    psum x4, waiting for transfers between devices, column_total(): return lax.psum(partial_value, 'pcol')  185 us
    psum x1, waiting for transfers between devices, per_device(): lax.psum(root_part[0] + root_part[1] + upper_part, ('layer', 'pcol'))  55 us
    dot_general x6, matrix products, forward_product(): jnp.einsum('nij,njk->nik', matrix, vector, precision=lax.Precision.HIGHEST)  23.2 us
    dot_general x5, matrix products, transpose_product(): jnp.einsum('nij,nik->njk', matrix, vector, precision=lax.Precision.HIGHEST)  22.1 us
  transfers between devices with their start and end apart: 20, of which 20 were waited for; matrix products, arithmetic and copies ran while one was open for 3% of the time, Pallas kernels for 0%

commit v1 on v0

v1 whole, which is shorter than its diff:
```python
import jax
import jax.numpy as jnp
from jax import lax
from jax.sharding import PartitionSpec as P

TILE = 128
GRID = ("prow", "pcol")


def dot(matrix, vector):
    return lax.dot_general(
        matrix, vector, (((1,), (0,)), ((), ())), precision=lax.Precision.HIGH
    )


def dot_t(matrix, vector):
    return lax.dot_general(
        matrix, vector, (((0,), (0,)), ((), ())), precision=lax.Precision.HIGH
    )


def send(value, target):
    rows, cols = lax.axis_size("prow"), lax.axis_size("pcol")
    pairs = []
    for i in range(rows):
        for j in range(cols):
            a, b = target(i, j)
            pairs.append((i * cols + j, a * cols + b))
    if all(s == d for s, d in pairs):
        return value
    return lax.ppermute(value, GRID, pairs)


def swap_layers(value):
    return lax.ppermute(value, "layer", [(0, 1), (1, 0)])


def split(value, count):
    size = value.shape[0] // count
    return [value[k * size : (k + 1) * size] for k in range(count)]


def total(pieces):
    result = pieces[0]
    for piece in pieces[1:]:
        result = result + piece
    return result


def reduce_chunks(partial):
    cols = lax.axis_size("pcol")
    pieces = split(partial, cols)
    return total([send(pieces[q], lambda i, j: (i, (j + q) % cols)) for q in range(cols)])


def gather_rows(chunk):
    cols = lax.axis_size("pcol")
    return jnp.concatenate(
        [send(chunk, lambda i, j: (i, (j - q) % cols)) for q in range(cols)], axis=0
    )


def gather_columns(chunk):
    rows, cols = lax.axis_size("prow"), lax.axis_size("pcol")
    ratio = cols // rows
    return jnp.concatenate(
        [
            send(chunk, lambda i, c: ((c % rows - i - q) % rows, i * ratio + c // rows))
            for q in range(rows)
        ],
        axis=0,
    )


def reduce_columns(partial):
    rows, cols = lax.axis_size("prow"), lax.axis_size("pcol")
    ratio = cols // rows
    pieces = split(partial, rows)
    moved = []
    for q in range(rows):
        near = send(
            pieces[q],
            lambda i, j: (i, j % ratio * rows + (i + j // ratio + q) % rows),
        )
        moved.append(send(near, lambda i, c: ((c % rows - i - q) % rows, c)))
    return total(moved)


def rotate(value, start, axis):
    doubled = jnp.concatenate([value, value], axis=axis)
    return lax.dynamic_slice_in_dim(doubled, start, value.shape[axis], axis)


def per_device(diag_inverse, root_inverse, coupling, tile_mask, sketch, root_sketch):
    rows, cols = lax.axis_size("prow"), lax.axis_size("pcol")
    row_index, col_index = lax.axis_index("prow"), lax.axis_index("pcol")
    layer = lax.axis_index("layer")
    ratio = cols // rows
    rows_here, cols_here = root_inverse.shape
    size = rows_here // cols
    width = sketch.shape[3]
    half = width // 2
    row_turn = col_index * size
    col_turn = (row_index + col_index // ratio) % rows * size

    def own(value):
        return lax.dynamic_slice_in_dim(value, col_index * size, size, value.ndim - 2)

    row_tiles = (row_index * rows_here + (row_turn + lax.iota(jnp.int32, rows_here)) % rows_here) // TILE
    col_tiles = (col_index * cols_here + (col_turn + lax.iota(jnp.int32, cols_here)) % cols_here) // TILE
    tiles = tile_mask.shape[2]
    row_pick = (row_tiles[:, None] == lax.iota(jnp.int32, tiles)[None]).astype(jnp.float32)
    col_pick = (lax.iota(jnp.int32, tiles)[:, None] == col_tiles[None]).astype(jnp.float32)

    def turned(matrix):
        return rotate(rotate(matrix, row_turn, 0), col_turn, 1)

    inverse = [turned(diag_inverse[0, n]) for n in range(3)]
    root = turned(root_inverse)
    blocks = []
    for n in range(5):
        mask = row_pick @ tile_mask[0, n].astype(jnp.float32) @ col_pick
        blocks.append(turned(coupling[0, n]) * mask)

    rhs = own(sketch[0])
    root_rhs = own(root_sketch)

    leaves, fed = [], []
    for a in range(2):
        leaves.append(reduce_chunks(dot(inverse[a], gather_columns(rhs[a]))))
        fed.append(gather_columns(leaves[a]))
    mid_part = dot(blocks[0], fed[0]) + dot(blocks[1], fed[1])
    mid_rhs = rhs[2] - reduce_chunks(mid_part)
    root_part = dot(blocks[2], fed[0]) + dot(blocks[3], fed[1])
    middle = reduce_chunks(dot(inverse[2], gather_columns(mid_rhs)))
    root_part = root_part + dot(blocks[4], gather_columns(middle))

    other = swap_layers(lax.dynamic_slice_in_dim(root_part, (1 - layer) * half, half, 1))
    mine = lax.dynamic_slice_in_dim(root_part, layer * half, half, 1) + other
    root_mine = lax.dynamic_slice_in_dim(root_rhs, layer * half, half, 1)
    root_in = gather_columns(root_mine - reduce_chunks(mine))
    root_forward = gather_rows(reduce_chunks(dot(root, root_in)))
    root_half = gather_rows(reduce_columns(dot_t(root, root_forward)))
    other_half = swap_layers(root_half)
    first = layer == 0
    root_rows = jnp.concatenate(
        [jnp.where(first, root_half, other_half), jnp.where(first, other_half, root_half)], axis=1
    )

    mid_back = middle - reduce_columns(dot_t(blocks[4], root_rows))
    mid_solution = reduce_columns(dot_t(inverse[2], gather_rows(mid_back)))
    mid_rows = gather_rows(mid_solution)
    answers = []
    for a in range(2):
        terms = dot_t(blocks[2 + a], root_rows) + dot_t(blocks[a], mid_rows)
        leaf_back = leaves[a] - reduce_columns(terms)
        leaf_chunk = reduce_columns(dot_t(inverse[a], gather_rows(leaf_back)))
        answers.append(gather_rows(leaf_chunk))
    back = rows_here - row_turn
    solution = jnp.stack([rotate(v, back, 0) for v in answers + [mid_rows]])[None]
    return solution, rotate(root_rows, back, 0)


def solution(mesh):
    in_specs = (
        P("layer", None, "prow", "pcol"),
        P("prow", "pcol"),
        P("layer", None, "prow", "pcol"),
        P("layer", None, None, None),
        P("layer", None, "prow", None),
        P("prow", None),
    )
    out_specs = (P("layer", None, "prow", None), P("prow", None))
    return jax.shard_map(
        per_device, mesh=mesh, in_specs=in_specs, out_specs=out_specs, check_vma=False
    )
```

time: 1050 us -> 472 us (0.45)
  waiting for transfers between devices: 939 us -> 71.3 us
  starting transfers between devices: 1.22 us -> 326 us
  matrix products: 45.3 us -> 30.1 us
  between operations: 14.5 us -> 2.75 us
    psum x15 -> x0, waiting for transfers between devices: 686 us -> none  [the longest x5 250 us: row_total(): return regroup(lax.psum(partial_value, 'prow'))]
    ppermute x0 -> x128, starting transfers between devices: none -> 326 us  [the longest x126 325 us: send(): return lax.ppermute(value, GRID, pairs)]
    all_gather x5 -> x0, waiting for transfers between devices: 253 us -> none  [regroup(): complete = lax.all_gather(column_rows, 'pcol', axis=1, tiled=True)]
    ppermute x0 -> x128, waiting for transfers between devices: none -> 71.3 us  [the longest x126 68 us: send(): return lax.ppermute(value, GRID, pairs)]
    gather x3 -> x0, local copies, waits for them, and re-layouts: 15.9 us -> none  [the longest x2 13.2 us: local_mask(): table = jnp.take(table, col_tiles, axis=2)]
    dot_general x11 -> x23, matrix products: 45.3 us -> 30.1 us  [the longest x9 12.3 us: dot_t(): lax.dot_general(matrix, vector, (((0,), (0,)), ((), ())), precision=lax.P...]
    concatenate x0 -> x10, other arithmetic: none -> 14.2 us  [the longest x9 14.2 us: rotate(): doubled = jnp.concatenate([value, value], axis=axis)]
  transfers between devices with their start and end apart: 20 -> 128, of which waited for: 20 -> 40; matrix products, arithmetic and copies ran while one was open for 3% -> 10% of each run, Pallas kernels for 0% -> 0%
where the time goes in v1:
time: 472 us; the launch traced here: 469 us
  starting transfers between devices  326 us (69%)
  waiting for transfers between devices  71.3 us (15%)
  matrix products  30.1 us (6%)
  other arithmetic  21.5 us (5%)
  local copies, waits for them, and re-layouts  17.6 us (4%)
    ppermute x126, starting transfers between devices, send(): return lax.ppermute(value, GRID, pairs)  325 us
    ppermute x126, waiting for transfers between devices, send(): return lax.ppermute(value, GRID, pairs)  68 us
    concatenate x9, other arithmetic, rotate(): doubled = jnp.concatenate([value, value], axis=axis)  14.2 us
    dot_general x9, matrix products, dot_t(): lax.dot_general(matrix, vector, (((0,), (0,)), ((), ())), precision=lax.P...  12.3 us
  transfers between devices with their start and end apart: 128, of which 40 were waited for; matrix products, arithmetic and copies ran while one was open for 10% of the time, Pallas kernels for 0%

profile of v1, /device:TPU:0, one launch (start us, length us, event | category | flops | bytes accessed | tf_op | source)
XLA Modules:
  0.0 468.7 jit_solution(1561608921054584414)
XLA Ops:
  2.9 9.8 %collective-permute-start.12 = (f32[128,256]{1,0:T(8,128)S(1)}, f32[128,256]{1,0:T(8,128)}, u32[]{:S(2)}, u32[]{:S(2)}) collective-permute-start(f32[128,256]{1,0:T(8,128)S(1)} %get-tuple-element.17), channel_id=1, source_target_pairs={{0,12},{1,0},{2,4},{3,8},{4,9},{5,13},{6,1},{7,5},{8,6},{9,10},{10... | collective-permute-start | bytes 393224 | tf_op jit(solution)/shard_map/ppermute | solution.py:31
  19.1 3.7 slice_bitcast_fusion.2
  41.0 9.0 %collective-permute-start.1 = (f32[128,256]{1,0:T(8,128)S(1)}, f32[128,256]{1,0:T(8,128)S(1)}, u32[]{:S(2)}, u32[]{:S(2)}) collective-permute-start(f32[128,256]{1,0:T(8,128)S(1)} %get-tuple-element.16), channel_id=1, source_target_pairs={{0,12},{1,0},{2,4},{3,8},{4,9},{5,13},{6,1},{7,5},{8,6},{9,10},{10... | collective-permute-start | bytes 393224 | tf_op jit(solution)/shard_map/ppermute | solution.py:31
  69.6 8.4 %collective-permute-start.19 = (f32[128,256]{1,0:T(8,128)S(1)}, f32[128,256]{1,0:T(8,128)S(1)}, u32[]{:S(2)}, u32[]{:S(2)}) collective-permute-start(f32[128,256]{1,0:T(8,128)S(1)} %fusion.113), channel_id=1, source_target_pairs={{0,12},{1,0},{2,4},{3,8},{4,9},{5,13},{6,1},{7,5},{8,6},{9,10},{10... | collective-permute-start | bytes 393224 | tf_op jit(solution)/shard_map/ppermute | solution.py:31
  78.7 5.2 %collective-permute-start.8 = (f32[128,256]{1,0:T(8,128)S(1)}, f32[128,256]{1,0:T(8,128)S(1)}, u32[]{:S(2)}, u32[]{:S(2)}) collective-permute-start(f32[128,256]{1,0:T(8,128)S(1)} %fusion.115), channel_id=1, source_target_pairs={{0,12},{1,0},{2,4},{3,8},{4,9},{5,13},{6,1},{7,5},{8,6},{9,10},{10... | collective-permute-start | bytes 393224 | tf_op jit(solution)/shard_map/ppermute | solution.py:31
  86.2 4.2 collective-permute-start.20
  94.4 5.8 %collective-permute-start.10 = (f32[128,256]{1,0:T(8,128)S(1)}, f32[128,256]{1,0:T(8,128)S(1)}, u32[]{:S(2)}, u32[]{:S(2)}) collective-permute-start(f32[128,256]{1,0:T(8,128)S(1)} %fusion.115), channel_id=1, source_target_pairs={{0,4},{1,8},{2,12},{3,0},{4,1},{5,5},{6,9},{7,13},{8,14},{9,2},{10... | collective-permute-start | bytes 393224 | tf_op jit(solution)/shard_map/ppermute | solution.py:31
  105.3 4.8 %collective-permute-start.22 = (f32[128,256]{1,0:T(8,128)S(1)}, f32[128,256]{1,0:T(8,128)S(1)}, u32[]{:S(2)}, u32[]{:S(2)}) collective-permute-start(f32[128,256]{1,0:T(8,128)S(1)} %get-tuple-element.47), channel_id=1, source_target_pairs={{0,1},{1,2},{2,3},{3,0},{4,5},{5,6},{6,7},{7,4},{8,9},{9,10},{10,1... | collective-permute-start | bytes 393224 | tf_op jit(solution)/shard_map/ppermute | solution.py:31
  119.4 8.0 %collective-permute-start.26 = (f32[128,256]{1,0:T(8,128)S(1)}, f32[128,256]{1,0:T(8,128)S(1)}, u32[]{:S(2)}, u32[]{:S(2)}) collective-permute-start(f32[128,256]{1,0:T(8,128)S(1)} %fusion.111), channel_id=1, source_target_pairs={{0,12},{1,0},{2,4},{3,8},{4,9},{5,13},{6,1},{7,5},{8,6},{9,10},{10... | collective-permute-start | bytes 393224 | tf_op jit(solution)/shard_map/ppermute | solution.py:31
  129.3 4.8 %collective-permute-start.28 = (f32[128,256]{1,0:T(8,128)S(1)}, f32[128,256]{1,0:T(8,128)S(1)}, u32[]{:S(2)}, u32[]{:S(2)}) collective-permute-start(f32[128,256]{1,0:T(8,128)S(1)} %fusion.111), channel_id=1, source_target_pairs={{0,4},{1,8},{2,12},{3,0},{4,1},{5,5},{6,9},{7,13},{8,14},{9,2},{10... | collective-permute-start | bytes 393224 | tf_op jit(solution)/shard_map/ppermute | solution.py:31
  150.8 9.4 %collective-permute-start.33 = (f32[128,256]{1,0:T(8,128)S(1)}, f32[128,256]{1,0:T(8,128)S(1)}, u32[]{:S(2)}, u32[]{:S(2)}) collective-permute-start(f32[128,256]{1,0:T(8,128)S(1)} %fusion.108), channel_id=1, source_target_pairs={{0,12},{1,0},{2,4},{3,8},{4,9},{5,13},{6,1},{7,5},{8,6},{9,10},{10... | collective-permute-start | bytes 393224 | tf_op jit(solution)/shard_map/ppermute | solution.py:31
  187.4 8.1 %collective-permute-start.41 = (f32[128,128]{1,0:T(8,128)S(1)}, f32[128,128]{1,0:T(8,128)S(1)}, u32[]{:S(2)}, u32[]{:S(2)}) collective-permute-start(f32[128,128]{1,0:T(8,128)S(1)} %fusion.138), channel_id=1, source_target_pairs={{0,12},{1,0},{2,4},{3,8},{4,9},{5,13},{6,1},{7,5},{8,6},{9,10},{10... | collective-permute-start | bytes 196616 | tf_op jit(solution)/shard_map/ppermute | solution.py:31
  226.8 3.8 collective-permute-start.54
  230.6 4.8 %collective-permute-start.56 = (f32[128,128]{1,0:T(8,128)S(1)}, f32[128,128]{1,0:T(8,128)S(1)}, u32[]{:S(2)}, u32[]{:S(2)}) collective-permute-start(f32[128,128]{1,0:T(8,128)S(1)} %get-tuple-element.57), channel_id=1, source_target_pairs={{0,3},{1,0},{2,1},{3,2},{4,4},{5,5},{6,6},{7,7},{8,9},{9,10},{10,1... | collective-permute-start | bytes 196616 | tf_op jit(solution)/shard_map/ppermute | solution.py:31
  236.1 4.3 collective-permute-start.53
  248.7 4.7 collective-permute-start.59
  269.5 4.6 collective-permute-start.68
  274.9 5.3 %collective-permute-start.65 = (f32[128,256]{1,0:T(8,128)S(1)}, f32[128,256]{1,0:T(8,128)S(1)}, u32[]{:S(2)}, u32[]{:S(2)}) collective-permute-start(f32[128,256]{1,0:T(8,128)S(1)} %collective-permute-done.64), channel_id=1, source_target_pairs={{0,12},{1,1},{2,6},{3,11},{4,8},{5,13},{6,2},{7,7},{8,4},{9,9},{10... | collective-permute-start | bytes 393224 | tf_op jit(solution)/shard_map/ppermute | solution.py:31
  284.5 5.2 %collective-permute-done.67 = f32[128,256]{1,0:T(8,128)S(1)} collective-permute-done((f32[128,256]{1,0:T(8,128)S(1)}, f32[128,256]{1,0:T(8,128)S(1)}, u32[]{:S(2)}, u32[]{:S(2)}) %collective-permute-start.67) | collective-permute-done | bytes 131104 | tf_op jit(solution)/shard_map/ppermute | solution.py:31
  291.2 4.4 collective-permute-start.71
  309.2 4.5 collective-permute-start.79
  314.5 6.9 %collective-permute-start.76 = (f32[128,256]{1,0:T(8,128)S(1)}, f32[128,256]{1,0:T(8,128)S(1)}, u32[]{:S(2)}, u32[]{:S(2)}) collective-permute-start(f32[128,256]{1,0:T(8,128)S(1)} %collective-permute-done.75), channel_id=1, source_target_pairs={{0,12},{1,1},{2,6},{3,11},{4,8},{5,13},{6,2},{7,7},{8,4},{9,9},{10... | collective-permute-start | bytes 393224 | tf_op jit(solution)/shard_map/ppermute | solution.py:31
  325.3 4.4 collective-permute-done.78
  349.7 4.6 collective-permute-start.90
  364.6 4.7 collective-permute-start.112
  369.9 6.4 %collective-permute-start.87 = (f32[128,256]{1,0:T(8,128)S(1)}, f32[128,256]{1,0:T(8,128)S(1)}, u32[]{:S(2)}, u32[]{:S(2)}) collective-permute-start(f32[128,256]{1,0:T(8,128)S(1)} %collective-permute-done.86), channel_id=1, source_target_pairs={{0,12},{1,1},{2,6},{3,11},{4,8},{5,13},{6,2},{7,7},{8,4},{9,9},{10... | collective-permute-start | bytes 393224 | tf_op jit(solution)/shard_map/ppermute | solution.py:31
  381.8 7.5 %collective-permute-start.109 = (f32[128,256]{1,0:T(8,128)S(1)}, f32[128,256]{1,0:T(8,128)S(1)}, u32[]{:S(2)}, u32[]{:S(2)}) collective-permute-start(f32[128,256]{1,0:T(8,128)S(1)} %collective-permute-done.108), channel_id=1, source_target_pairs={{0,12},{1,1},{2,6},{3,11},{4,8},{5,13},{6,2},{7,7},{8,4},{9,9},{10... | collective-permute-start | bytes 393224 | tf_op jit(solution)/shard_map/ppermute | solution.py:31
  389.4 3.9 collective-permute-start.111
  409.6 4.0 collective-permute-start.101
  421.4 3.9 collective-permute-start.121
  433.7 7.5 %collective-permute-start.98 = (f32[128,256]{1,0:T(8,128)S(1)}, f32[128,256]{1,0:T(8,128)S(1)}, u32[]{:S(2)}, u32[]{:S(2)}) collective-permute-start(f32[128,256]{1,0:T(8,128)S(1)} %collective-permute-done.97), channel_id=1, source_target_pairs={{0,12},{1,1},{2,6},{3,11},{4,8},{5,13},{6,2},{7,7},{8,4},{9,9},{10... | collective-permute-start | bytes 393224 | tf_op jit(solution)/shard_map/ppermute | solution.py:31
  442.0 6.1 %collective-permute-start.120 = (f32[128,256]{1,0:T(8,128)S(1)}, f32[128,256]{1,0:T(8,128)S(1)}, u32[]{:S(2)}, u32[]{:S(2)}) collective-permute-start(f32[128,256]{1,0:T(8,128)S(1)} %collective-permute-done.119), channel_id=1, source_target_pairs={{0,12},{1,1},{2,6},{3,11},{4,8},{5,13},{6,2},{7,7},{8,4},{9,9},{10... | collective-permute-start | bytes 393224 | tf_op jit(solution)/shard_map/ppermute | solution.py:31
  (383 shorter events, 283.2 us)
Async XLA Ops:
  1.6 39.4 %collective-permute-start.11 = (f32[128,256]{1,0:T(8,128)S(1)}, f32[128,256]{1,0:T(8,128)}, u32[]{:S(2)}, u32[]{:S(2)}) collective-permute-start(f32[128,256]{1,0:T(8,128)S(1)} %get-tuple-element.17), channel_id=1, source_target_pairs={{0,0},{1,4},{2,8},{3,12},{4,13},{5,1},{6,5},{7,9},{8,10},{9,14},{1... | collective-permute-start | bytes 393224 | tf_op jit(solution)/shard_map/ppermute | solution.py:31
  2.9 47.1 %collective-permute-start.12 = (f32[128,256]{1,0:T(8,128)S(1)}, f32[128,256]{1,0:T(8,128)}, u32[]{:S(2)}, u32[]{:S(2)}) collective-permute-start(f32[128,256]{1,0:T(8,128)S(1)} %get-tuple-element.17), channel_id=1, source_target_pairs={{0,12},{1,0},{2,4},{3,8},{4,9},{5,13},{6,1},{7,5},{8,6},{9,10},{10... | collective-permute-start | bytes 393224 | tf_op jit(solution)/shard_map/ppermute | solution.py:31
  12.7 39.2 %collective-permute-start.13 = (f32[128,256]{1,0:T(8,128)S(1)}, f32[128,256]{1,0:T(8,128)}, u32[]{:S(2)}, u32[]{:S(2)}) collective-permute-start(f32[128,256]{1,0:T(8,128)S(1)} %get-tuple-element.17), channel_id=1, source_target_pairs={{0,8},{1,12},{2,0},{3,4},{4,5},{5,9},{6,13},{7,1},{8,2},{9,6},{10,... | collective-permute-start | bytes 393224 | tf_op jit(solution)/shard_map/ppermute | solution.py:31
  14.7 39.8 %collective-permute-start.14 = (f32[128,256]{1,0:T(8,128)S(1)}, f32[128,256]{1,0:T(8,128)}, u32[]{:S(2)}, u32[]{:S(2)}) collective-permute-start(f32[128,256]{1,0:T(8,128)S(1)} %get-tuple-element.17), channel_id=1, source_target_pairs={{0,4},{1,8},{2,12},{3,0},{4,1},{5,5},{6,9},{7,13},{8,14},{9,2},{10... | collective-permute-start | bytes 393224 | tf_op jit(solution)/shard_map/ppermute | solution.py:31
  17.8 41.7 %collective-permute-start = (f32[128,256]{1,0:T(8,128)S(1)}, f32[128,256]{1,0:T(8,128)}, u32[]{:S(2)}, u32[]{:S(2)}) collective-permute-start(f32[128,256]{1,0:T(8,128)S(1)} %get-tuple-element.16), channel_id=1, source_target_pairs={{0,0},{1,4},{2,8},{3,12},{4,13},{5,1},{6,5},{7,9},{8,10},{9,14},{1... | collective-permute-start | bytes 393224 | tf_op jit(solution)/shard_map/ppermute | solution.py:31
  41.0 18.5 %collective-permute-start.1 = (f32[128,256]{1,0:T(8,128)S(1)}, f32[128,256]{1,0:T(8,128)S(1)}, u32[]{:S(2)}, u32[]{:S(2)}) collective-permute-start(f32[128,256]{1,0:T(8,128)S(1)} %get-tuple-element.16), channel_id=1, source_target_pairs={{0,12},{1,0},{2,4},{3,8},{4,9},{5,13},{6,1},{7,5},{8,6},{9,10},{10... | collective-permute-start | bytes 393224 | tf_op jit(solution)/shard_map/ppermute | solution.py:31
  68.9 17.3 %collective-permute-start.18 = (f32[128,256]{1,0:T(8,128)S(1)}, f32[128,256]{1,0:T(8,128)S(1)}, u32[]{:S(2)}, u32[]{:S(2)}) collective-permute-start(f32[128,256]{1,0:T(8,128)S(1)} %fusion.113), channel_id=1, source_target_pairs={{0,0},{1,4},{2,8},{3,12},{4,13},{5,1},{6,5},{7,9},{8,10},{9,14},{1... | collective-permute-start | bytes 393224 | tf_op jit(solution)/shard_map/ppermute | solution.py:31
  69.6 20.9 %collective-permute-start.19 = (f32[128,256]{1,0:T(8,128)S(1)}, f32[128,256]{1,0:T(8,128)S(1)}, u32[]{:S(2)}, u32[]{:S(2)}) collective-permute-start(f32[128,256]{1,0:T(8,128)S(1)} %fusion.113), channel_id=1, source_target_pairs={{0,12},{1,0},{2,4},{3,8},{4,9},{5,13},{6,1},{7,5},{8,6},{9,10},{10... | collective-permute-start | bytes 393224 | tf_op jit(solution)/shard_map/ppermute | solution.py:31
  78.1 23.0 %collective-permute-start.7 = (f32[128,256]{1,0:T(8,128)S(1)}, f32[128,256]{1,0:T(8,128)S(1)}, u32[]{:S(2)}, u32[]{:S(2)}) collective-permute-start(f32[128,256]{1,0:T(8,128)S(1)} %fusion.115), channel_id=1, source_target_pairs={{0,0},{1,4},{2,8},{3,12},{4,13},{5,1},{6,5},{7,9},{8,10},{9,14},{1... | collective-permute-start | bytes 393224 | tf_op jit(solution)/shard_map/ppermute | solution.py:31
  78.7 22.4 %collective-permute-start.8 = (f32[128,256]{1,0:T(8,128)S(1)}, f32[128,256]{1,0:T(8,128)S(1)}, u32[]{:S(2)}, u32[]{:S(2)}) collective-permute-start(f32[128,256]{1,0:T(8,128)S(1)} %fusion.115), channel_id=1, source_target_pairs={{0,12},{1,0},{2,4},{3,8},{4,9},{5,13},{6,1},{7,5},{8,6},{9,10},{10... | collective-permute-start | bytes 393224 | tf_op jit(solution)/shard_map/ppermute | solution.py:31
  83.9 17.2 %collective-permute-start.9 = (f32[128,256]{1,0:T(8,128)S(1)}, f32[128,256]{1,0:T(8,128)S(1)}, u32[]{:S(2)}, u32[]{:S(2)}) collective-permute-start(f32[128,256]{1,0:T(8,128)S(1)} %fusion.115), channel_id=1, source_target_pairs={{0,8},{1,12},{2,0},{3,4},{4,5},{5,9},{6,13},{7,1},{8,2},{9,6},{10,... | collective-permute-start | bytes 393224 | tf_op jit(solution)/shard_map/ppermute | solution.py:31
  118.7 16.8 %collective-permute-start.25 = (f32[128,256]{1,0:T(8,128)S(1)}, f32[128,256]{1,0:T(8,128)S(1)}, u32[]{:S(2)}, u32[]{:S(2)}) collective-permute-start(f32[128,256]{1,0:T(8,128)S(1)} %fusion.111), channel_id=1, source_target_pairs={{0,0},{1,4},{2,8},{3,12},{4,13},{5,1},{6,5},{7,9},{8,10},{9,14},{1... | collective-permute-start | bytes 393224 | tf_op jit(solution)/shard_map/ppermute | solution.py:31
  119.4 16.1 %collective-permute-start.26 = (f32[128,256]{1,0:T(8,128)S(1)}, f32[128,256]{1,0:T(8,128)S(1)}, u32[]{:S(2)}, u32[]{:S(2)}) collective-permute-start(f32[128,256]{1,0:T(8,128)S(1)} %fusion.111), channel_id=1, source_target_pairs={{0,12},{1,0},{2,4},{3,8},{4,9},{5,13},{6,1},{7,5},{8,6},{9,10},{10... | collective-permute-start | bytes 393224 | tf_op jit(solution)/shard_map/ppermute | solution.py:31
  150.0 17.1 %collective-permute-start.32 = (f32[128,256]{1,0:T(8,128)S(1)}, f32[128,256]{1,0:T(8,128)S(1)}, u32[]{:S(2)}, u32[]{:S(2)}) collective-permute-start(f32[128,256]{1,0:T(8,128)S(1)} %fusion.108), channel_id=1, source_target_pairs={{0,0},{1,4},{2,8},{3,12},{4,13},{5,1},{6,5},{7,9},{8,10},{9,14},{1... | collective-permute-start | bytes 393224 | tf_op jit(solution)/shard_map/ppermute | solution.py:31
  150.8 16.3 %collective-permute-start.33 = (f32[128,256]{1,0:T(8,128)S(1)}, f32[128,256]{1,0:T(8,128)S(1)}, u32[]{:S(2)}, u32[]{:S(2)}) collective-permute-start(f32[128,256]{1,0:T(8,128)S(1)} %fusion.108), channel_id=1, source_target_pairs={{0,12},{1,0},{2,4},{3,8},{4,9},{5,13},{6,1},{7,5},{8,6},{9,10},{10... | collective-permute-start | bytes 393224 | tf_op jit(solution)/shard_map/ppermute | solution.py:31
  305.9 15.5 %collective-permute-start.77 = (f32[128,256]{1,0:T(8,128)S(1)}, f32[128,256]{1,0:T(8,128)S(1)}, u32[]{:S(2)}, u32[]{:S(2)}) collective-permute-start(f32[128,256]{1,0:T(8,128)S(1)} %get-tuple-element.36), channel_id=1, source_target_pairs={{0,2},{1,3},{2,0},{3,1},{4,7},{5,4},{6,5},{7,6},{8,8},{9,9},{10,10... | collective-permute-start | bytes 393224 | tf_op jit(solution)/shard_map/ppermute | solution.py:31
  343.3 14.9 %collective-permute-start.84 = (f32[128,256]{1,0:T(8,128)S(1)}, f32[128,256]{1,0:T(8,128)S(1)}, u32[]{:S(2)}, u32[]{:S(2)}) collective-permute-start(f32[128,256]{1,0:T(8,128)S(1)} %get-tuple-element.25), channel_id=1, source_target_pairs={{0,0},{1,1},{2,2},{3,3},{4,5},{5,6},{6,7},{7,4},{8,10},{9,11},{10,... | collective-permute-start | bytes 393224 | tf_op jit(solution)/shard_map/ppermute | solution.py:31
  344.0 16.2 %collective-permute-start.86 = (f32[128,256]{1,0:T(8,128)S(1)}, f32[128,256]{1,0:T(8,128)S(1)}, u32[]{:S(2)}, u32[]{:S(2)}) collective-permute-start(f32[128,256]{1,0:T(8,128)S(1)} %get-tuple-element.22), channel_id=1, source_target_pairs={{0,1},{1,2},{2,3},{3,0},{4,6},{5,7},{6,4},{7,5},{8,11},{9,8},{10,9... | collective-permute-start | bytes 393224 | tf_op jit(solution)/shard_map/ppermute | solution.py:31
  346.7 17.9 %collective-permute-start.88 = (f32[128,256]{1,0:T(8,128)S(1)}, f32[128,256]{1,0:T(8,128)S(1)}, u32[]{:S(2)}, u32[]{:S(2)}) collective-permute-start(f32[128,256]{1,0:T(8,128)S(1)} %get-tuple-element.24), channel_id=1, source_target_pairs={{0,2},{1,3},{2,0},{3,1},{4,7},{5,4},{6,5},{7,6},{8,8},{9,9},{10,10... | collective-permute-start | bytes 393224 | tf_op jit(solution)/shard_map/ppermute | solution.py:31
  349.7 19.5 %collective-permute-start.90 = (f32[128,256]{1,0:T(8,128)S(1)}, f32[128,256]{1,0:T(8,128)S(1)}, u32[]{:S(2)}, u32[]{:S(2)}) collective-permute-start(f32[128,256]{1,0:T(8,128)S(1)} %get-tuple-element.23), channel_id=1, source_target_pairs={{0,3},{1,0},{2,1},{3,2},{4,4},{5,5},{6,6},{7,7},{8,9},{9,10},{10,1... | collective-permute-start | bytes 393224 | tf_op jit(solution)/shard_map/ppermute | solution.py:31
  358.3 18.1 %collective-permute-start.108 = (f32[128,256]{1,0:T(8,128)S(1)}, f32[128,256]{1,0:T(8,128)S(1)}, u32[]{:S(2)}, u32[]{:S(2)}) collective-permute-start(f32[128,256]{1,0:T(8,128)S(1)} %get-tuple-element.30), channel_id=1, source_target_pairs={{0,1},{1,2},{2,3},{3,0},{4,6},{5,7},{6,4},{7,5},{8,11},{9,8},{10,9... | collective-permute-start | bytes 393224 | tf_op jit(solution)/shard_map/ppermute | solution.py:31
  360.2 18.1 %collective-permute-start.110 = (f32[128,256]{1,0:T(8,128)S(1)}, f32[128,256]{1,0:T(8,128)S(1)}, u32[]{:S(2)}, u32[]{:S(2)}) collective-permute-start(f32[128,256]{1,0:T(8,128)S(1)} %get-tuple-element.32), channel_id=1, source_target_pairs={{0,2},{1,3},{2,0},{3,1},{4,7},{5,4},{6,5},{7,6},{8,8},{9,9},{10,10... | collective-permute-start | bytes 393224 | tf_op jit(solution)/shard_map/ppermute | solution.py:31
  364.6 16.6 %collective-permute-start.112 = (f32[128,256]{1,0:T(8,128)S(1)}, f32[128,256]{1,0:T(8,128)S(1)}, u32[]{:S(2)}, u32[]{:S(2)}) collective-permute-start(f32[128,256]{1,0:T(8,128)S(1)} %get-tuple-element.31), channel_id=1, source_target_pairs={{0,3},{1,0},{2,1},{3,2},{4,4},{5,5},{6,6},{7,7},{8,9},{9,10},{10,1... | collective-permute-start | bytes 393224 | tf_op jit(solution)/shard_map/ppermute | solution.py:31
  369.9 19.5 %collective-permute-start.87 = (f32[128,256]{1,0:T(8,128)S(1)}, f32[128,256]{1,0:T(8,128)S(1)}, u32[]{:S(2)}, u32[]{:S(2)}) collective-permute-start(f32[128,256]{1,0:T(8,128)S(1)} %collective-permute-done.86), channel_id=1, source_target_pairs={{0,12},{1,1},{2,6},{3,11},{4,8},{5,13},{6,2},{7,7},{8,4},{9,9},{10... | collective-permute-start | bytes 393224 | tf_op jit(solution)/shard_map/ppermute | solution.py:31
  376.3 17.0 %collective-permute-start.89 = (f32[128,256]{1,0:T(8,128)S(1)}, f32[128,256]{1,0:T(8,128)S(1)}, u32[]{:S(2)}, u32[]{:S(2)}) collective-permute-start(f32[128,256]{1,0:T(8,128)S(1)} %collective-permute-done.88), channel_id=1, source_target_pairs={{0,8},{1,13},{2,2},{3,7},{4,4},{5,9},{6,14},{7,3},{8,0},{9,5},{10,... | collective-permute-start | bytes 393224 | tf_op jit(solution)/shard_map/ppermute | solution.py:31
  378.3 17.0 %collective-permute-start.91 = (f32[128,256]{1,0:T(8,128)S(1)}, f32[128,256]{1,0:T(8,128)S(1)}, u32[]{:S(2)}, u32[]{:S(2)}) collective-permute-start(f32[128,256]{1,0:T(8,128)S(1)} %collective-permute-done.90), channel_id=1, source_target_pairs={{0,4},{1,9},{2,14},{3,3},{4,0},{5,5},{6,10},{7,15},{8,12},{9,1},{1... | collective-permute-start | bytes 393224 | tf_op jit(solution)/shard_map/ppermute | solution.py:31
  381.8 16.4 %collective-permute-start.109 = (f32[128,256]{1,0:T(8,128)S(1)}, f32[128,256]{1,0:T(8,128)S(1)}, u32[]{:S(2)}, u32[]{:S(2)}) collective-permute-start(f32[128,256]{1,0:T(8,128)S(1)} %collective-permute-done.108), channel_id=1, source_target_pairs={{0,12},{1,1},{2,6},{3,11},{4,8},{5,13},{6,2},{7,7},{8,4},{9,9},{10... | collective-permute-start | bytes 393224 | tf_op jit(solution)/shard_map/ppermute | solution.py:31
  414.3 14.8 %collective-permute-start.97 = (f32[128,256]{1,0:T(8,128)S(1)}, f32[128,256]{1,0:T(8,128)S(1)}, u32[]{:S(2)}, u32[]{:S(2)}) collective-permute-start(f32[128,256]{1,0:T(8,128)S(1)} %get-tuple-element.18), channel_id=1, source_target_pairs={{0,1},{1,2},{2,3},{3,0},{4,6},{5,7},{6,4},{7,5},{8,11},{9,8},{10,9... | collective-permute-start | bytes 393224 | tf_op jit(solution)/shard_map/ppermute | solution.py:31
  418.0 15.0 %collective-permute-start.119 = (f32[128,256]{1,0:T(8,128)S(1)}, f32[128,256]{1,0:T(8,128)S(1)}, u32[]{:S(2)}, u32[]{:S(2)}) collective-permute-start(f32[128,256]{1,0:T(8,128)S(1)} %get-tuple-element.26), channel_id=1, source_target_pairs={{0,1},{1,2},{2,3},{3,0},{4,6},{5,7},{6,4},{7,5},{8,11},{9,8},{10,9... | collective-permute-start | bytes 393224 | tf_op jit(solution)/shard_map/ppermute | solution.py:31
  431.0 17.0 %collective-permute-start.102 = (f32[128,256]{1,0:T(8,128)S(1)}, f32[128,256]{1,0:T(8,128)S(1)}, u32[]{:S(2)}, u32[]{:S(2)}) collective-permute-start(f32[128,256]{1,0:T(8,128)S(1)} %collective-permute-done.101), channel_id=1, source_target_pairs={{0,4},{1,9},{2,14},{3,3},{4,0},{5,5},{6,10},{7,15},{8,12},{9,1},{1... | collective-permute-start | bytes 393224 | tf_op jit(solution)/shard_map/ppermute | solution.py:31
  433.0 17.0 %collective-permute-start.96 = (f32[128,256]{1,0:T(8,128)S(1)}, f32[128,256]{1,0:T(8,128)S(1)}, u32[]{:S(2)}, u32[]{:S(2)}) collective-permute-start(f32[128,256]{1,0:T(8,128)S(1)} %collective-permute-done.95), channel_id=1, source_target_pairs={{0,0},{1,5},{2,10},{3,15},{4,12},{5,1},{6,6},{7,11},{8,8},{9,13},{... | collective-permute-start | bytes 393224 | tf_op jit(solution)/shard_map/ppermute | solution.py:31
  433.7 18.3 %collective-permute-start.98 = (f32[128,256]{1,0:T(8,128)S(1)}, f32[128,256]{1,0:T(8,128)S(1)}, u32[]{:S(2)}, u32[]{:S(2)}) collective-permute-start(f32[128,256]{1,0:T(8,128)S(1)} %collective-permute-done.97), channel_id=1, source_target_pairs={{0,12},{1,1},{2,6},{3,11},{4,8},{5,13},{6,2},{7,7},{8,4},{9,9},{10... | collective-permute-start | bytes 393224 | tf_op jit(solution)/shard_map/ppermute | solution.py:31
  (126 other events, 1386.6 us)

commit v2 on v0

--- a/solution.py
+++ b/solution.py
@@ -53,7 +53,7 @@
     return table.astype(jnp.float32)
 
 
-def per_device(diag_inverse, root_inverse, coupling, tile_mask, sketch, root_sketch):
+def per_device_any(diag_inverse, root_inverse, coupling, tile_mask, sketch, root_sketch):
     layer_inverse = diag_inverse[0]
     rows_here = coupling.shape[2]
     cols_here = coupling.shape[3]
@@ -82,8 +82,139 @@
     solution = jnp.concatenate([leaf_solution, mid_solution[None]], axis=0)[None]
     return (solution, root_solution)
 
+GRID = ("prow", "pcol")
+SIDE = 4
+
+
+def dot(matrices, vectors):
+    return jnp.einsum("nij,njk->nik", matrices, vectors, precision=lax.Precision.HIGH)
+
+
+def dot_t(matrices, vectors):
+    return jnp.einsum("nij,nik->njk", matrices, vectors, precision=lax.Precision.HIGH)
+
+
+def send(value, target):
+    pairs = []
+    for i in range(SIDE):
+        for j in range(SIDE):
+            a, b = target(i, j)
+            if (a, b) != (i, j):
+                pairs.append((i * SIDE + j, a * SIDE + b))
+    return lax.ppermute(value, GRID, pairs)
+
+
+def swap_layers(value):
+    return lax.ppermute(value, "layer", [(0, 1), (1, 0)])
+
+
+def pick(values, index):
+    low = jnp.where(index % 2 == 0, values[0], values[1])
+    high = jnp.where(index % 2 == 0, values[2], values[3])
+    return jnp.where(index // 2 == 0, low, high)
+
+
+def per_device_square(diag_inverse, root_inverse, coupling, tile_mask, sketch, root_sketch):
+    i, j = lax.axis_index("prow"), lax.axis_index("pcol")
+    layer = lax.axis_index("layer")
+    rows_here, cols_here = root_inverse.shape
+    size = rows_here // SIDE
+    half = sketch.shape[3] // 2
+
+    def chunk(value, index):
+        return lax.dynamic_slice_in_dim(value, index * size, size, value.ndim - 2)
+
+    def ordered(value, turn, axis):
+        parts = [
+            lax.dynamic_slice_in_dim(value, (turn ^ k) * size, size, axis) for k in range(SIDE)
+        ]
+        return jnp.concatenate(parts, axis=axis)
+
+    def arranged(matrices):
+        return ordered(ordered(matrices, j, 1), i, 2)
+
+    def reduce_rows(partial):
+        parts = [partial[:, k * size : (k + 1) * size] for k in range(SIDE)]
+        moved = [send(parts[k], lambda a, b: (a, b ^ k)) for k in range(1, SIDE)]
+        return parts[0] + moved[0] + moved[1] + moved[2]
+
+    def gather_parts(value):
+        return [value] + [send(value, lambda a, b: (a, b ^ k)) for k in range(1, SIDE)]
+
+    def gather_rows(value):
+        return jnp.concatenate(gather_parts(value), axis=1)
+
+    def gather_columns(value):
+        parts = [send(value, lambda a, b: (b ^ k, a)) for k in range(SIDE)]
+        parts[0] = jnp.where(i == j, value, parts[0])
+        return jnp.concatenate(parts, axis=1)
+
+    def reduce_columns(partial):
+        parts = [chunk(partial, i ^ j ^ k) for k in range(SIDE)]
+        near = [parts[0]] + [send(parts[k], lambda a, b: (a, b ^ k)) for k in range(1, SIDE)]
+        parts = [pick(near, i ^ j ^ k) for k in range(SIDE)]
+        moved = [send(parts[k], lambda a, b: (a ^ k, b)) for k in range(1, SIDE)]
+        return parts[0] + moved[0] + moved[1] + moved[2]
+
+    def natural(parts):
+        return jnp.concatenate([pick(parts, j ^ k) for k in range(SIDE)], axis=1)
+
+    def columns(value, which):
+        return lax.dynamic_slice_in_dim(value, which * half, half, value.ndim - 1)
+
+    order = lax.iota(jnp.int32, rows_here)
+    row_tiles = (i * rows_here + ((order // size) ^ j) * size + order % size) // TILE
+    col_tiles = (j * cols_here + ((order // size) ^ i) * size + order % size) // TILE
+    tiles = lax.iota(jnp.int32, tile_mask.shape[2])
+    row_pick = (row_tiles[:, None] == tiles[None]).astype(jnp.float32)
+    col_pick = (tiles[:, None] == col_tiles[None]).astype(jnp.float32)
+
+    def blocks(first, last):
+        rows = jnp.einsum("rt,ntu->nru", row_pick, tile_mask[0, first:last].astype(jnp.float32))
+        return arranged(coupling[0, first:last]) * jnp.einsum("nru,uc->nrc", rows, col_pick)
+
+    rhs = chunk(sketch[0], j)
+    root_rhs = chunk(root_sketch, j)
+
+    lower = arranged(diag_inverse[0, 0:2])
+    leaves = reduce_rows(dot(lower, gather_columns(rhs[0:2])))
+    fed = gather_columns(leaves)
+    to_mid, to_root, mid_root = blocks(0, 2), blocks(2, 4), blocks(4, 5)
+    upper = arranged(diag_inverse[0, 2:3])
+    root = arranged(root_inverse[None])
+    mid_part = jnp.sum(dot(to_mid, fed), axis=0, keepdims=True)
+    mid_rhs = rhs[2:3] - reduce_rows(mid_part)
+    root_part = jnp.sum(dot(to_root, fed), axis=0, keepdims=True)
+    middle = reduce_rows(dot(upper, gather_columns(mid_rhs)))
+    root_part = root_part + dot(mid_root, gather_columns(middle))
+
+    mine = columns(root_part, layer) + swap_layers(columns(root_part, 1 - layer))
+    root_in = columns(root_rhs, layer)[None] - reduce_rows(mine)
+    root_forward = gather_rows(reduce_rows(dot(root, gather_columns(root_in))))
+    root_half = gather_rows(reduce_columns(dot_t(root, root_forward)))
+    other_half = swap_layers(root_half)
+    first = layer == 0
+    root_rows = jnp.concatenate(
+        [jnp.where(first, root_half, other_half), jnp.where(first, other_half, root_half)], axis=2
+    )
+
+    def both(value):
+        return jnp.broadcast_to(value, (2,) + value.shape[1:])
+
+    from_root = dot_t(to_root, both(root_rows))
+    mid_back = middle - reduce_columns(dot_t(mid_root, root_rows))
+    mid_parts = gather_parts(reduce_columns(dot_t(upper, gather_rows(mid_back))))
+    mid_rows = jnp.concatenate(mid_parts, axis=1)
+    leaf_back = leaves - reduce_columns(from_root + dot_t(to_mid, both(mid_rows)))
+    leaf_parts = gather_parts(reduce_columns(dot_t(lower, gather_rows(leaf_back))))
+    solved = jnp.concatenate([natural(leaf_parts), natural(mid_parts)], axis=0)
+    root_parts = [root_rows[:, k * size : (k + 1) * size] for k in range(SIDE)]
+    return solved[None], natural(root_parts)[0]
+
 
 def solution(mesh):
+    square = dict(mesh.shape) == {"layer": 2, "prow": SIDE, "pcol": SIDE}
+    per_device = per_device_square if square else per_device_any
     in_specs = (
         P("layer", None, "prow", "pcol"),
         P("prow", "pcol"),

time: 1050 us -> 389 us (0.37)
  waiting for transfers between devices: 939 us -> 165 us
  starting transfers between devices: 1.22 us -> 145 us
  matrix products: 45.3 us -> 26.5 us
  between operations: 14.5 us -> 1.66 us
    psum x15 -> x0, waiting for transfers between devices: 686 us -> none  [the longest x5 250 us: row_total(): return regroup(lax.psum(partial_value, 'prow'))]
    all_gather x5 -> x0, waiting for transfers between devices: 253 us -> none  [regroup(): complete = lax.all_gather(column_rows, 'pcol', axis=1, tiled=True)]
    ppermute x0 -> x85, waiting for transfers between devices: none -> 165 us  [the longest x83 163 us: send(): return lax.ppermute(value, GRID, pairs)]
    ppermute x0 -> x85, starting transfers between devices: none -> 145 us  [the longest x83 145 us: send(): return lax.ppermute(value, GRID, pairs)]
    dot_general x11 -> x15, matrix products: 45.3 us -> 26.5 us  [the longest x6 10.2 us: dot_t(): jnp.einsum('nij,nik->njk', matrices, vectors, precision=lax.Precision.HIGH)]
    gather x3 -> x0, local copies, waits for them, and re-layouts: 15.9 us -> none  [the longest x2 13.2 us: local_mask(): table = jnp.take(table, col_tiles, axis=2)]
  transfers between devices with their start and end apart: 20 -> 85, of which waited for: 20 -> 62; matrix products, arithmetic and copies ran while one was open for 3% -> 9% of each run, Pallas kernels for 0% -> 0%
where the time goes in v2:
time: 389 us; the launch traced here: 384 us
  waiting for transfers between devices  165 us (42%)
  starting transfers between devices  145 us (37%)
  matrix products  26.5 us (7%)
  local copies, waits for them, and re-layouts  26.4 us (7%)
  other arithmetic  18.9 us (5%)
    ppermute x83, waiting for transfers between devices, send(): return lax.ppermute(value, GRID, pairs)  163 us
    ppermute x83, starting transfers between devices, send(): return lax.ppermute(value, GRID, pairs)  145 us
    dynamic_slice x9, local copies, waits for them, and re-layouts, ordered(): lax.dynamic_slice_in_dim(value, (turn ^ k) * size, size, axis)  12.8 us
    dot_general x6, matrix products, dot_t(): jnp.einsum('nij,nik->njk', matrices, vectors, precision=lax.Precision.HIGH)  10.2 us
    dot_general x6, matrix products, dot(): jnp.einsum('nij,njk->nik', matrices, vectors, precision=lax.Precision.HIGH)  8.78 us
  transfers between devices with their start and end apart: 85, of which 62 were waited for; matrix products, arithmetic and copies ran while one was open for 9% of the time, Pallas kernels for 0%

profile of v2, /device:TPU:0, one launch (start us, length us, event | category | flops | bytes accessed | tf_op | source)
XLA Modules:
  0.0 384.1 jit_solution(512234908096055896)
XLA Ops:
  3.0 5.0 %collective-permute-start.1 = (f32[2,128,256]{2,1,0:T(8,128)S(1)}, f32[2,128,256]{2,1,0:T(8,128)}, u32[]{:S(2)}, u32[]{:S(2)}) collective-permute-start(f32[2,128,256]{2,1,0:T(8,128)S(1)} %dynamic-slice_bitcast_fusion.12), channel_id=1, source_target_pairs={{0,4},{1,0},{2,12},{3,8},{4,5},{5,1},{6,13},{7,9},{8,6},{9,2},{10,... | collective-permute-start | bytes 786440 | tf_op jit(solution)/shard_map/ppermute | solution.py:104
  8.0 3.5 collective-permute-start.2
  13.4 4.7 %fusion.163 = (f32[1,2,512,512]{3,2,1,0:T(8,128)}, f32[1,2,512,512]{3,2,1,0:T(8,128)}) fusion(f32[1,5,512,512]{3,2,1,0:T(8,128)} %param.8), kind=kLoop, calls=%fused_computation.304 | loop fusion | bytes 8388608 | tf_op jit(solution)/shard_map/slice | solution.py:174
  42.3 3.6 maximum_multiply_fusion.1
  46.9 4.0 %collective-permute-done.5 = f32[2,128,256]{2,1,0:T(8,128)} collective-permute-done((f32[2,128,256]{2,1,0:T(8,128)}, f32[2,128,256]{2,1,0:T(8,128)}, u32[]{:S(2)}, u32[]{:S(2)}) %collective-permute-start.5) | collective-permute-done | bytes 262176 | tf_op jit(solution)/shard_map/ppermute | solution.py:104
  58.2 5.6 %collective-permute-start.10 = (f32[2,128,256]{2,1,0:T(8,128)}, f32[2,128,256]{2,1,0:T(8,128)}, u32[]{:S(2)}, u32[]{:S(2)}) collective-permute-start(f32[2,128,256]{2,1,0:T(8,128)} %fusion.45), channel_id=1, source_target_pairs={{0,12},{1,8},{2,4},{3,0},{4,13},{5,9},{6,5},{7,1},{8,14},{9,10},{1... | collective-permute-start | bytes 786440 | tf_op jit(solution)/shard_map/ppermute | solution.py:104
  65.0 6.5 %collective-permute-done.10 = f32[2,128,256]{2,1,0:T(8,128)} collective-permute-done((f32[2,128,256]{2,1,0:T(8,128)}, f32[2,128,256]{2,1,0:T(8,128)}, u32[]{:S(2)}, u32[]{:S(2)}) %collective-permute-start.10) | collective-permute-done | bytes 262176 | tf_op jit(solution)/shard_map/ppermute | solution.py:104
  71.5 3.2 collective-permute-done.8
  83.3 5.6 %collective-permute-start.12 = (f32[1,128,256]{2,1,0:T(8,128)S(1)}, f32[1,128,256]{2,1,0:T(8,128)S(1)}, u32[]{:S(2)}, u32[]{:S(2)}) collective-permute-start(f32[1,128,256]{2,1,0:T(8,128)S(1)} %get-tuple-element.102), channel_id=1, source_target_pairs={{0,2},{1,3},{2,0},{3,1},{4,6},{5,7},{6,4},{7,5},{8,10},{9,11},{10,... | collective-permute-start | bytes 393224 | tf_op jit(solution)/shard_map/ppermute | solution.py:104
  96.5 4.7 %collective-permute-start.15 = (f32[1,128,256]{2,1,0:T(8,128)S(1)}, f32[1,128,256]{2,1,0:T(8,128)S(1)}, u32[]{:S(2)}, u32[]{:S(2)}) collective-permute-start(f32[1,128,256]{2,1,0:T(8,128)S(1)} %fusion.71), channel_id=1, source_target_pairs={{0,4},{1,0},{2,12},{3,8},{4,5},{5,1},{6,13},{7,9},{8,6},{9,2},{10,... | collective-permute-start | bytes 393224 | tf_op jit(solution)/shard_map/ppermute | solution.py:104
  105.2 3.5 collective-permute-done.16
  109.4 4.4 %collective-permute-start.18 = (f32[1,128,256]{2,1,0:T(8,128)S(1)}, f32[1,128,256]{2,1,0:T(8,128)S(1)}, u32[]{:S(2)}, u32[]{:S(2)}) collective-permute-start(f32[1,128,256]{2,1,0:T(8,128)S(1)} %get-tuple-element.97), channel_id=1, source_target_pairs={{0,1},{1,0},{2,3},{3,2},{4,5},{5,4},{6,7},{7,6},{8,9},{9,8},{10,11... | collective-permute-start | bytes 393224 | tf_op jit(solution)/shard_map/ppermute | solution.py:104
  113.8 3.8 %collective-permute-start.19 = (f32[1,128,256]{2,1,0:T(8,128)S(1)}, f32[1,128,256]{2,1,0:T(8,128)S(1)}, u32[]{:S(2)}, u32[]{:S(2)}) collective-permute-start(f32[1,128,256]{2,1,0:T(8,128)S(1)} %get-tuple-element.99), channel_id=1, source_target_pairs={{0,2},{1,3},{2,0},{3,1},{4,6},{5,7},{6,4},{7,5},{8,10},{9,11},{10,... | collective-permute-start | bytes 393224 | tf_op jit(solution)/shard_map/ppermute | solution.py:104
  127.4 3.2 collective-permute-start.22
  134.0 4.4 %collective-permute-done.23 = f32[1,128,256]{2,1,0:T(8,128)S(1)} collective-permute-done((f32[1,128,256]{2,1,0:T(8,128)S(1)}, f32[1,128,256]{2,1,0:T(8,128)S(1)}, u32[]{:S(2)}, u32[]{:S(2)}) %collective-permute-start.23) | collective-permute-done | bytes 131104 | tf_op jit(solution)/shard_map/ppermute | solution.py:104
  145.4 5.7 %collective-permute-start.26 = (f32[1,128,128]{2,1,0:T(8,128)}, f32[1,128,128]{2,1,0:T(8,128)}, u32[]{:S(2)}, u32[]{:S(2)}) collective-permute-start(f32[1,128,128]{2,1,0:T(8,128)} %get-tuple-element.112), channel_id=1, source_target_pairs={{0,1},{1,0},{2,3},{3,2},{4,5},{5,4},{6,7},{7,6},{8,9},{9,8},{10,11... | collective-permute-start | bytes 196616 | tf_op jit(solution)/shard_map/ppermute | solution.py:104
  160.1 4.8 %collective-permute-start.30 = (f32[1,128,128]{2,1,0:T(8,128)S(1)}, f32[1,128,128]{2,1,0:T(8,128)S(1)}, u32[]{:S(2)}, u32[]{:S(2)}) collective-permute-start(f32[1,128,128]{2,1,0:T(8,128)S(1)} %fusion.97), channel_id=1, source_target_pairs={{0,4},{1,0},{2,12},{3,8},{4,5},{5,1},{6,13},{7,9},{8,6},{9,2},{10,... | collective-permute-start | bytes 196616 | tf_op jit(solution)/shard_map/ppermute | solution.py:104
  172.6 3.5 collective-permute-start.33
  234.1 3.0 collective-permute-start.53
  240.7 6.2 %collective-permute-done.53 = f32[1,128,256]{2,1,0:T(8,128)S(1)} collective-permute-done((f32[1,128,256]{2,1,0:T(8,128)S(1)}, f32[1,128,256]{2,1,0:T(8,128)S(1)}, u32[]{:S(2)}, u32[]{:S(2)}) %collective-permute-start.53) | collective-permute-done | bytes 131104 | tf_op jit(solution)/shard_map/ppermute | solution.py:104
  252.1 3.8 collective-permute-done.57
  272.3 3.9 %collective-permute-done.62 = f32[1,128,256]{2,1,0:T(8,128)S(1)} collective-permute-done((f32[1,128,256]{2,1,0:T(8,128)S(1)}, f32[1,128,256]{2,1,0:T(8,128)S(1)}, u32[]{:S(2)}, u32[]{:S(2)}) %collective-permute-start.62) | collective-permute-done | bytes 131104 | tf_op jit(solution)/shard_map/ppermute | solution.py:104
  281.8 3.3 collective-permute-done.66
  297.2 3.1 collective-permute-start.70
  302.7 7.1 %collective-permute-done.70 = f32[2,128,256]{2,1,0:T(8,128)S(1)} collective-permute-done((f32[2,128,256]{2,1,0:T(8,128)S(1)}, f32[2,128,256]{2,1,0:T(8,128)S(1)}, u32[]{:S(2)}, u32[]{:S(2)}) %collective-permute-start.70) | collective-permute-done | bytes 262176 | tf_op jit(solution)/shard_map/ppermute | solution.py:104
  309.9 8.6 %collective-permute-done.71 = f32[2,128,256]{2,1,0:T(8,128)S(1)} collective-permute-done((f32[2,128,256]{2,1,0:T(8,128)S(1)}, f32[2,128,256]{2,1,0:T(8,128)S(1)}, u32[]{:S(2)}, u32[]{:S(2)}) %collective-permute-start.71) | collective-permute-done | bytes 262176 | tf_op jit(solution)/shard_map/ppermute | solution.py:104
  323.1 4.0 %collective-permute-done.73 = f32[2,128,256]{2,1,0:T(8,128)S(1)} collective-permute-done((f32[2,128,256]{2,1,0:T(8,128)S(1)}, f32[2,128,256]{2,1,0:T(8,128)S(1)}, u32[]{:S(2)}, u32[]{:S(2)}) %collective-permute-start.73) | collective-permute-done | bytes 262176 | tf_op jit(solution)/shard_map/ppermute | solution.py:104
  327.2 8.4 %collective-permute-done.74 = f32[2,128,256]{2,1,0:T(8,128)S(1)} collective-permute-done((f32[2,128,256]{2,1,0:T(8,128)S(1)}, f32[2,128,256]{2,1,0:T(8,128)S(1)}, u32[]{:S(2)}, u32[]{:S(2)}) %collective-permute-start.74) | collective-permute-done | bytes 262176 | tf_op jit(solution)/shard_map/ppermute | solution.py:104
  347.3 3.6 collective-permute-start.79
  353.5 4.2 %collective-permute-done.79 = f32[2,128,256]{2,1,0:T(8,128)S(1)} collective-permute-done((f32[2,128,256]{2,1,0:T(8,128)S(1)}, f32[2,128,256]{2,1,0:T(8,128)S(1)}, u32[]{:S(2)}, u32[]{:S(2)}) %collective-permute-start.79) | collective-permute-done | bytes 262176 | tf_op jit(solution)/shard_map/ppermute | solution.py:104
  357.7 12.8 %collective-permute-done.80 = f32[2,128,256]{2,1,0:T(8,128)S(1)} collective-permute-done((f32[2,128,256]{2,1,0:T(8,128)S(1)}, f32[2,128,256]{2,1,0:T(8,128)S(1)}, u32[]{:S(2)}, u32[]{:S(2)}) %collective-permute-start.80) | collective-permute-done | bytes 262176 | tf_op jit(solution)/shard_map/ppermute | solution.py:104
  378.0 4.7 %collective-permute-done.83 = f32[2,128,256]{2,1,0:T(8,128)S(1)} collective-permute-done((f32[2,128,256]{2,1,0:T(8,128)S(1)}, f32[2,128,256]{2,1,0:T(8,128)S(1)}, u32[]{:S(2)}, u32[]{:S(2)}) %collective-permute-start.83) | collective-permute-done | bytes 262176 | tf_op jit(solution)/shard_map/ppermute | solution.py:104
  (302 shorter events, 226.1 us)
Async XLA Ops:
  1.6 31.6 %collective-permute-start = (f32[2,128,256]{2,1,0:T(8,128)S(1)}, f32[2,128,256]{2,1,0:T(8,128)}, u32[]{:S(2)}, u32[]{:S(2)}) collective-permute-start(f32[2,128,256]{2,1,0:T(8,128)S(1)} %dynamic-slice_bitcast_fusion.12), channel_id=1, source_target_pairs={{1,4},{2,8},{3,12},{4,1},{6,9},{7,13},{8,2},{9,6},{11,14},{12,3},{... | collective-permute-start | bytes 786440 | tf_op jit(solution)/shard_map/ppermute | solution.py:104
  3.0 31.2 %collective-permute-start.1 = (f32[2,128,256]{2,1,0:T(8,128)S(1)}, f32[2,128,256]{2,1,0:T(8,128)}, u32[]{:S(2)}, u32[]{:S(2)}) collective-permute-start(f32[2,128,256]{2,1,0:T(8,128)S(1)} %dynamic-slice_bitcast_fusion.12), channel_id=1, source_target_pairs={{0,4},{1,0},{2,12},{3,8},{4,5},{5,1},{6,13},{7,9},{8,6},{9,2},{10,... | collective-permute-start | bytes 786440 | tf_op jit(solution)/shard_map/ppermute | solution.py:104
  8.0 26.2 %collective-permute-start.2 = (f32[2,128,256]{2,1,0:T(8,128)S(1)}, f32[2,128,256]{2,1,0:T(8,128)}, u32[]{:S(2)}, u32[]{:S(2)}) collective-permute-start(f32[2,128,256]{2,1,0:T(8,128)S(1)} %dynamic-slice_bitcast_fusion.12), channel_id=1, source_target_pairs={{0,8},{1,12},{2,0},{3,4},{4,9},{5,13},{6,1},{7,5},{8,10},{9,14},{1... | collective-permute-start | bytes 786440 | tf_op jit(solution)/shard_map/ppermute | solution.py:104
  11.5 22.8 %collective-permute-start.3 = (f32[2,128,256]{2,1,0:T(8,128)S(1)}, f32[2,128,256]{2,1,0:T(8,128)}, u32[]{:S(2)}, u32[]{:S(2)}) collective-permute-start(f32[2,128,256]{2,1,0:T(8,128)S(1)} %dynamic-slice_bitcast_fusion.12), channel_id=1, source_target_pairs={{0,12},{1,8},{2,4},{3,0},{4,13},{5,9},{6,5},{7,1},{8,14},{9,10},{1... | collective-permute-start | bytes 786440 | tf_op jit(solution)/shard_map/ppermute | solution.py:104
  37.4 9.5 %collective-permute-start.4 = (f32[2,128,256]{2,1,0:T(8,128)}, f32[2,128,256]{2,1,0:T(8,128)S(1)}, u32[]{:S(2)}, u32[]{:S(2)}) collective-permute-start(f32[2,128,256]{2,1,0:T(8,128)} %get-tuple-element.65), channel_id=1, source_target_pairs={{0,1},{1,0},{2,3},{3,2},{4,5},{5,4},{6,7},{7,6},{8,9},{9,8},{10,11... | collective-permute-start | bytes 786440 | tf_op jit(solution)/shard_map/ppermute | solution.py:104
  38.9 11.9 %collective-permute-start.5 = (f32[2,128,256]{2,1,0:T(8,128)}, f32[2,128,256]{2,1,0:T(8,128)}, u32[]{:S(2)}, u32[]{:S(2)}) collective-permute-start(f32[2,128,256]{2,1,0:T(8,128)} %get-tuple-element.67), channel_id=1, source_target_pairs={{0,2},{1,3},{2,0},{3,1},{4,6},{5,7},{6,4},{7,5},{8,10},{9,11},{10,... | collective-permute-start | bytes 786440 | tf_op jit(solution)/shard_map/ppermute | solution.py:104
  40.8 11.9 %collective-permute-start.6 = (f32[2,128,256]{2,1,0:T(8,128)}, f32[2,128,256]{2,1,0:T(8,128)}, u32[]{:S(2)}, u32[]{:S(2)}) collective-permute-start(f32[2,128,256]{2,1,0:T(8,128)} %get-tuple-element.66), channel_id=1, source_target_pairs={{0,3},{1,2},{2,1},{3,0},{4,7},{5,6},{6,5},{7,4},{8,11},{9,10},{10,... | collective-permute-start | bytes 786440 | tf_op jit(solution)/shard_map/ppermute | solution.py:104
  54.6 9.3 %collective-permute-start.7 = (f32[2,128,256]{2,1,0:T(8,128)}, f32[2,128,256]{2,1,0:T(8,128)}, u32[]{:S(2)}, u32[]{:S(2)}) collective-permute-start(f32[2,128,256]{2,1,0:T(8,128)} %fusion.45), channel_id=1, source_target_pairs={{1,4},{2,8},{3,12},{4,1},{6,9},{7,13},{8,2},{9,6},{11,14},{12,3},{... | collective-permute-start | bytes 786440 | tf_op jit(solution)/shard_map/ppermute | solution.py:104
  58.2 13.3 %collective-permute-start.10 = (f32[2,128,256]{2,1,0:T(8,128)}, f32[2,128,256]{2,1,0:T(8,128)}, u32[]{:S(2)}, u32[]{:S(2)}) collective-permute-start(f32[2,128,256]{2,1,0:T(8,128)} %fusion.45), channel_id=1, source_target_pairs={{0,12},{1,8},{2,4},{3,0},{4,13},{5,9},{6,5},{7,1},{8,14},{9,10},{1... | collective-permute-start | bytes 786440 | tf_op jit(solution)/shard_map/ppermute | solution.py:104
  63.8 10.9 %collective-permute-start.8 = (f32[2,128,256]{2,1,0:T(8,128)}, f32[2,128,256]{2,1,0:T(8,128)}, u32[]{:S(2)}, u32[]{:S(2)}) collective-permute-start(f32[2,128,256]{2,1,0:T(8,128)} %fusion.45), channel_id=1, source_target_pairs={{0,4},{1,0},{2,12},{3,8},{4,5},{5,1},{6,13},{7,9},{8,6},{9,2},{10,... | collective-permute-start | bytes 786440 | tf_op jit(solution)/shard_map/ppermute | solution.py:104
  63.8 13.7 %collective-permute-start.9 = (f32[2,128,256]{2,1,0:T(8,128)}, f32[2,128,256]{2,1,0:T(8,128)}, u32[]{:S(2)}, u32[]{:S(2)}) collective-permute-start(f32[2,128,256]{2,1,0:T(8,128)} %fusion.45), channel_id=1, source_target_pairs={{0,8},{1,12},{2,0},{3,4},{4,9},{5,13},{6,1},{7,5},{8,10},{9,14},{1... | collective-permute-start | bytes 786440 | tf_op jit(solution)/shard_map/ppermute | solution.py:104
  80.4 10.1 %collective-permute-start.11 = (f32[1,128,256]{2,1,0:T(8,128)S(1)}, f32[1,128,256]{2,1,0:T(8,128)S(1)}, u32[]{:S(2)}, u32[]{:S(2)}) collective-permute-start(f32[1,128,256]{2,1,0:T(8,128)S(1)} %get-tuple-element.100), channel_id=1, source_target_pairs={{0,1},{1,0},{2,3},{3,2},{4,5},{5,4},{6,7},{7,6},{8,9},{9,8},{10,11... | collective-permute-start | bytes 393224 | tf_op jit(solution)/shard_map/ppermute | solution.py:104
  83.3 9.7 %collective-permute-start.12 = (f32[1,128,256]{2,1,0:T(8,128)S(1)}, f32[1,128,256]{2,1,0:T(8,128)S(1)}, u32[]{:S(2)}, u32[]{:S(2)}) collective-permute-start(f32[1,128,256]{2,1,0:T(8,128)S(1)} %get-tuple-element.102), channel_id=1, source_target_pairs={{0,2},{1,3},{2,0},{3,1},{4,6},{5,7},{6,4},{7,5},{8,10},{9,11},{10,... | collective-permute-start | bytes 393224 | tf_op jit(solution)/shard_map/ppermute | solution.py:104
  96.5 8.7 %collective-permute-start.15 = (f32[1,128,256]{2,1,0:T(8,128)S(1)}, f32[1,128,256]{2,1,0:T(8,128)S(1)}, u32[]{:S(2)}, u32[]{:S(2)}) collective-permute-start(f32[1,128,256]{2,1,0:T(8,128)S(1)} %fusion.71), channel_id=1, source_target_pairs={{0,4},{1,0},{2,12},{3,8},{4,5},{5,1},{6,13},{7,9},{8,6},{9,2},{10,... | collective-permute-start | bytes 393224 | tf_op jit(solution)/shard_map/ppermute | solution.py:104
  109.4 10.7 %collective-permute-start.18 = (f32[1,128,256]{2,1,0:T(8,128)S(1)}, f32[1,128,256]{2,1,0:T(8,128)S(1)}, u32[]{:S(2)}, u32[]{:S(2)}) collective-permute-start(f32[1,128,256]{2,1,0:T(8,128)S(1)} %get-tuple-element.97), channel_id=1, source_target_pairs={{0,1},{1,0},{2,3},{3,2},{4,5},{5,4},{6,7},{7,6},{8,9},{9,8},{10,11... | collective-permute-start | bytes 393224 | tf_op jit(solution)/shard_map/ppermute | solution.py:104
  124.4 9.0 %collective-permute-start.21 = (f32[1,128,256]{2,1,0:T(8,128)S(1)}, f32[1,128,256]{2,1,0:T(8,128)}, u32[]{:S(2)}, u32[]{:S(2)}) collective-permute-start(f32[1,128,256]{2,1,0:T(8,128)S(1)} %fusion.68), channel_id=1, source_target_pairs={{1,4},{2,8},{3,12},{4,1},{6,9},{7,13},{8,2},{9,6},{11,14},{12,3},{... | collective-permute-start | bytes 393224 | tf_op jit(solution)/shard_map/ppermute | solution.py:104
  158.1 9.9 %collective-permute-start.29 = (f32[1,128,128]{2,1,0:T(8,128)S(1)}, f32[1,128,128]{2,1,0:T(8,128)S(1)}, u32[]{:S(2)}, u32[]{:S(2)}) collective-permute-start(f32[1,128,128]{2,1,0:T(8,128)S(1)} %fusion.97), channel_id=1, source_target_pairs={{1,4},{2,8},{3,12},{4,1},{6,9},{7,13},{8,2},{9,6},{11,14},{12,3},{... | collective-permute-start | bytes 196616 | tf_op jit(solution)/shard_map/ppermute | solution.py:104
  234.1 12.7 %collective-permute-start.53 = (f32[1,128,256]{2,1,0:T(8,128)S(1)}, f32[1,128,256]{2,1,0:T(8,128)S(1)}, u32[]{:S(2)}, u32[]{:S(2)}) collective-permute-start(f32[1,128,256]{2,1,0:T(8,128)S(1)} %get-tuple-element.81), channel_id=1, source_target_pairs={{0,8},{1,9},{2,10},{3,11},{4,12},{5,13},{6,14},{7,15},{8,0},{9,1},... | collective-permute-start | bytes 393224 | tf_op jit(solution)/shard_map/ppermute | solution.py:104
  237.2 9.7 %collective-permute-start.54 = (f32[1,128,256]{2,1,0:T(8,128)S(1)}, f32[1,128,256]{2,1,0:T(8,128)S(1)}, u32[]{:S(2)}, u32[]{:S(2)}) collective-permute-start(f32[1,128,256]{2,1,0:T(8,128)S(1)} %get-tuple-element.80), channel_id=1, source_target_pairs={{0,12},{1,13},{2,14},{3,15},{4,8},{5,9},{6,10},{7,11},{8,4},{9,5},... | collective-permute-start | bytes 393224 | tf_op jit(solution)/shard_map/ppermute | solution.py:104
  266.0 10.1 %collective-permute-start.62 = (f32[1,128,256]{2,1,0:T(8,128)S(1)}, f32[1,128,256]{2,1,0:T(8,128)S(1)}, u32[]{:S(2)}, u32[]{:S(2)}) collective-permute-start(f32[1,128,256]{2,1,0:T(8,128)S(1)} %get-tuple-element.78), channel_id=1, source_target_pairs={{0,8},{1,9},{2,10},{3,11},{4,12},{5,13},{6,14},{7,15},{8,0},{9,1},... | collective-permute-start | bytes 393224 | tf_op jit(solution)/shard_map/ppermute | solution.py:104
  287.6 8.8 %collective-permute-start.68 = (f32[2,128,256]{2,1,0:T(8,128)S(1)}, f32[2,128,256]{2,1,0:T(8,128)S(1)}, u32[]{:S(2)}, u32[]{:S(2)}) collective-permute-start(f32[2,128,256]{2,1,0:T(8,128)S(1)} %get-tuple-element.48), channel_id=1, source_target_pairs={{0,2},{1,3},{2,0},{3,1},{4,6},{5,7},{6,4},{7,5},{8,10},{9,11},{10,... | collective-permute-start | bytes 786440 | tf_op jit(solution)/shard_map/ppermute | solution.py:104
  297.2 12.7 %collective-permute-start.70 = (f32[2,128,256]{2,1,0:T(8,128)S(1)}, f32[2,128,256]{2,1,0:T(8,128)S(1)}, u32[]{:S(2)}, u32[]{:S(2)}) collective-permute-start(f32[2,128,256]{2,1,0:T(8,128)S(1)} %get-tuple-element.36), channel_id=1, source_target_pairs={{0,4},{1,5},{2,6},{3,7},{4,0},{5,1},{6,2},{7,3},{8,12},{9,13},{10,... | collective-permute-start | bytes 786440 | tf_op jit(solution)/shard_map/ppermute | solution.py:104
  300.3 18.2 %collective-permute-start.71 = (f32[2,128,256]{2,1,0:T(8,128)S(1)}, f32[2,128,256]{2,1,0:T(8,128)S(1)}, u32[]{:S(2)}, u32[]{:S(2)}) collective-permute-start(f32[2,128,256]{2,1,0:T(8,128)S(1)} %get-tuple-element.38), channel_id=1, source_target_pairs={{0,8},{1,9},{2,10},{3,11},{4,12},{5,13},{6,14},{7,15},{8,0},{9,1},... | collective-permute-start | bytes 786440 | tf_op jit(solution)/shard_map/ppermute | solution.py:104
  300.4 18.1 %collective-permute-start.72 = (f32[2,128,256]{2,1,0:T(8,128)S(1)}, f32[2,128,256]{2,1,0:T(8,128)S(1)}, u32[]{:S(2)}, u32[]{:S(2)}) collective-permute-start(f32[2,128,256]{2,1,0:T(8,128)S(1)} %get-tuple-element.37), channel_id=1, source_target_pairs={{0,12},{1,13},{2,14},{3,15},{4,8},{5,9},{6,10},{7,11},{8,4},{9,5},... | collective-permute-start | bytes 786440 | tf_op jit(solution)/shard_map/ppermute | solution.py:104
  321.4 14.1 %collective-permute-start.74 = (f32[2,128,256]{2,1,0:T(8,128)S(1)}, f32[2,128,256]{2,1,0:T(8,128)S(1)}, u32[]{:S(2)}, u32[]{:S(2)}) collective-permute-start(f32[2,128,256]{2,1,0:T(8,128)S(1)} %add_subtract_fusion), channel_id=1, source_target_pairs={{0,2},{1,3},{2,0},{3,1},{4,6},{5,7},{6,4},{7,5},{8,10},{9,11},{10,... | collective-permute-start | bytes 786440 | tf_op jit(solution)/shard_map/ppermute | solution.py:104
  321.8 13.8 %collective-permute-start.75 = (f32[2,128,256]{2,1,0:T(8,128)S(1)}, f32[2,128,256]{2,1,0:T(8,128)S(1)}, u32[]{:S(2)}, u32[]{:S(2)}) collective-permute-start(f32[2,128,256]{2,1,0:T(8,128)S(1)} %add_subtract_fusion), channel_id=1, source_target_pairs={{0,3},{1,2},{2,1},{3,0},{4,7},{5,6},{6,5},{7,4},{8,11},{9,10},{10,... | collective-permute-start | bytes 786440 | tf_op jit(solution)/shard_map/ppermute | solution.py:104
  338.0 9.2 %collective-permute-start.77 = (f32[2,128,256]{2,1,0:T(8,128)S(1)}, f32[2,128,256]{2,1,0:T(8,128)S(1)}, u32[]{:S(2)}, u32[]{:S(2)}) collective-permute-start(f32[2,128,256]{2,1,0:T(8,128)S(1)} %get-tuple-element.45), channel_id=1, source_target_pairs={{0,2},{1,3},{2,0},{3,1},{4,6},{5,7},{6,4},{7,5},{8,10},{9,11},{10,... | collective-permute-start | bytes 786440 | tf_op jit(solution)/shard_map/ppermute | solution.py:104
  347.3 10.4 %collective-permute-start.79 = (f32[2,128,256]{2,1,0:T(8,128)S(1)}, f32[2,128,256]{2,1,0:T(8,128)S(1)}, u32[]{:S(2)}, u32[]{:S(2)}) collective-permute-start(f32[2,128,256]{2,1,0:T(8,128)S(1)} %get-tuple-element.33), channel_id=1, source_target_pairs={{0,4},{1,5},{2,6},{3,7},{4,0},{5,1},{6,2},{7,3},{8,12},{9,13},{10,... | collective-permute-start | bytes 786440 | tf_op jit(solution)/shard_map/ppermute | solution.py:104
  350.9 19.5 %collective-permute-start.80 = (f32[2,128,256]{2,1,0:T(8,128)S(1)}, f32[2,128,256]{2,1,0:T(8,128)S(1)}, u32[]{:S(2)}, u32[]{:S(2)}) collective-permute-start(f32[2,128,256]{2,1,0:T(8,128)S(1)} %get-tuple-element.35), channel_id=1, source_target_pairs={{0,8},{1,9},{2,10},{3,11},{4,12},{5,13},{6,14},{7,15},{8,0},{9,1},... | collective-permute-start | bytes 786440 | tf_op jit(solution)/shard_map/ppermute | solution.py:104
  351.1 19.3 %collective-permute-start.81 = (f32[2,128,256]{2,1,0:T(8,128)S(1)}, f32[2,128,256]{2,1,0:T(8,128)S(1)}, u32[]{:S(2)}, u32[]{:S(2)}) collective-permute-start(f32[2,128,256]{2,1,0:T(8,128)S(1)} %get-tuple-element.34), channel_id=1, source_target_pairs={{0,12},{1,13},{2,14},{3,15},{4,8},{5,9},{6,10},{7,11},{8,4},{9,5},... | collective-permute-start | bytes 786440 | tf_op jit(solution)/shard_map/ppermute | solution.py:104
  372.2 10.6 %collective-permute-start.83 = (f32[2,128,256]{2,1,0:T(8,128)S(1)}, f32[2,128,256]{2,1,0:T(8,128)S(1)}, u32[]{:S(2)}, u32[]{:S(2)}) collective-permute-start(f32[2,128,256]{2,1,0:T(8,128)S(1)} %add_add_fusion), channel_id=1, source_target_pairs={{0,2},{1,3},{2,0},{3,1},{4,6},{5,7},{6,4},{7,5},{8,10},{9,11},{10,... | collective-permute-start | bytes 786440 | tf_op jit(solution)/shard_map/ppermute | solution.py:104
  373.4 9.3 %collective-permute-start.84 = (f32[2,128,256]{2,1,0:T(8,128)S(1)}, f32[2,128,256]{2,1,0:T(8,128)S(1)}, u32[]{:S(2)}, u32[]{:S(2)}) collective-permute-start(f32[2,128,256]{2,1,0:T(8,128)S(1)} %add_add_fusion), channel_id=1, source_target_pairs={{0,3},{1,2},{2,1},{3,0},{4,7},{5,6},{6,5},{7,4},{8,11},{9,10},{10,... | collective-permute-start | bytes 786440 | tf_op jit(solution)/shard_map/ppermute | solution.py:104
  (96 other events, 1034.2 us)

commit v3 on v2

--- a/solution.py
+++ b/solution.py
@@ -177,14 +177,17 @@
     root_rhs = chunk(root_sketch, j)
 
     lower = arranged(diag_inverse[0, 0:2])
-    leaves = reduce_rows(dot(lower, gather_columns(rhs[0:2])))
-    fed = gather_columns(leaves)
+    first = gather_columns(rhs[0:2])
+    leaves, fed = [], []
+    for a in range(2):
+        leaves.append(reduce_rows(dot(lower[a : a + 1], first[a : a + 1])))
+        fed.append(gather_columns(leaves[a]))
     to_mid, to_root, mid_root = blocks(0, 2), blocks(2, 4), blocks(4, 5)
     upper = arranged(diag_inverse[0, 2:3])
     root = arranged(root_inverse[None])
-    mid_part = jnp.sum(dot(to_mid, fed), axis=0, keepdims=True)
+    mid_part = dot(to_mid[0:1], fed[0]) + dot(to_mid[1:2], fed[1])
     mid_rhs = rhs[2:3] - reduce_rows(mid_part)
-    root_part = jnp.sum(dot(to_root, fed), axis=0, keepdims=True)
+    root_part = dot(to_root[0:1], fed[0]) + dot(to_root[1:2], fed[1])
     middle = reduce_rows(dot(upper, gather_columns(mid_rhs)))
     root_part = root_part + dot(mid_root, gather_columns(middle))
 
@@ -205,9 +208,13 @@
     mid_back = middle - reduce_columns(dot_t(mid_root, root_rows))
     mid_parts = gather_parts(reduce_columns(dot_t(upper, gather_rows(mid_back))))
     mid_rows = jnp.concatenate(mid_parts, axis=1)
-    leaf_back = leaves - reduce_columns(from_root + dot_t(to_mid, both(mid_rows)))
-    leaf_parts = gather_parts(reduce_columns(dot_t(lower, gather_rows(leaf_back))))
-    solved = jnp.concatenate([natural(leaf_parts), natural(mid_parts)], axis=0)
+    solved = []
+    for a in range(2):
+        leaf = slice(a, a + 1)
+        terms = from_root[leaf] + dot_t(to_mid[leaf], mid_rows)
+        leaf_back = leaves[a] - reduce_columns(terms)
+        solved.append(natural(gather_parts(reduce_columns(dot_t(lower[leaf], gather_rows(leaf_back))))))
+    solved = jnp.concatenate(solved + [natural(mid_parts)], axis=0)
     root_parts = [root_rows[:, k * size : (k + 1) * size] for k in range(SIDE)]
     return solved[None], natural(root_parts)[0]
 

time: 389 us -> 362 us (0.931); the launches traced: 384 us -> 361 us
  waiting for transfers between devices: 165 us -> 115 us
  starting transfers between devices: 145 us -> 175 us
    ppermute x83 -> x108, waiting for transfers between devices: 163 us -> 113 us  [send(): return lax.ppermute(value, GRID, pairs)]
    ppermute x83 -> x108, starting transfers between devices: 145 us -> 175 us  [send(): return lax.ppermute(value, GRID, pairs)]
    dot_general x6 -> x9, matrix products: 8.78 us -> 6.67 us  [dot(): jnp.einsum('nij,njk->nik', matrices, vectors, precision=lax.Precision.HIGH)]
    dot_general x6 -> x8, matrix products: 10.2 us -> 11.7 us  [dot_t(): jnp.einsum('nij,nik->njk', matrices, vectors, precision=lax.Precision.HIGH)]
  transfers between devices with their start and end apart: 85 -> 110, of which waited for: 62 -> 53; matrix products, arithmetic and copies ran while one was open for 9% -> 10% of each run, Pallas kernels for 0% -> 0%
where the time goes in v3:
time: 362 us; the launch traced here: 361 us
  starting transfers between devices  175 us (48%)
  waiting for transfers between devices  115 us (32%)
  matrix products  26.9 us (7%)
  local copies, waits for them, and re-layouts  23.7 us (7%)
  other arithmetic  18.5 us (5%)
    ppermute x108, starting transfers between devices, send(): return lax.ppermute(value, GRID, pairs)  175 us
    ppermute x108, waiting for transfers between devices, send(): return lax.ppermute(value, GRID, pairs)  113 us
    dot_general x8, matrix products, dot_t(): jnp.einsum('nij,nik->njk', matrices, vectors, precision=lax.Precision.HIGH)  11.7 us
    dynamic_slice x9, local copies, waits for them, and re-layouts, ordered(): lax.dynamic_slice_in_dim(value, (turn ^ k) * size, size, axis)  9.6 us
    dot_general x3, matrix products, blocks(): jnp.einsum('nru,uc->nrc', rows, col_pick)  8.49 us
  transfers between devices with their start and end apart: 110, of which 53 were waited for; matrix products, arithmetic and copies ran while one was open for 10% of the time, Pallas kernels for 0%

profile of v3, /device:TPU:0, one launch (start us, length us, event | category | flops | bytes accessed | tf_op | source)
XLA Modules:
  0.0 361.2 jit_solution(421979012530203053)
XLA Ops:
  3.7 5.0 %collective-permute-start.1 = (f32[2,128,256]{2,1,0:T(8,128)}, f32[2,128,256]{2,1,0:T(8,128)}, u32[]{:S(2)}, u32[]{:S(2)}) collective-permute-start(f32[2,128,256]{2,1,0:T(8,128)} %dynamic-slice_bitcast_fusion.12), channel_id=1, source_target_pairs={{0,4},{1,0},{2,12},{3,8},{4,5},{5,1},{6,13},{7,9},{8,6},{9,2},{10,... | collective-permute-start | bytes 786440 | tf_op jit(solution)/shard_map/ppermute | solution.py:104
  8.7 3.5 collective-permute-start.2
  14.1 4.6 %fusion.185 = (f32[1,2,512,512]{3,2,1,0:T(8,128)}, f32[1,2,512,512]{3,2,1,0:T(8,128)}) fusion(f32[1,5,512,512]{3,2,1,0:T(8,128)} %param.8), kind=kLoop, calls=%fused_computation.361 | loop fusion | bytes 8388608 | tf_op jit(solution)/shard_map/slice | solution.py:174
  28.7 3.2 maximum_multiply_fusion
  32.0 3.6 maximum_multiply_fusion.1
  47.1 3.2 collective-permute-done.12
  51.1 3.3 collective-permute-start.15
  59.3 6.1 %collective-permute-start.10 = (f32[1,128,256]{2,1,0:T(8,128)S(1)}, f32[1,128,256]{2,1,0:T(8,128)S(1)}, u32[]{:S(2)}, u32[]{:S(2)}) collective-permute-start(f32[1,128,256]{2,1,0:T(8,128)S(1)} %fusion.75), channel_id=1, source_target_pairs={{0,12},{1,8},{2,4},{3,0},{4,13},{5,9},{6,5},{7,1},{8,14},{9,10},{1... | collective-permute-start | bytes 393224 | tf_op jit(solution)/shard_map/ppermute | solution.py:104
  67.4 4.7 %collective-permute-start.9 = (f32[1,128,256]{2,1,0:T(8,128)S(1)}, f32[1,128,256]{2,1,0:T(8,128)S(1)}, u32[]{:S(2)}, u32[]{:S(2)}) collective-permute-start(f32[1,128,256]{2,1,0:T(8,128)S(1)} %fusion.75), channel_id=1, source_target_pairs={{0,8},{1,12},{2,0},{3,4},{4,9},{5,13},{6,1},{7,5},{8,10},{9,14},{1... | collective-permute-start | bytes 393224 | tf_op jit(solution)/shard_map/ppermute | solution.py:104
  72.9 6.2 %collective-permute-done.9 = f32[1,128,256]{2,1,0:T(8,128)S(1)} collective-permute-done((f32[1,128,256]{2,1,0:T(8,128)S(1)}, f32[1,128,256]{2,1,0:T(8,128)S(1)}, u32[]{:S(2)}, u32[]{:S(2)}) %collective-permute-start.9) | collective-permute-done | bytes 131104 | tf_op jit(solution)/shard_map/ppermute | solution.py:104
  80.5 3.0 collective-permute-start.19
  86.5 3.8 %collective-permute-done.20 = f32[1,128,256]{2,1,0:T(8,128)S(1)} collective-permute-done((f32[1,128,256]{2,1,0:T(8,128)S(1)}, f32[1,128,256]{2,1,0:T(8,128)S(1)}, u32[]{:S(2)}, u32[]{:S(2)}) %collective-permute-start.20) | collective-permute-done | bytes 131104 | tf_op jit(solution)/shard_map/ppermute | solution.py:104
  92.9 3.8 %collective-permute-start.22 = (f32[1,128,256]{2,1,0:T(8,128)S(1)}, f32[1,128,256]{2,1,0:T(8,128)S(1)}, u32[]{:S(2)}, u32[]{:S(2)}) collective-permute-start(f32[1,128,256]{2,1,0:T(8,128)S(1)} %fusion.71), channel_id=1, source_target_pairs={{0,4},{1,0},{2,12},{3,8},{4,5},{5,1},{6,13},{7,9},{8,6},{9,2},{10,... | collective-permute-start | bytes 393224 | tf_op jit(solution)/shard_map/ppermute | solution.py:104
  96.7 3.8 %collective-permute-start.23 = (f32[1,128,256]{2,1,0:T(8,128)S(1)}, f32[1,128,256]{2,1,0:T(8,128)S(1)}, u32[]{:S(2)}, u32[]{:S(2)}) collective-permute-start(f32[1,128,256]{2,1,0:T(8,128)S(1)} %fusion.71), channel_id=1, source_target_pairs={{0,8},{1,12},{2,0},{3,4},{4,9},{5,13},{6,1},{7,5},{8,10},{9,14},{1... | collective-permute-start | bytes 393224 | tf_op jit(solution)/shard_map/ppermute | solution.py:104
  100.9 7.0 %collective-permute-done.23 = f32[1,128,256]{2,1,0:T(8,128)S(1)} collective-permute-done((f32[1,128,256]{2,1,0:T(8,128)S(1)}, f32[1,128,256]{2,1,0:T(8,128)S(1)}, u32[]{:S(2)}, u32[]{:S(2)}) %collective-permute-start.23) | collective-permute-done | bytes 131104 | tf_op jit(solution)/shard_map/ppermute | solution.py:104
  125.7 4.8 %collective-permute-start.30 = (f32[1,128,256]{2,1,0:T(8,128)S(1)}, f32[1,128,256]{2,1,0:T(8,128)S(1)}, u32[]{:S(2)}, u32[]{:S(2)}) collective-permute-start(f32[1,128,256]{2,1,0:T(8,128)S(1)} %fusion.68), channel_id=1, source_target_pairs={{0,8},{1,12},{2,0},{3,4},{4,9},{5,13},{6,1},{7,5},{8,10},{9,14},{1... | collective-permute-start | bytes 393224 | tf_op jit(solution)/shard_map/ppermute | solution.py:104
  132.0 5.5 %collective-permute-done.30 = f32[1,128,256]{2,1,0:T(8,128)S(1)} collective-permute-done((f32[1,128,256]{2,1,0:T(8,128)S(1)}, f32[1,128,256]{2,1,0:T(8,128)S(1)}, u32[]{:S(2)}, u32[]{:S(2)}) %collective-permute-start.30) | collective-permute-done | bytes 131104 | tf_op jit(solution)/shard_map/ppermute | solution.py:104
  142.9 3.2 collective-permute-start.33
  148.8 3.1 collective-permute-done.34
  155.0 4.4 %collective-permute-start.37 = (f32[1,128,128]{2,1,0:T(8,128)S(1)}, f32[1,128,128]{2,1,0:T(8,128)S(1)}, u32[]{:S(2)}, u32[]{:S(2)}) collective-permute-start(f32[1,128,128]{2,1,0:T(8,128)S(1)} %fusion.115), channel_id=1, source_target_pairs={{0,4},{1,0},{2,12},{3,8},{4,5},{5,1},{6,13},{7,9},{8,6},{9,2},{10,... | collective-permute-start | bytes 196616 | tf_op jit(solution)/shard_map/ppermute | solution.py:104
  159.4 3.3 collective-permute-start.38
  201.6 3.1 collective-permute-done.50
  225.4 4.2 %collective-permute-done.57 = f32[1,128,256]{2,1,0:T(8,128)S(1)} collective-permute-done((f32[1,128,256]{2,1,0:T(8,128)S(1)}, f32[1,128,256]{2,1,0:T(8,128)S(1)}, u32[]{:S(2)}, u32[]{:S(2)}) %collective-permute-start.57) | collective-permute-done | bytes 131104 | tf_op jit(solution)/shard_map/ppermute | solution.py:104
  236.1 6.1 %collective-permute-done.60 = f32[1,128,256]{2,1,0:T(8,128)S(1)} collective-permute-done((f32[1,128,256]{2,1,0:T(8,128)S(1)}, f32[1,128,256]{2,1,0:T(8,128)S(1)}, u32[]{:S(2)}, u32[]{:S(2)}) %collective-permute-start.60) | collective-permute-done | bytes 131104 | tf_op jit(solution)/shard_map/ppermute | solution.py:104
  248.4 3.1 collective-permute-done.64
  263.8 3.3 collective-permute-start.70
  267.1 3.5 fusion.44
  279.6 3.1 collective-permute-done.72
  303.5 7.1 %collective-permute-done.78 = f32[1,128,256]{2,1,0:T(8,128)S(1)} collective-permute-done((f32[1,128,256]{2,1,0:T(8,128)S(1)}, f32[1,128,256]{2,1,0:T(8,128)S(1)}, u32[]{:S(2)}, u32[]{:S(2)}) %collective-permute-start.78) | collective-permute-done | bytes 131104 | tf_op jit(solution)/shard_map/ppermute | solution.py:104
  329.8 3.6 collective-permute-start.86
  341.5 3.0 collective-permute-done.87
  344.6 5.3 %collective-permute-start.89 = (f32[1,128,256]{2,1,0:T(8,128)S(1)}, f32[1,128,256]{2,1,0:T(8,128)S(1)}, u32[]{:S(2)}, u32[]{:S(2)}) collective-permute-start(f32[1,128,256]{2,1,0:T(8,128)S(1)} %fusion.86), channel_id=1, source_target_pairs={{0,1},{1,0},{2,3},{3,2},{4,5},{5,4},{6,7},{7,6},{8,9},{9,8},{10,11... | collective-permute-start | bytes 393224 | tf_op jit(solution)/shard_map/ppermute | solution.py:104
  (387 shorter events, 225.0 us)
Async XLA Ops:
  2.4 33.5 %collective-permute-start = (f32[2,128,256]{2,1,0:T(8,128)}, f32[2,128,256]{2,1,0:T(8,128)}, u32[]{:S(2)}, u32[]{:S(2)}) collective-permute-start(f32[2,128,256]{2,1,0:T(8,128)} %dynamic-slice_bitcast_fusion.12), channel_id=1, source_target_pairs={{1,4},{2,8},{3,12},{4,1},{6,9},{7,13},{8,2},{9,6},{11,14},{12,3},{... | collective-permute-start | bytes 786440 | tf_op jit(solution)/shard_map/ppermute | solution.py:104
  3.7 33.3 %collective-permute-start.1 = (f32[2,128,256]{2,1,0:T(8,128)}, f32[2,128,256]{2,1,0:T(8,128)}, u32[]{:S(2)}, u32[]{:S(2)}) collective-permute-start(f32[2,128,256]{2,1,0:T(8,128)} %dynamic-slice_bitcast_fusion.12), channel_id=1, source_target_pairs={{0,4},{1,0},{2,12},{3,8},{4,5},{5,1},{6,13},{7,9},{8,6},{9,2},{10,... | collective-permute-start | bytes 786440 | tf_op jit(solution)/shard_map/ppermute | solution.py:104
  8.7 28.4 %collective-permute-start.2 = (f32[2,128,256]{2,1,0:T(8,128)}, f32[2,128,256]{2,1,0:T(8,128)}, u32[]{:S(2)}, u32[]{:S(2)}) collective-permute-start(f32[2,128,256]{2,1,0:T(8,128)} %dynamic-slice_bitcast_fusion.12), channel_id=1, source_target_pairs={{0,8},{1,12},{2,0},{3,4},{4,9},{5,13},{6,1},{7,5},{8,10},{9,14},{1... | collective-permute-start | bytes 786440 | tf_op jit(solution)/shard_map/ppermute | solution.py:104
  12.2 24.9 %collective-permute-start.3 = (f32[2,128,256]{2,1,0:T(8,128)}, f32[2,128,256]{2,1,0:T(8,128)}, u32[]{:S(2)}, u32[]{:S(2)}) collective-permute-start(f32[2,128,256]{2,1,0:T(8,128)} %dynamic-slice_bitcast_fusion.12), channel_id=1, source_target_pairs={{0,12},{1,8},{2,4},{3,0},{4,13},{5,9},{6,5},{7,1},{8,14},{9,10},{1... | collective-permute-start | bytes 786440 | tf_op jit(solution)/shard_map/ppermute | solution.py:104
  43.1 11.2 %collective-permute-start.4 = (f32[1,128,256]{2,1,0:T(8,128)S(1)}, f32[1,128,256]{2,1,0:T(8,128)S(1)}, u32[]{:S(2)}, u32[]{:S(2)}) collective-permute-start(f32[1,128,256]{2,1,0:T(8,128)S(1)} %get-tuple-element.116), channel_id=1, source_target_pairs={{0,1},{1,0},{2,3},{3,2},{4,5},{5,4},{6,7},{7,6},{8,9},{9,8},{10,11... | collective-permute-start | bytes 393224 | tf_op jit(solution)/shard_map/ppermute | solution.py:104
  44.8 12.4 %collective-permute-start.5 = (f32[1,128,256]{2,1,0:T(8,128)S(1)}, f32[1,128,256]{2,1,0:T(8,128)S(1)}, u32[]{:S(2)}, u32[]{:S(2)}) collective-permute-start(f32[1,128,256]{2,1,0:T(8,128)S(1)} %get-tuple-element.118), channel_id=1, source_target_pairs={{0,2},{1,3},{2,0},{3,1},{4,6},{5,7},{6,4},{7,5},{8,10},{9,11},{10,... | collective-permute-start | bytes 393224 | tf_op jit(solution)/shard_map/ppermute | solution.py:104
  45.4 13.2 %collective-permute-start.6 = (f32[1,128,256]{2,1,0:T(8,128)S(1)}, f32[1,128,256]{2,1,0:T(8,128)S(1)}, u32[]{:S(2)}, u32[]{:S(2)}) collective-permute-start(f32[1,128,256]{2,1,0:T(8,128)S(1)} %get-tuple-element.117), channel_id=1, source_target_pairs={{0,3},{1,2},{2,1},{3,0},{4,7},{5,6},{6,5},{7,4},{8,11},{9,10},{10,... | collective-permute-start | bytes 393224 | tf_op jit(solution)/shard_map/ppermute | solution.py:104
  51.1 14.4 %collective-permute-start.15 = (f32[1,128,256]{2,1,0:T(8,128)S(1)}, f32[1,128,256]{2,1,0:T(8,128)S(1)}, u32[]{:S(2)}, u32[]{:S(2)}) collective-permute-start(f32[1,128,256]{2,1,0:T(8,128)S(1)} %fusion.73), channel_id=1, source_target_pairs={{0,4},{1,0},{2,12},{3,8},{4,5},{5,1},{6,13},{7,9},{8,6},{9,2},{10,... | collective-permute-start | bytes 393224 | tf_op jit(solution)/shard_map/ppermute | solution.py:104
  54.3 13.1 %collective-permute-start.16 = (f32[1,128,256]{2,1,0:T(8,128)S(1)}, f32[1,128,256]{2,1,0:T(8,128)S(1)}, u32[]{:S(2)}, u32[]{:S(2)}) collective-permute-start(f32[1,128,256]{2,1,0:T(8,128)S(1)} %fusion.73), channel_id=1, source_target_pairs={{0,8},{1,12},{2,0},{3,4},{4,9},{5,13},{6,1},{7,5},{8,10},{9,14},{1... | collective-permute-start | bytes 393224 | tf_op jit(solution)/shard_map/ppermute | solution.py:104
  57.2 14.9 %collective-permute-start.17 = (f32[1,128,256]{2,1,0:T(8,128)S(1)}, f32[1,128,256]{2,1,0:T(8,128)S(1)}, u32[]{:S(2)}, u32[]{:S(2)}) collective-permute-start(f32[1,128,256]{2,1,0:T(8,128)S(1)} %fusion.73), channel_id=1, source_target_pairs={{0,12},{1,8},{2,4},{3,0},{4,13},{5,9},{6,5},{7,1},{8,14},{9,10},{1... | collective-permute-start | bytes 393224 | tf_op jit(solution)/shard_map/ppermute | solution.py:104
  58.7 14.1 %collective-permute-start.7 = (f32[1,128,256]{2,1,0:T(8,128)S(1)}, f32[1,128,256]{2,1,0:T(8,128)S(1)}, u32[]{:S(2)}, u32[]{:S(2)}) collective-permute-start(f32[1,128,256]{2,1,0:T(8,128)S(1)} %fusion.75), channel_id=1, source_target_pairs={{1,4},{2,8},{3,12},{4,1},{6,9},{7,13},{8,2},{9,6},{11,14},{12,3},{... | collective-permute-start | bytes 393224 | tf_op jit(solution)/shard_map/ppermute | solution.py:104
  59.3 13.5 %collective-permute-start.10 = (f32[1,128,256]{2,1,0:T(8,128)S(1)}, f32[1,128,256]{2,1,0:T(8,128)S(1)}, u32[]{:S(2)}, u32[]{:S(2)}) collective-permute-start(f32[1,128,256]{2,1,0:T(8,128)S(1)} %fusion.75), channel_id=1, source_target_pairs={{0,12},{1,8},{2,4},{3,0},{4,13},{5,9},{6,5},{7,1},{8,14},{9,10},{1... | collective-permute-start | bytes 393224 | tf_op jit(solution)/shard_map/ppermute | solution.py:104
  67.4 11.7 %collective-permute-start.9 = (f32[1,128,256]{2,1,0:T(8,128)S(1)}, f32[1,128,256]{2,1,0:T(8,128)S(1)}, u32[]{:S(2)}, u32[]{:S(2)}) collective-permute-start(f32[1,128,256]{2,1,0:T(8,128)S(1)} %fusion.75), channel_id=1, source_target_pairs={{0,8},{1,12},{2,0},{3,4},{4,9},{5,13},{6,1},{7,5},{8,10},{9,14},{1... | collective-permute-start | bytes 393224 | tf_op jit(solution)/shard_map/ppermute | solution.py:104
  91.2 9.6 %collective-permute-start.21 = (f32[1,128,256]{2,1,0:T(8,128)S(1)}, f32[1,128,256]{2,1,0:T(8,128)S(1)}, u32[]{:S(2)}, u32[]{:S(2)}) collective-permute-start(f32[1,128,256]{2,1,0:T(8,128)S(1)} %fusion.71), channel_id=1, source_target_pairs={{1,4},{2,8},{3,12},{4,1},{6,9},{7,13},{8,2},{9,6},{11,14},{12,3},{... | collective-permute-start | bytes 393224 | tf_op jit(solution)/shard_map/ppermute | solution.py:104
  96.7 11.2 %collective-permute-start.23 = (f32[1,128,256]{2,1,0:T(8,128)S(1)}, f32[1,128,256]{2,1,0:T(8,128)S(1)}, u32[]{:S(2)}, u32[]{:S(2)}) collective-permute-start(f32[1,128,256]{2,1,0:T(8,128)S(1)} %fusion.71), channel_id=1, source_target_pairs={{0,8},{1,12},{2,0},{3,4},{4,9},{5,13},{6,1},{7,5},{8,10},{9,14},{1... | collective-permute-start | bytes 393224 | tf_op jit(solution)/shard_map/ppermute | solution.py:104
  120.7 11.2 %collective-permute-start.28 = (f32[1,128,256]{2,1,0:T(8,128)S(1)}, f32[1,128,256]{2,1,0:T(8,128)S(1)}, u32[]{:S(2)}, u32[]{:S(2)}) collective-permute-start(f32[1,128,256]{2,1,0:T(8,128)S(1)} %fusion.68), channel_id=1, source_target_pairs={{1,4},{2,8},{3,12},{4,1},{6,9},{7,13},{8,2},{9,6},{11,14},{12,3},{... | collective-permute-start | bytes 393224 | tf_op jit(solution)/shard_map/ppermute | solution.py:104
  125.7 11.8 %collective-permute-start.30 = (f32[1,128,256]{2,1,0:T(8,128)S(1)}, f32[1,128,256]{2,1,0:T(8,128)S(1)}, u32[]{:S(2)}, u32[]{:S(2)}) collective-permute-start(f32[1,128,256]{2,1,0:T(8,128)S(1)} %fusion.68), channel_id=1, source_target_pairs={{0,8},{1,12},{2,0},{3,4},{4,9},{5,13},{6,1},{7,5},{8,10},{9,14},{1... | collective-permute-start | bytes 393224 | tf_op jit(solution)/shard_map/ppermute | solution.py:104
  153.0 9.7 %collective-permute-start.36 = (f32[1,128,128]{2,1,0:T(8,128)S(1)}, f32[1,128,128]{2,1,0:T(8,128)S(1)}, u32[]{:S(2)}, u32[]{:S(2)}) collective-permute-start(f32[1,128,128]{2,1,0:T(8,128)S(1)} %fusion.115), channel_id=1, source_target_pairs={{1,4},{2,8},{3,12},{4,1},{6,9},{7,13},{8,2},{9,6},{11,14},{12,3},{... | collective-permute-start | bytes 196616 | tf_op jit(solution)/shard_map/ppermute | solution.py:104
  229.8 12.5 %collective-permute-start.60 = (f32[1,128,256]{2,1,0:T(8,128)S(1)}, f32[1,128,256]{2,1,0:T(8,128)S(1)}, u32[]{:S(2)}, u32[]{:S(2)}) collective-permute-start(f32[1,128,256]{2,1,0:T(8,128)S(1)} %get-tuple-element.74), channel_id=1, source_target_pairs={{0,8},{1,9},{2,10},{3,11},{4,12},{5,13},{6,14},{7,15},{8,0},{9,1},... | collective-permute-start | bytes 393224 | tf_op jit(solution)/shard_map/ppermute | solution.py:104
  231.6 10.6 %collective-permute-start.61 = (f32[1,128,256]{2,1,0:T(8,128)S(1)}, f32[1,128,256]{2,1,0:T(8,128)S(1)}, u32[]{:S(2)}, u32[]{:S(2)}) collective-permute-start(f32[1,128,256]{2,1,0:T(8,128)S(1)} %get-tuple-element.73), channel_id=1, source_target_pairs={{0,12},{1,13},{2,14},{3,15},{4,8},{5,9},{6,10},{7,11},{8,4},{9,5},... | collective-permute-start | bytes 393224 | tf_op jit(solution)/shard_map/ppermute | solution.py:104
  263.4 9.7 %collective-permute-start.69 = (f32[1,128,256]{2,1,0:T(8,128)S(1)}, f32[1,128,256]{2,1,0:T(8,128)S(1)}, u32[]{:S(2)}, u32[]{:S(2)}) collective-permute-start(f32[1,128,256]{2,1,0:T(8,128)S(1)} %get-tuple-element.71), channel_id=1, source_target_pairs={{0,8},{1,9},{2,10},{3,11},{4,12},{5,13},{6,14},{7,15},{8,0},{9,1},... | collective-permute-start | bytes 393224 | tf_op jit(solution)/shard_map/ppermute | solution.py:104
  294.9 15.7 %collective-permute-start.78 = (f32[1,128,256]{2,1,0:T(8,128)S(1)}, f32[1,128,256]{2,1,0:T(8,128)S(1)}, u32[]{:S(2)}, u32[]{:S(2)}) collective-permute-start(f32[1,128,256]{2,1,0:T(8,128)S(1)} %get-tuple-element.62), channel_id=1, source_target_pairs={{0,8},{1,9},{2,10},{3,11},{4,12},{5,13},{6,14},{7,15},{8,0},{9,1},... | collective-permute-start | bytes 393224 | tf_op jit(solution)/shard_map/ppermute | solution.py:104
  295.0 15.5 %collective-permute-start.79 = (f32[1,128,256]{2,1,0:T(8,128)S(1)}, f32[1,128,256]{2,1,0:T(8,128)S(1)}, u32[]{:S(2)}, u32[]{:S(2)}) collective-permute-start(f32[1,128,256]{2,1,0:T(8,128)S(1)} %get-tuple-element.61), channel_id=1, source_target_pairs={{0,12},{1,13},{2,14},{3,15},{4,8},{5,9},{6,10},{7,11},{8,4},{9,5},... | collective-permute-start | bytes 393224 | tf_op jit(solution)/shard_map/ppermute | solution.py:104
  297.7 15.2 %collective-permute-start.95 = (f32[1,128,256]{2,1,0:T(8,128)S(1)}, f32[1,128,256]{2,1,0:T(8,128)S(1)}, u32[]{:S(2)}, u32[]{:S(2)}) collective-permute-start(f32[1,128,256]{2,1,0:T(8,128)S(1)} %get-tuple-element.66), channel_id=1, source_target_pairs={{0,4},{1,5},{2,6},{3,7},{4,0},{5,1},{6,2},{7,3},{8,12},{9,13},{10,... | collective-permute-start | bytes 393224 | tf_op jit(solution)/shard_map/ppermute | solution.py:104
  298.7 15.5 %collective-permute-start.96 = (f32[1,128,256]{2,1,0:T(8,128)S(1)}, f32[1,128,256]{2,1,0:T(8,128)S(1)}, u32[]{:S(2)}, u32[]{:S(2)}) collective-permute-start(f32[1,128,256]{2,1,0:T(8,128)S(1)} %get-tuple-element.68), channel_id=1, source_target_pairs={{0,8},{1,9},{2,10},{3,11},{4,12},{5,13},{6,14},{7,15},{8,0},{9,1},... | collective-permute-start | bytes 393224 | tf_op jit(solution)/shard_map/ppermute | solution.py:104
  301.5 12.7 %collective-permute-start.97 = (f32[1,128,256]{2,1,0:T(8,128)S(1)}, f32[1,128,256]{2,1,0:T(8,128)S(1)}, u32[]{:S(2)}, u32[]{:S(2)}) collective-permute-start(f32[1,128,256]{2,1,0:T(8,128)S(1)} %get-tuple-element.67), channel_id=1, source_target_pairs={{0,12},{1,13},{2,14},{3,15},{4,8},{5,9},{6,10},{7,11},{8,4},{9,5},... | collective-permute-start | bytes 393224 | tf_op jit(solution)/shard_map/ppermute | solution.py:104
  314.3 9.6 %collective-permute-start.100 = (f32[1,128,256]{2,1,0:T(8,128)S(1)}, f32[1,128,256]{2,1,0:T(8,128)S(1)}, u32[]{:S(2)}, u32[]{:S(2)}) collective-permute-start(f32[1,128,256]{2,1,0:T(8,128)S(1)} %add_subtract_fusion), channel_id=1, source_target_pairs={{0,3},{1,2},{2,1},{3,0},{4,7},{5,6},{6,5},{7,4},{8,11},{9,10},{10,... | collective-permute-start | bytes 393224 | tf_op jit(solution)/shard_map/ppermute | solution.py:104
  333.4 11.1 %collective-permute-start.87 = (f32[1,128,256]{2,1,0:T(8,128)S(1)}, f32[1,128,256]{2,1,0:T(8,128)S(1)}, u32[]{:S(2)}, u32[]{:S(2)}) collective-permute-start(f32[1,128,256]{2,1,0:T(8,128)S(1)} %get-tuple-element.59), channel_id=1, source_target_pairs={{0,8},{1,9},{2,10},{3,11},{4,12},{5,13},{6,14},{7,15},{8,0},{9,1},... | collective-permute-start | bytes 393224 | tf_op jit(solution)/shard_map/ppermute | solution.py:104
  334.3 10.1 %collective-permute-start.88 = (f32[1,128,256]{2,1,0:T(8,128)S(1)}, f32[1,128,256]{2,1,0:T(8,128)S(1)}, u32[]{:S(2)}, u32[]{:S(2)}) collective-permute-start(f32[1,128,256]{2,1,0:T(8,128)S(1)} %get-tuple-element.58), channel_id=1, source_target_pairs={{0,12},{1,13},{2,14},{3,15},{4,8},{5,9},{6,10},{7,11},{8,4},{9,5},... | collective-permute-start | bytes 393224 | tf_op jit(solution)/shard_map/ppermute | solution.py:104
  335.9 14.0 %collective-permute-start.104 = (f32[1,128,256]{2,1,0:T(8,128)S(1)}, f32[1,128,256]{2,1,0:T(8,128)S(1)}, u32[]{:S(2)}, u32[]{:S(2)}) collective-permute-start(f32[1,128,256]{2,1,0:T(8,128)S(1)} %get-tuple-element.63), channel_id=1, source_target_pairs={{0,4},{1,5},{2,6},{3,7},{4,0},{5,1},{6,2},{7,3},{8,12},{9,13},{10,... | collective-permute-start | bytes 393224 | tf_op jit(solution)/shard_map/ppermute | solution.py:104
  337.8 13.6 %collective-permute-start.105 = (f32[1,128,256]{2,1,0:T(8,128)S(1)}, f32[1,128,256]{2,1,0:T(8,128)S(1)}, u32[]{:S(2)}, u32[]{:S(2)}) collective-permute-start(f32[1,128,256]{2,1,0:T(8,128)S(1)} %get-tuple-element.65), channel_id=1, source_target_pairs={{0,8},{1,9},{2,10},{3,11},{4,12},{5,13},{6,14},{7,15},{8,0},{9,1},... | collective-permute-start | bytes 393224 | tf_op jit(solution)/shard_map/ppermute | solution.py:104
  338.9 12.6 %collective-permute-start.106 = (f32[1,128,256]{2,1,0:T(8,128)S(1)}, f32[1,128,256]{2,1,0:T(8,128)S(1)}, u32[]{:S(2)}, u32[]{:S(2)}) collective-permute-start(f32[1,128,256]{2,1,0:T(8,128)S(1)} %get-tuple-element.64), channel_id=1, source_target_pairs={{0,12},{1,13},{2,14},{3,15},{4,8},{5,9},{6,10},{7,11},{8,4},{9,5},... | collective-permute-start | bytes 393224 | tf_op jit(solution)/shard_map/ppermute | solution.py:104
  (131 other events, 1398.5 us)

commit v4 on v3

--- a/solution.py
+++ b/solution.py
@@ -124,67 +124,55 @@
     def chunk(value, index):
         return lax.dynamic_slice_in_dim(value, index * size, size, value.ndim - 2)
 
-    def ordered(value, turn, axis):
-        parts = [
-            lax.dynamic_slice_in_dim(value, (turn ^ k) * size, size, axis) for k in range(SIDE)
-        ]
-        return jnp.concatenate(parts, axis=axis)
-
-    def arranged(matrices):
-        return ordered(ordered(matrices, j, 1), i, 2)
+    def natural(parts, turn):
+        return jnp.concatenate([pick(parts, turn ^ k) for k in range(SIDE)], axis=1)
 
     def reduce_rows(partial):
-        parts = [partial[:, k * size : (k + 1) * size] for k in range(SIDE)]
-        moved = [send(parts[k], lambda a, b: (a, b ^ k)) for k in range(1, SIDE)]
-        return parts[0] + moved[0] + moved[1] + moved[2]
-
-    def gather_parts(value):
-        return [value] + [send(value, lambda a, b: (a, b ^ k)) for k in range(1, SIDE)]
+        moved = [send(chunk(partial, j ^ k), lambda a, b: (a, b ^ k)) for k in range(1, SIDE)]
+        return chunk(partial, j) + moved[0] + moved[1] + moved[2]
 
     def gather_rows(value):
-        return jnp.concatenate(gather_parts(value), axis=1)
+        parts = [send(value, lambda a, b: (a, b ^ k)) for k in range(1, SIDE)]
+        return natural([value] + parts, j)
 
     def gather_columns(value):
         parts = [send(value, lambda a, b: (b ^ k, a)) for k in range(SIDE)]
         parts[0] = jnp.where(i == j, value, parts[0])
-        return jnp.concatenate(parts, axis=1)
+        return natural(parts, i)
 
     def reduce_columns(partial):
-        parts = [chunk(partial, i ^ j ^ k) for k in range(SIDE)]
-        near = [parts[0]] + [send(parts[k], lambda a, b: (a, b ^ k)) for k in range(1, SIDE)]
+        near = [chunk(partial, j)] + [
+            send(chunk(partial, j ^ k), lambda a, b: (a, b ^ k)) for k in range(1, SIDE)
+        ]
         parts = [pick(near, i ^ j ^ k) for k in range(SIDE)]
         moved = [send(parts[k], lambda a, b: (a ^ k, b)) for k in range(1, SIDE)]
         return parts[0] + moved[0] + moved[1] + moved[2]
 
-    def natural(parts):
-        return jnp.concatenate([pick(parts, j ^ k) for k in range(SIDE)], axis=1)
-
     def columns(value, which):
         return lax.dynamic_slice_in_dim(value, which * half, half, value.ndim - 1)
 
-    order = lax.iota(jnp.int32, rows_here)
-    row_tiles = (i * rows_here + ((order // size) ^ j) * size + order % size) // TILE
-    col_tiles = (j * cols_here + ((order // size) ^ i) * size + order % size) // TILE
+    row_tiles = (i * rows_here + lax.iota(jnp.int32, rows_here)) // TILE
+    col_tiles = (j * cols_here + lax.iota(jnp.int32, cols_here)) // TILE
     tiles = lax.iota(jnp.int32, tile_mask.shape[2])
     row_pick = (row_tiles[:, None] == tiles[None]).astype(jnp.float32)
     col_pick = (tiles[:, None] == col_tiles[None]).astype(jnp.float32)
 
     def blocks(first, last):
         rows = jnp.einsum("rt,ntu->nru", row_pick, tile_mask[0, first:last].astype(jnp.float32))
-        return arranged(coupling[0, first:last]) * jnp.einsum("nru,uc->nrc", rows, col_pick)
+        return coupling[0, first:last] * jnp.einsum("nru,uc->nrc", rows, col_pick)
 
     rhs = chunk(sketch[0], j)
     root_rhs = chunk(root_sketch, j)
 
-    lower = arranged(diag_inverse[0, 0:2])
+    lower = diag_inverse[0, 0:2]
     first = gather_columns(rhs[0:2])
     leaves, fed = [], []
     for a in range(2):
         leaves.append(reduce_rows(dot(lower[a : a + 1], first[a : a + 1])))
         fed.append(gather_columns(leaves[a]))
     to_mid, to_root, mid_root = blocks(0, 2), blocks(2, 4), blocks(4, 5)
-    upper = arranged(diag_inverse[0, 2:3])
-    root = arranged(root_inverse[None])
+    upper = diag_inverse[0, 2:3]
+    root = root_inverse[None]
     mid_part = dot(to_mid[0:1], fed[0]) + dot(to_mid[1:2], fed[1])
     mid_rhs = rhs[2:3] - reduce_rows(mid_part)
     root_part = dot(to_root[0:1], fed[0]) + dot(to_root[1:2], fed[1])
@@ -206,17 +194,15 @@
 
     from_root = dot_t(to_root, both(root_rows))
     mid_back = middle - reduce_columns(dot_t(mid_root, root_rows))
-    mid_parts = gather_parts(reduce_columns(dot_t(upper, gather_rows(mid_back))))
-    mid_rows = jnp.concatenate(mid_parts, axis=1)
+    mid_rows = gather_rows(reduce_columns(dot_t(upper, gather_rows(mid_back))))
     solved = []
     for a in range(2):
         leaf = slice(a, a + 1)
         terms = from_root[leaf] + dot_t(to_mid[leaf], mid_rows)
         leaf_back = leaves[a] - reduce_columns(terms)
-        solved.append(natural(gather_parts(reduce_columns(dot_t(lower[leaf], gather_rows(leaf_back))))))
-    solved = jnp.concatenate(solved + [natural(mid_parts)], axis=0)
-    root_parts = [root_rows[:, k * size : (k + 1) * size] for k in range(SIDE)]
-    return solved[None], natural(root_parts)[0]
+        solved.append(gather_rows(reduce_columns(dot_t(lower[leaf], gather_rows(leaf_back)))))
+    solved = jnp.concatenate(solved + [mid_rows], axis=0)
+    return solved[None], root_rows[0]
 
 
 def solution(mesh):

time: 362 us -> 347 us (0.959)
  local copies, waits for them, and re-layouts: 23.7 us -> 7.67 us
  other arithmetic: 18.5 us -> 12 us
  starting transfers between devices: 175 us -> 181 us
    dynamic_slice x9 -> x0, local copies, waits for them, and re-layouts: 9.6 us -> none  [ordered(): lax.dynamic_slice_in_dim(value, (turn ^ k) * size, size, axis)]
    slice x13 -> x1, local copies, waits for them, and re-layouts: 7.28 us -> 0.01 us  [per_device_square(): mid_rhs = rhs[2:3] - reduce_rows(mid_part)]
    ppermute x108, starting transfers between devices: 175 us -> 181 us  [send(): return lax.ppermute(value, GRID, pairs)]
    concatenate x9 -> x2, other arithmetic: 3.79 us -> 0.09 us  [natural(): return jnp.concatenate([pick(parts, turn ^ k) for k in range(SIDE)], axis=1)]
  transfers between devices with their start and end apart: 110 -> 110, of which waited for: 53 -> 57; matrix products, arithmetic and copies ran while one was open for 10% -> 6% of each run, Pallas kernels for 0% -> 0%
where the time goes in v4:
time: 347 us; the launch traced here: 346 us
  starting transfers between devices  181 us (52%)
  waiting for transfers between devices  116 us (33%)
  matrix products  26.7 us (8%)
  other arithmetic  12 us (3%)
  local copies, waits for them, and re-layouts  7.67 us (2%)
    ppermute x108, starting transfers between devices, send(): return lax.ppermute(value, GRID, pairs)  181 us
    ppermute x108, waiting for transfers between devices, send(): return lax.ppermute(value, GRID, pairs)  113 us
    dot_general x8, matrix products, dot_t(): jnp.einsum('nij,nik->njk', matrices, vectors, precision=lax.Precision.HIGH)  9.56 us
    dot_general x3, matrix products, blocks(): return coupling[0, first:last] * jnp.einsum('nru,uc->nrc', rows, col_pick)  9 us
    dot_general x9, matrix products, dot(): jnp.einsum('nij,njk->nik', matrices, vectors, precision=lax.Precision.HIGH)  8.11 us
  transfers between devices with their start and end apart: 110, of which 57 were waited for; matrix products, arithmetic and copies ran while one was open for 6% of the time, Pallas kernels for 0%

profile of v4, /device:TPU:0, one launch (start us, length us, event | category | flops | bytes accessed | tf_op | source)
XLA Modules:
  0.0 345.8 jit_solution(6387269485360473766)
XLA Ops:
  2.2 4.1 %collective-permute-start.2 = (f32[2,128,256]{1,2,0:T(8,128)S(1)}, f32[2,128,256]{1,2,0:T(8,128)S(1)}, u32[]{:S(2)}, u32[]{:S(2)}) collective-permute-start(f32[2,128,256]{1,2,0:T(8,128)S(1)} %bitcast.382), channel_id=1, source_target_pairs={{0,8},{1,12},{2,0},{3,4},{4,9},{5,13},{6,1},{7,5},{8,10},{9,14},{1... | collective-permute-start | bytes 786440 | tf_op jit(solution)/shard_map/ppermute | solution.py:104
  6.3 3.3 collective-permute-start.3
  11.2 3.6 %bitcast_multiply_fusion = f32[2,512,512]{2,1,0:T(8,128)} fusion(f32[1,5,512,512]{3,2,1,0:T(8,128)} %param.8, s32[512]{0:T(512)S(1)} %get-tuple-element.131, s32[1,5,16,16]{3,2,1,0:T(8,128)} %param.9, s32[512]{0:T(512)S(1)} %get-tuple-element.130), kind=kOutput, calls=%fused_computation | convolution fusion | flops 17842688 | bytes 4214784 | tf_op jit(solution)/shard_map/nru,uc->nrc/dot_general | solution.py:162
  18.7 4.5 %collective-permute-done.1 = f32[2,128,256]{1,2,0:T(8,128)S(1)} collective-permute-done((f32[2,128,256]{1,2,0:T(8,128)S(1)}, f32[2,128,256]{1,2,0:T(8,128)S(1)}, u32[]{:S(2)}, u32[]{:S(2)}) %collective-permute-start.1) | collective-permute-done | bytes 262176 | tf_op jit(solution)/shard_map/ppermute | solution.py:104
  25.9 8.6 %collective-permute-start.6 = (f32[1,128,256]{1,2,0:T(8,128)S(1)}, f32[1,128,256]{1,2,0:T(8,128)S(1)}, u32[]{:S(2)}, u32[]{:S(2)}) collective-permute-start(f32[1,128,256]{1,2,0:T(8,128)S(1)} %get-tuple-element.105), channel_id=1, source_target_pairs={{0,3},{1,2},{2,1},{3,0},{4,7},{5,6},{6,5},{7,4},{8,11},{9,10},{10,... | collective-permute-start | bytes 393224 | tf_op jit(solution)/shard_map/ppermute | solution.py:104
  34.5 4.3 %collective-permute-start.5 = (f32[1,128,256]{1,2,0:T(8,128)S(1)}, f32[1,128,256]{1,2,0:T(8,128)S(1)}, u32[]{:S(2)}, u32[]{:S(2)}) collective-permute-start(f32[1,128,256]{1,2,0:T(8,128)S(1)} %get-tuple-element.106), channel_id=1, source_target_pairs={{0,2},{1,3},{2,0},{3,1},{4,6},{5,7},{6,4},{7,5},{8,10},{9,11},{10,... | collective-permute-start | bytes 393224 | tf_op jit(solution)/shard_map/ppermute | solution.py:104
  47.5 3.0 collective-permute-start.10
  53.0 4.6 %collective-permute-start.16 = (f32[1,128,256]{1,2,0:T(8,128)S(1)}, f32[1,128,256]{1,2,0:T(8,128)S(1)}, u32[]{:S(2)}, u32[]{:S(2)}) collective-permute-start(f32[1,128,256]{1,2,0:T(8,128)S(1)} %fusion.78), channel_id=1, source_target_pairs={{0,8},{1,12},{2,0},{3,4},{4,9},{5,13},{6,1},{7,5},{8,10},{9,14},{1... | collective-permute-start | bytes 393224 | tf_op jit(solution)/shard_map/ppermute | solution.py:104
  57.6 3.8 %collective-permute-start.17 = (f32[1,128,256]{1,2,0:T(8,128)S(1)}, f32[1,128,256]{1,2,0:T(8,128)S(1)}, u32[]{:S(2)}, u32[]{:S(2)}) collective-permute-start(f32[1,128,256]{1,2,0:T(8,128)S(1)} %fusion.78), channel_id=1, source_target_pairs={{0,12},{1,8},{2,4},{3,0},{4,13},{5,9},{6,5},{7,1},{8,14},{9,10},{1... | collective-permute-start | bytes 393224 | tf_op jit(solution)/shard_map/ppermute | solution.py:104
  63.9 2.7 collective-permute-done.15
  67.5 10.3 %collective-permute-start.20 = (f32[1,128,256]{1,2,0:T(8,128)S(1)}, f32[1,128,256]{1,2,0:T(8,128)S(1)}, u32[]{:S(2)}, u32[]{:S(2)}) collective-permute-start(f32[1,128,256]{1,2,0:T(8,128)S(1)} %bitcast.386), channel_id=1, source_target_pairs={{0,3},{1,2},{2,1},{3,0},{4,7},{5,6},{6,5},{7,4},{8,11},{9,10},{10,... | collective-permute-start | bytes 393224 | tf_op jit(solution)/shard_map/ppermute | solution.py:104
  78.7 3.7 %bitcast_multiply_fusion.1 = f32[2,512,512]{2,1,0:T(8,128)} fusion(f32[1,5,512,512]{3,2,1,0:T(8,128)} %param.8, s32[512]{0:T(512)S(1)} %get-tuple-element.131, s32[512]{0:T(512)S(1)} %get-tuple-element.130, s32[1,5,16,16]{3,2,1,0:T(8,128)} %param.9), kind=kOutput, calls=%fused_computation.1 | convolution fusion | flops 17842688 | bytes 4214784 | tf_op jit(solution)/shard_map/nru,uc->nrc/dot_general | solution.py:162
  97.0 11.3 %collective-permute-start.27 = (f32[1,128,256]{1,2,0:T(8,128)S(1)}, f32[1,128,256]{1,2,0:T(8,128)S(1)}, u32[]{:S(2)}, u32[]{:S(2)}) collective-permute-start(f32[1,128,256]{1,2,0:T(8,128)S(1)} %get-tuple-element.86), channel_id=1, source_target_pairs={{0,3},{1,2},{2,1},{3,0},{4,7},{5,6},{6,5},{7,4},{8,11},{9,10},{10,... | collective-permute-start | bytes 393224 | tf_op jit(solution)/shard_map/ppermute | solution.py:104
  111.3 4.7 %collective-permute-done.26 = f32[1,128,256]{1,2,0:T(8,128)S(1)} collective-permute-done((f32[1,128,256]{1,2,0:T(8,128)S(1)}, f32[1,128,256]{1,2,0:T(8,128)S(1)}, u32[]{:S(2)}, u32[]{:S(2)}) %collective-permute-start.26) | collective-permute-done | bytes 131104 | tf_op jit(solution)/shard_map/ppermute | solution.py:104
  119.4 3.0 collective-permute-done.30
  127.7 8.3 %collective-permute-start.35 = (f32[1,128,128]{2,1,0:T(8,128)S(1)}, f32[1,128,128]{2,1,0:T(8,128)S(1)}, u32[]{:S(2)}, u32[]{:S(2)}) collective-permute-start(f32[1,128,128]{2,1,0:T(8,128)S(1)} %get-tuple-element.128), channel_id=1, source_target_pairs={{0,3},{1,2},{2,1},{3,0},{4,7},{5,6},{6,5},{7,4},{8,11},{9,10},{10,... | collective-permute-start | bytes 196616 | tf_op jit(solution)/shard_map/ppermute | solution.py:104
  142.3 2.8 collective-permute-start.39
  152.1 8.6 %collective-permute-start.42 = (f32[1,128,128]{1,2,0:T(8,128)S(1)}, f32[1,128,128]{1,2,0:T(8,128)S(1)}, u32[]{:S(2)}, u32[]{:S(2)}) collective-permute-start(f32[1,128,128]{1,2,0:T(8,128)S(1)} %get-tuple-element.122), channel_id=1, source_target_pairs={{0,3},{1,2},{2,1},{3,0},{4,7},{5,6},{6,5},{7,4},{8,11},{9,10},{10,... | collective-permute-start | bytes 196616 | tf_op jit(solution)/shard_map/ppermute | solution.py:104
  183.1 3.9 %collective-permute-start.51 = (f32[1,128,128]{1,2,0:T(8,128)}, f32[1,128,128]{1,2,0:T(8,128)S(1)}, u32[]{:S(2)}, u32[]{:S(2)}) collective-permute-start(f32[1,128,128]{1,2,0:T(8,128)} %get-tuple-element.108), channel_id=1, source_target_pairs={{0,12},{1,13},{2,14},{3,15},{4,8},{5,9},{6,10},{7,11},{8,4},{9,5},... | collective-permute-start | bytes 196616 | tf_op jit(solution)/shard_map/ppermute | solution.py:104
  189.5 2.7 collective-permute-done.50
  196.5 2.6 collective-permute-done.54
  216.8 3.9 %collective-permute-done.61 = f32[1,128,256]{1,2,0:T(8,128)S(1)} collective-permute-done((f32[1,128,256]{1,2,0:T(8,128)S(1)}, f32[1,128,256]{1,2,0:T(8,128)S(1)}, u32[]{:S(2)}, u32[]{:S(2)}) %collective-permute-start.61) | collective-permute-done | bytes 131104 | tf_op jit(solution)/shard_map/ppermute | solution.py:104
  220.7 4.9 %collective-permute-done.60 = f32[1,128,256]{1,2,0:T(8,128)S(1)} collective-permute-done((f32[1,128,256]{1,2,0:T(8,128)S(1)}, f32[1,128,256]{1,2,0:T(8,128)S(1)}, u32[]{:S(2)}, u32[]{:S(2)}) %collective-permute-start.60) | collective-permute-done | bytes 131104 | tf_op jit(solution)/shard_map/ppermute | solution.py:104
  244.8 3.0 collective-permute-start.70
  252.4 3.4 collective-permute-done.69
  260.6 2.6 fusion.54
  273.0 2.9 collective-permute-done.93
  286.2 7.0 %collective-permute-done.96 = f32[1,128,256]{1,2,0:T(8,128)S(1)} collective-permute-done((f32[1,128,256]{1,2,0:T(8,128)S(1)}, f32[1,128,256]{1,2,0:T(8,128)S(1)}, u32[]{:S(2)}, u32[]{:S(2)}) %collective-permute-start.96) | collective-permute-done | bytes 131104 | tf_op jit(solution)/shard_map/ppermute | solution.py:104
  299.3 3.2 collective-permute-done.99
  326.4 2.9 collective-permute-done.105
  332.9 3.1 collective-permute-done.87
  339.7 2.9 collective-permute-done.90
  (309 shorter events, 199.8 us)
Async XLA Ops:
  2.2 14.9 %collective-permute-start.2 = (f32[2,128,256]{1,2,0:T(8,128)S(1)}, f32[2,128,256]{1,2,0:T(8,128)S(1)}, u32[]{:S(2)}, u32[]{:S(2)}) collective-permute-start(f32[2,128,256]{1,2,0:T(8,128)S(1)} %bitcast.382), channel_id=1, source_target_pairs={{0,8},{1,12},{2,0},{3,4},{4,9},{5,13},{6,1},{7,5},{8,10},{9,14},{1... | collective-permute-start | bytes 786440 | tf_op jit(solution)/shard_map/ppermute | solution.py:104
  6.3 12.4 %collective-permute-start.3 = (f32[2,128,256]{1,2,0:T(8,128)S(1)}, f32[2,128,256]{1,2,0:T(8,128)S(1)}, u32[]{:S(2)}, u32[]{:S(2)}) collective-permute-start(f32[2,128,256]{1,2,0:T(8,128)S(1)} %bitcast.383), channel_id=1, source_target_pairs={{0,12},{1,8},{2,4},{3,0},{4,13},{5,9},{6,5},{7,1},{8,14},{9,10},{1... | collective-permute-start | bytes 786440 | tf_op jit(solution)/shard_map/ppermute | solution.py:104
  9.6 13.5 %collective-permute-start.1 = (f32[2,128,256]{1,2,0:T(8,128)S(1)}, f32[2,128,256]{1,2,0:T(8,128)S(1)}, u32[]{:S(2)}, u32[]{:S(2)}) collective-permute-start(f32[2,128,256]{1,2,0:T(8,128)S(1)} %bitcast.384), channel_id=1, source_target_pairs={{0,4},{1,0},{2,12},{3,8},{4,5},{5,1},{6,13},{7,9},{8,6},{9,2},{10,... | collective-permute-start | bytes 786440 | tf_op jit(solution)/shard_map/ppermute | solution.py:104
  10.3 12.9 %collective-permute-start = (f32[2,128,256]{1,2,0:T(8,128)S(1)}, f32[2,128,256]{1,2,0:T(8,128)S(1)}, u32[]{:S(2)}, u32[]{:S(2)}) collective-permute-start(f32[2,128,256]{1,2,0:T(8,128)S(1)} %bitcast.385), channel_id=1, source_target_pairs={{1,4},{2,8},{3,12},{4,1},{6,9},{7,13},{8,2},{9,6},{11,14},{12,3},{... | collective-permute-start | bytes 786440 | tf_op jit(solution)/shard_map/ppermute | solution.py:104
  25.9 17.2 %collective-permute-start.6 = (f32[1,128,256]{1,2,0:T(8,128)S(1)}, f32[1,128,256]{1,2,0:T(8,128)S(1)}, u32[]{:S(2)}, u32[]{:S(2)}) collective-permute-start(f32[1,128,256]{1,2,0:T(8,128)S(1)} %get-tuple-element.105), channel_id=1, source_target_pairs={{0,3},{1,2},{2,1},{3,0},{4,7},{5,6},{6,5},{7,4},{8,11},{9,10},{10,... | collective-permute-start | bytes 393224 | tf_op jit(solution)/shard_map/ppermute | solution.py:104
  34.5 10.5 %collective-permute-start.5 = (f32[1,128,256]{1,2,0:T(8,128)S(1)}, f32[1,128,256]{1,2,0:T(8,128)S(1)}, u32[]{:S(2)}, u32[]{:S(2)}) collective-permute-start(f32[1,128,256]{1,2,0:T(8,128)S(1)} %get-tuple-element.106), channel_id=1, source_target_pairs={{0,2},{1,3},{2,0},{3,1},{4,6},{5,7},{6,4},{7,5},{8,10},{9,11},{10,... | collective-permute-start | bytes 393224 | tf_op jit(solution)/shard_map/ppermute | solution.py:104
  40.9 9.7 %collective-permute-start.13 = (f32[1,128,256]{1,2,0:T(8,128)S(1)}, f32[1,128,256]{1,2,0:T(8,128)S(1)}, u32[]{:S(2)}, u32[]{:S(2)}) collective-permute-start(f32[1,128,256]{1,2,0:T(8,128)S(1)} %get-tuple-element.99), channel_id=1, source_target_pairs={{0,3},{1,2},{2,1},{3,0},{4,7},{5,6},{6,5},{7,4},{8,11},{9,10},{10,... | collective-permute-start | bytes 393224 | tf_op jit(solution)/shard_map/ppermute | solution.py:104
  42.4 9.9 %collective-permute-start.12 = (f32[1,128,256]{1,2,0:T(8,128)S(1)}, f32[1,128,256]{1,2,0:T(8,128)S(1)}, u32[]{:S(2)}, u32[]{:S(2)}) collective-permute-start(f32[1,128,256]{1,2,0:T(8,128)S(1)} %get-tuple-element.100), channel_id=1, source_target_pairs={{0,2},{1,3},{2,0},{3,1},{4,6},{5,7},{6,4},{7,5},{8,10},{9,11},{10,... | collective-permute-start | bytes 393224 | tf_op jit(solution)/shard_map/ppermute | solution.py:104
  43.0 9.9 %collective-permute-start.11 = (f32[1,128,256]{1,2,0:T(8,128)S(1)}, f32[1,128,256]{1,2,0:T(8,128)S(1)}, u32[]{:S(2)}, u32[]{:S(2)}) collective-permute-start(f32[1,128,256]{1,2,0:T(8,128)S(1)} %get-tuple-element.98), channel_id=1, source_target_pairs={{0,1},{1,0},{2,3},{3,2},{4,5},{5,4},{6,7},{7,6},{8,9},{9,8},{10,11... | collective-permute-start | bytes 393224 | tf_op jit(solution)/shard_map/ppermute | solution.py:104
  46.9 10.7 %collective-permute-start.9 = (f32[1,128,256]{1,2,0:T(8,128)S(1)}, f32[1,128,256]{1,2,0:T(8,128)S(1)}, u32[]{:S(2)}, u32[]{:S(2)}) collective-permute-start(f32[1,128,256]{1,2,0:T(8,128)S(1)} %fusion.80), channel_id=1, source_target_pairs={{0,8},{1,12},{2,0},{3,4},{4,9},{5,13},{6,1},{7,5},{8,10},{9,14},{1... | collective-permute-start | bytes 393224 | tf_op jit(solution)/shard_map/ppermute | solution.py:104
  47.5 13.9 %collective-permute-start.10 = (f32[1,128,256]{1,2,0:T(8,128)S(1)}, f32[1,128,256]{1,2,0:T(8,128)S(1)}, u32[]{:S(2)}, u32[]{:S(2)}) collective-permute-start(f32[1,128,256]{1,2,0:T(8,128)S(1)} %fusion.80), channel_id=1, source_target_pairs={{0,12},{1,8},{2,4},{3,0},{4,13},{5,9},{6,5},{7,1},{8,14},{9,10},{1... | collective-permute-start | bytes 393224 | tf_op jit(solution)/shard_map/ppermute | solution.py:104
  50.5 10.9 %collective-permute-start.8 = (f32[1,128,256]{1,2,0:T(8,128)S(1)}, f32[1,128,256]{1,2,0:T(8,128)S(1)}, u32[]{:S(2)}, u32[]{:S(2)}) collective-permute-start(f32[1,128,256]{1,2,0:T(8,128)S(1)} %fusion.80), channel_id=1, source_target_pairs={{0,4},{1,0},{2,12},{3,8},{4,5},{5,1},{6,13},{7,9},{8,6},{9,2},{10,... | collective-permute-start | bytes 393224 | tf_op jit(solution)/shard_map/ppermute | solution.py:104
  52.3 9.8 %collective-permute-start.7 = (f32[1,128,256]{1,2,0:T(8,128)S(1)}, f32[1,128,256]{1,2,0:T(8,128)S(1)}, u32[]{:S(2)}, u32[]{:S(2)}) collective-permute-start(f32[1,128,256]{1,2,0:T(8,128)S(1)} %fusion.80), channel_id=1, source_target_pairs={{1,4},{2,8},{3,12},{4,1},{6,9},{7,13},{8,2},{9,6},{11,14},{12,3},{... | collective-permute-start | bytes 393224 | tf_op jit(solution)/shard_map/ppermute | solution.py:104
  53.0 9.8 %collective-permute-start.16 = (f32[1,128,256]{1,2,0:T(8,128)S(1)}, f32[1,128,256]{1,2,0:T(8,128)S(1)}, u32[]{:S(2)}, u32[]{:S(2)}) collective-permute-start(f32[1,128,256]{1,2,0:T(8,128)S(1)} %fusion.78), channel_id=1, source_target_pairs={{0,8},{1,12},{2,0},{3,4},{4,9},{5,13},{6,1},{7,5},{8,10},{9,14},{1... | collective-permute-start | bytes 393224 | tf_op jit(solution)/shard_map/ppermute | solution.py:104
  67.5 15.1 %collective-permute-start.20 = (f32[1,128,256]{1,2,0:T(8,128)S(1)}, f32[1,128,256]{1,2,0:T(8,128)S(1)}, u32[]{:S(2)}, u32[]{:S(2)}) collective-permute-start(f32[1,128,256]{1,2,0:T(8,128)S(1)} %bitcast.386), channel_id=1, source_target_pairs={{0,3},{1,2},{2,1},{3,0},{4,7},{5,6},{6,5},{7,4},{8,11},{9,10},{10,... | collective-permute-start | bytes 393224 | tf_op jit(solution)/shard_map/ppermute | solution.py:104
  97.0 14.3 %collective-permute-start.27 = (f32[1,128,256]{1,2,0:T(8,128)S(1)}, f32[1,128,256]{1,2,0:T(8,128)S(1)}, u32[]{:S(2)}, u32[]{:S(2)}) collective-permute-start(f32[1,128,256]{1,2,0:T(8,128)S(1)} %get-tuple-element.86), channel_id=1, source_target_pairs={{0,3},{1,2},{2,1},{3,0},{4,7},{5,6},{6,5},{7,4},{8,11},{9,10},{10,... | collective-permute-start | bytes 393224 | tf_op jit(solution)/shard_map/ppermute | solution.py:104
  127.7 10.7 %collective-permute-start.35 = (f32[1,128,128]{2,1,0:T(8,128)S(1)}, f32[1,128,128]{2,1,0:T(8,128)S(1)}, u32[]{:S(2)}, u32[]{:S(2)}) collective-permute-start(f32[1,128,128]{2,1,0:T(8,128)S(1)} %get-tuple-element.128), channel_id=1, source_target_pairs={{0,3},{1,2},{2,1},{3,0},{4,7},{5,6},{6,5},{7,4},{8,11},{9,10},{10,... | collective-permute-start | bytes 196616 | tf_op jit(solution)/shard_map/ppermute | solution.py:104
  152.1 11.3 %collective-permute-start.42 = (f32[1,128,128]{1,2,0:T(8,128)S(1)}, f32[1,128,128]{1,2,0:T(8,128)S(1)}, u32[]{:S(2)}, u32[]{:S(2)}) collective-permute-start(f32[1,128,128]{1,2,0:T(8,128)S(1)} %get-tuple-element.122), channel_id=1, source_target_pairs={{0,3},{1,2},{2,1},{3,0},{4,7},{5,6},{6,5},{7,4},{8,11},{9,10},{10,... | collective-permute-start | bytes 196616 | tf_op jit(solution)/shard_map/ppermute | solution.py:104
  214.2 11.3 %collective-permute-start.60 = (f32[1,128,256]{1,2,0:T(8,128)S(1)}, f32[1,128,256]{1,2,0:T(8,128)S(1)}, u32[]{:S(2)}, u32[]{:S(2)}) collective-permute-start(f32[1,128,256]{1,2,0:T(8,128)S(1)} %get-tuple-element.75), channel_id=1, source_target_pairs={{0,8},{1,9},{2,10},{3,11},{4,12},{5,13},{6,14},{7,15},{8,0},{9,1},... | collective-permute-start | bytes 393224 | tf_op jit(solution)/shard_map/ppermute | solution.py:104
  214.6 10.9 %collective-permute-start.59 = (f32[1,128,256]{1,2,0:T(8,128)S(1)}, f32[1,128,256]{1,2,0:T(8,128)S(1)}, u32[]{:S(2)}, u32[]{:S(2)}) collective-permute-start(f32[1,128,256]{1,2,0:T(8,128)S(1)} %get-tuple-element.73), channel_id=1, source_target_pairs={{0,4},{1,5},{2,6},{3,7},{4,0},{5,1},{6,2},{7,3},{8,12},{9,13},{10,... | collective-permute-start | bytes 393224 | tf_op jit(solution)/shard_map/ppermute | solution.py:104
  279.3 13.9 %collective-permute-start.96 = (f32[1,128,256]{1,2,0:T(8,128)S(1)}, f32[1,128,256]{1,2,0:T(8,128)S(1)}, u32[]{:S(2)}, u32[]{:S(2)}) collective-permute-start(f32[1,128,256]{1,2,0:T(8,128)S(1)} %get-tuple-element.30), channel_id=1, source_target_pairs={{0,8},{1,9},{2,10},{3,11},{4,12},{5,13},{6,14},{7,15},{8,0},{9,1},... | collective-permute-start | bytes 393224 | tf_op jit(solution)/shard_map/ppermute | solution.py:104
  279.4 13.9 %collective-permute-start.95 = (f32[1,128,256]{1,2,0:T(8,128)S(1)}, f32[1,128,256]{1,2,0:T(8,128)S(1)}, u32[]{:S(2)}, u32[]{:S(2)}) collective-permute-start(f32[1,128,256]{1,2,0:T(8,128)S(1)} %get-tuple-element.28), channel_id=1, source_target_pairs={{0,4},{1,5},{2,6},{3,7},{4,0},{5,1},{6,2},{7,3},{8,12},{9,13},{10,... | collective-permute-start | bytes 393224 | tf_op jit(solution)/shard_map/ppermute | solution.py:104
  281.8 13.8 %collective-permute-start.79 = (f32[1,128,256]{1,2,0:T(8,128)S(1)}, f32[1,128,256]{1,2,0:T(8,128)S(1)}, u32[]{:S(2)}, u32[]{:S(2)}) collective-permute-start(f32[1,128,256]{1,2,0:T(8,128)S(1)} %get-tuple-element.23), channel_id=1, source_target_pairs={{0,12},{1,13},{2,14},{3,15},{4,8},{5,9},{6,10},{7,11},{8,4},{9,5},... | collective-permute-start | bytes 393224 | tf_op jit(solution)/shard_map/ppermute | solution.py:104
  283.9 13.0 %collective-permute-start.78 = (f32[1,128,256]{1,2,0:T(8,128)S(1)}, f32[1,128,256]{1,2,0:T(8,128)S(1)}, u32[]{:S(2)}, u32[]{:S(2)}) collective-permute-start(f32[1,128,256]{1,2,0:T(8,128)S(1)} %get-tuple-element.24), channel_id=1, source_target_pairs={{0,8},{1,9},{2,10},{3,11},{4,12},{5,13},{6,14},{7,15},{8,0},{9,1},... | collective-permute-start | bytes 393224 | tf_op jit(solution)/shard_map/ppermute | solution.py:104
  285.6 11.3 %collective-permute-start.77 = (f32[1,128,256]{1,2,0:T(8,128)S(1)}, f32[1,128,256]{1,2,0:T(8,128)S(1)}, u32[]{:S(2)}, u32[]{:S(2)}) collective-permute-start(f32[1,128,256]{1,2,0:T(8,128)S(1)} %get-tuple-element.22), channel_id=1, source_target_pairs={{0,4},{1,5},{2,6},{3,7},{4,0},{5,1},{6,2},{7,3},{8,12},{9,13},{10,... | collective-permute-start | bytes 393224 | tf_op jit(solution)/shard_map/ppermute | solution.py:104
  297.0 10.5 %collective-permute-start.81 = (f32[1,128,256]{1,2,0:T(8,128)S(1)}, f32[1,128,256]{1,2,0:T(8,128)S(1)}, u32[]{:S(2)}, u32[]{:S(2)}) collective-permute-start(f32[1,128,256]{1,2,0:T(8,128)S(1)} %add_subtract_fusion.1), channel_id=1, source_target_pairs={{0,2},{1,3},{2,0},{3,1},{4,6},{5,7},{6,4},{7,5},{8,10},{9,11},{10,... | collective-permute-start | bytes 393224 | tf_op jit(solution)/shard_map/ppermute | solution.py:104
  298.3 10.3 %collective-permute-start.82 = (f32[1,128,256]{1,2,0:T(8,128)S(1)}, f32[1,128,256]{1,2,0:T(8,128)S(1)}, u32[]{:S(2)}, u32[]{:S(2)}) collective-permute-start(f32[1,128,256]{1,2,0:T(8,128)S(1)} %add_subtract_fusion.1), channel_id=1, source_target_pairs={{0,3},{1,2},{2,1},{3,0},{4,7},{5,6},{6,5},{7,4},{8,11},{9,10},{10,... | collective-permute-start | bytes 393224 | tf_op jit(solution)/shard_map/ppermute | solution.py:104
  318.2 11.1 %collective-permute-start.105 = (f32[1,128,256]{1,2,0:T(8,128)S(1)}, f32[1,128,256]{1,2,0:T(8,128)S(1)}, u32[]{:S(2)}, u32[]{:S(2)}) collective-permute-start(f32[1,128,256]{1,2,0:T(8,128)S(1)} %get-tuple-element.27), channel_id=1, source_target_pairs={{0,8},{1,9},{2,10},{3,11},{4,12},{5,13},{6,14},{7,15},{8,0},{9,1},... | collective-permute-start | bytes 393224 | tf_op jit(solution)/shard_map/ppermute | solution.py:104
  318.2 11.1 %collective-permute-start.104 = (f32[1,128,256]{1,2,0:T(8,128)S(1)}, f32[1,128,256]{1,2,0:T(8,128)S(1)}, u32[]{:S(2)}, u32[]{:S(2)}) collective-permute-start(f32[1,128,256]{1,2,0:T(8,128)S(1)} %get-tuple-element.25), channel_id=1, source_target_pairs={{0,4},{1,5},{2,6},{3,7},{4,0},{5,1},{6,2},{7,3},{8,12},{9,13},{10,... | collective-permute-start | bytes 393224 | tf_op jit(solution)/shard_map/ppermute | solution.py:104
  320.3 12.0 %collective-permute-start.88 = (f32[1,128,256]{1,2,0:T(8,128)S(1)}, f32[1,128,256]{1,2,0:T(8,128)S(1)}, u32[]{:S(2)}, u32[]{:S(2)}) collective-permute-start(f32[1,128,256]{1,2,0:T(8,128)S(1)} %get-tuple-element.20), channel_id=1, source_target_pairs={{0,12},{1,13},{2,14},{3,15},{4,8},{5,9},{6,10},{7,11},{8,4},{9,5},... | collective-permute-start | bytes 393224 | tf_op jit(solution)/shard_map/ppermute | solution.py:104
  322.7 13.3 %collective-permute-start.87 = (f32[1,128,256]{1,2,0:T(8,128)S(1)}, f32[1,128,256]{1,2,0:T(8,128)S(1)}, u32[]{:S(2)}, u32[]{:S(2)}) collective-permute-start(f32[1,128,256]{1,2,0:T(8,128)S(1)} %get-tuple-element.21), channel_id=1, source_target_pairs={{0,8},{1,9},{2,10},{3,11},{4,12},{5,13},{6,14},{7,15},{8,0},{9,1},... | collective-permute-start | bytes 393224 | tf_op jit(solution)/shard_map/ppermute | solution.py:104
  324.1 12.0 %collective-permute-start.86 = (f32[1,128,256]{1,2,0:T(8,128)S(1)}, f32[1,128,256]{1,2,0:T(8,128)S(1)}, u32[]{:S(2)}, u32[]{:S(2)}) collective-permute-start(f32[1,128,256]{1,2,0:T(8,128)S(1)} %get-tuple-element.19), channel_id=1, source_target_pairs={{0,4},{1,5},{2,6},{3,7},{4,0},{5,1},{6,2},{7,3},{8,12},{9,13},{10,... | collective-permute-start | bytes 393224 | tf_op jit(solution)/shard_map/ppermute | solution.py:104
  (91 other events, 684.8 us)

commit v5 on v4

--- a/solution.py
+++ b/solution.py
@@ -128,7 +128,7 @@
         return jnp.concatenate([pick(parts, turn ^ k) for k in range(SIDE)], axis=1)
 
     def reduce_rows(partial):
-        moved = [send(chunk(partial, j ^ k), lambda a, b: (a, b ^ k)) for k in range(1, SIDE)]
+        moved = [send(chunk(partial, j ^ k), lambda a, b: (a, b ^ k)) for k in (3, 2, 1)]
         return chunk(partial, j) + moved[0] + moved[1] + moved[2]
 
     def gather_rows(value):
@@ -145,7 +145,7 @@
             send(chunk(partial, j ^ k), lambda a, b: (a, b ^ k)) for k in range(1, SIDE)
         ]
         parts = [pick(near, i ^ j ^ k) for k in range(SIDE)]
-        moved = [send(parts[k], lambda a, b: (a ^ k, b)) for k in range(1, SIDE)]
+        moved = [send(parts[k], lambda a, b: (a ^ k, b)) for k in (2, 3, 1)]
         return parts[0] + moved[0] + moved[1] + moved[2]
 
     def columns(value, which):
@@ -181,7 +181,9 @@
 
     mine = columns(root_part, layer) + swap_layers(columns(root_part, 1 - layer))
     root_in = columns(root_rhs, layer)[None] - reduce_rows(mine)
-    root_forward = gather_rows(reduce_rows(dot(root, gather_columns(root_in))))
+    root_forward = dot(root, gather_columns(root_in))
+    root_forward = root_forward + send(root_forward, lambda a, b: (a, b ^ 1))
+    root_forward = root_forward + send(root_forward, lambda a, b: (a, b ^ 2))
     root_half = gather_rows(reduce_columns(dot_t(root, root_forward)))
     other_half = swap_layers(root_half)
     first = layer == 0

time: 347 us -> 342 us (0.986)
  starting transfers between devices: 181 us -> 171 us
  waiting for transfers between devices: 116 us -> 124 us
    ppermute x108 -> x104, starting transfers between devices: 181 us -> 171 us  [send(): return lax.ppermute(value, GRID, pairs)]
    ppermute x108 -> x104, waiting for transfers between devices: 113 us -> 121 us  [send(): return lax.ppermute(value, GRID, pairs)]
  transfers between devices with their start and end apart: 110 -> 106, of which waited for: 57 -> 61; matrix products, arithmetic and copies ran while one was open for 6% -> 6% of each run, Pallas kernels for 0% -> 0%
where the time goes in v5:
time: 342 us
  starting transfers between devices  171 us (50%)
  waiting for transfers between devices  124 us (36%)
  matrix products  25.4 us (7%)
  other arithmetic  12 us (4%)
  local copies, waits for them, and re-layouts  7.63 us (2%)
    ppermute x104, starting transfers between devices, send(): return lax.ppermute(value, GRID, pairs)  171 us
    ppermute x104, waiting for transfers between devices, send(): return lax.ppermute(value, GRID, pairs)  121 us
    dot_general x3, matrix products, blocks(): return coupling[0, first:last] * jnp.einsum('nru,uc->nrc', rows, col_pick)  8.97 us
    dot_general x8, matrix products, dot_t(): jnp.einsum('nij,nik->njk', matrices, vectors, precision=lax.Precision.HIGH)  8.35 us
    dot_general x9, matrix products, dot(): jnp.einsum('nij,njk->nik', matrices, vectors, precision=lax.Precision.HIGH)  8.1 us
  transfers between devices with their start and end apart: 106, of which 61 were waited for; matrix products, arithmetic and copies ran while one was open for 6% of the time, Pallas kernels for 0%

profile of v5, /device:TPU:0, one launch (start us, length us, event | category | flops | bytes accessed | tf_op | source)
XLA Modules:
  0.0 341.5 jit_solution(5504779739577629917)
XLA Ops:
  2.2 4.1 %collective-permute-start.2 = (f32[2,128,256]{1,2,0:T(8,128)S(1)}, f32[2,128,256]{1,2,0:T(8,128)S(1)}, u32[]{:S(2)}, u32[]{:S(2)}) collective-permute-start(f32[2,128,256]{1,2,0:T(8,128)S(1)} %bitcast.366), channel_id=1, source_target_pairs={{0,8},{1,12},{2,0},{3,4},{4,9},{5,13},{6,1},{7,5},{8,10},{9,14},{1... | collective-permute-start | bytes 786440 | tf_op jit(solution)/shard_map/ppermute | solution.py:104
  6.3 3.3 collective-permute-start.3
  11.2 3.6 %bitcast_multiply_fusion = f32[2,512,512]{2,1,0:T(8,128)} fusion(f32[1,5,512,512]{3,2,1,0:T(8,128)} %param.8, s32[512]{0:T(512)S(1)} %get-tuple-element.124, s32[1,5,16,16]{3,2,1,0:T(8,128)} %param.9, s32[512]{0:T(512)S(1)} %get-tuple-element.123), kind=kOutput, calls=%fused_computation | convolution fusion | flops 17842688 | bytes 4214784 | tf_op jit(solution)/shard_map/nru,uc->nrc/dot_general | solution.py:162
  18.7 4.5 %collective-permute-done.1 = f32[2,128,256]{1,2,0:T(8,128)S(1)} collective-permute-done((f32[2,128,256]{1,2,0:T(8,128)S(1)}, f32[2,128,256]{1,2,0:T(8,128)S(1)}, u32[]{:S(2)}, u32[]{:S(2)}) %collective-permute-start.1) | collective-permute-done | bytes 262176 | tf_op jit(solution)/shard_map/ppermute | solution.py:104
  25.9 4.5 %collective-permute-start.6 = (f32[1,128,256]{1,2,0:T(8,128)S(1)}, f32[1,128,256]{1,2,0:T(8,128)S(1)}, u32[]{:S(2)}, u32[]{:S(2)}) collective-permute-start(f32[1,128,256]{1,2,0:T(8,128)S(1)} %get-tuple-element.105), channel_id=1, source_target_pairs={{0,1},{1,0},{2,3},{3,2},{4,5},{5,4},{6,7},{7,6},{8,9},{9,8},{10,11... | collective-permute-start | bytes 393224 | tf_op jit(solution)/shard_map/ppermute | solution.py:104
  30.4 8.4 %collective-permute-start.5 = (f32[1,128,256]{1,2,0:T(8,128)S(1)}, f32[1,128,256]{1,2,0:T(8,128)S(1)}, u32[]{:S(2)}, u32[]{:S(2)}) collective-permute-start(f32[1,128,256]{1,2,0:T(8,128)S(1)} %get-tuple-element.106), channel_id=1, source_target_pairs={{0,2},{1,3},{2,0},{3,1},{4,6},{5,7},{6,4},{7,5},{8,10},{9,11},{10,... | collective-permute-start | bytes 393224 | tf_op jit(solution)/shard_map/ppermute | solution.py:104
  48.9 5.2 %collective-permute-start.10 = (f32[1,128,256]{1,2,0:T(8,128)S(1)}, f32[1,128,256]{1,2,0:T(8,128)S(1)}, u32[]{:S(2)}, u32[]{:S(2)}) collective-permute-start(f32[1,128,256]{1,2,0:T(8,128)S(1)} %fusion.75), channel_id=1, source_target_pairs={{0,12},{1,8},{2,4},{3,0},{4,13},{5,9},{6,5},{7,1},{8,14},{9,10},{1... | collective-permute-start | bytes 393224 | tf_op jit(solution)/shard_map/ppermute | solution.py:104
  54.9 5.4 %collective-permute-start.16 = (f32[1,128,256]{1,2,0:T(8,128)S(1)}, f32[1,128,256]{1,2,0:T(8,128)S(1)}, u32[]{:S(2)}, u32[]{:S(2)}) collective-permute-start(f32[1,128,256]{1,2,0:T(8,128)S(1)} %fusion.73), channel_id=1, source_target_pairs={{0,8},{1,12},{2,0},{3,4},{4,9},{5,13},{6,1},{7,5},{8,10},{9,14},{1... | collective-permute-start | bytes 393224 | tf_op jit(solution)/shard_map/ppermute | solution.py:104
  69.2 4.8 %collective-permute-start.20 = (f32[1,128,256]{1,2,0:T(8,128)S(1)}, f32[1,128,256]{1,2,0:T(8,128)S(1)}, u32[]{:S(2)}, u32[]{:S(2)}) collective-permute-start(f32[1,128,256]{1,2,0:T(8,128)S(1)} %bitcast.370), channel_id=1, source_target_pairs={{0,1},{1,0},{2,3},{3,2},{4,5},{5,4},{6,7},{7,6},{8,9},{9,8},{10,11... | collective-permute-start | bytes 393224 | tf_op jit(solution)/shard_map/ppermute | solution.py:104
  74.1 5.5 %collective-permute-start.19 = (f32[1,128,256]{1,2,0:T(8,128)S(1)}, f32[1,128,256]{1,2,0:T(8,128)S(1)}, u32[]{:S(2)}, u32[]{:S(2)}) collective-permute-start(f32[1,128,256]{1,2,0:T(8,128)S(1)} %bitcast.371), channel_id=1, source_target_pairs={{0,2},{1,3},{2,0},{3,1},{4,6},{5,7},{6,4},{7,5},{8,10},{9,11},{10,... | collective-permute-start | bytes 393224 | tf_op jit(solution)/shard_map/ppermute | solution.py:104
  80.3 3.7 %bitcast_multiply_fusion.1 = f32[2,512,512]{2,1,0:T(8,128)} fusion(f32[1,5,512,512]{3,2,1,0:T(8,128)} %param.8, s32[512]{0:T(512)S(1)} %get-tuple-element.124, s32[512]{0:T(512)S(1)} %get-tuple-element.123, s32[1,5,16,16]{3,2,1,0:T(8,128)} %param.9), kind=kOutput, calls=%fused_computation.1 | convolution fusion | flops 17842688 | bytes 4214784 | tf_op jit(solution)/shard_map/nru,uc->nrc/dot_general | solution.py:162
  89.1 2.7 collective-permute-start.22
  99.0 4.4 %collective-permute-start.27 = (f32[1,128,256]{1,2,0:T(8,128)S(1)}, f32[1,128,256]{1,2,0:T(8,128)S(1)}, u32[]{:S(2)}, u32[]{:S(2)}) collective-permute-start(f32[1,128,256]{1,2,0:T(8,128)S(1)} %get-tuple-element.86), channel_id=1, source_target_pairs={{0,1},{1,0},{2,3},{3,2},{4,5},{5,4},{6,7},{7,6},{8,9},{9,8},{10,11... | collective-permute-start | bytes 393224 | tf_op jit(solution)/shard_map/ppermute | solution.py:104
  103.4 6.5 %collective-permute-start.26 = (f32[1,128,256]{1,2,0:T(8,128)S(1)}, f32[1,128,256]{1,2,0:T(8,128)S(1)}, u32[]{:S(2)}, u32[]{:S(2)}) collective-permute-start(f32[1,128,256]{1,2,0:T(8,128)S(1)} %get-tuple-element.87), channel_id=1, source_target_pairs={{0,2},{1,3},{2,0},{3,1},{4,6},{5,7},{6,4},{7,5},{8,10},{9,11},{10,... | collective-permute-start | bytes 393224 | tf_op jit(solution)/shard_map/ppermute | solution.py:104
  110.5 5.7 %collective-permute-done.26 = f32[1,128,256]{1,2,0:T(8,128)S(1)} collective-permute-done((f32[1,128,256]{1,2,0:T(8,128)S(1)}, f32[1,128,256]{1,2,0:T(8,128)S(1)}, u32[]{:S(2)}, u32[]{:S(2)}) %collective-permute-start.26) | collective-permute-done | bytes 131104 | tf_op jit(solution)/shard_map/ppermute | solution.py:104
  129.2 4.1 %collective-permute-start.35 = (f32[1,128,128]{2,1,0:T(8,128)S(1)}, f32[1,128,128]{2,1,0:T(8,128)S(1)}, u32[]{:S(2)}, u32[]{:S(2)}) collective-permute-start(f32[1,128,128]{2,1,0:T(8,128)S(1)} %get-tuple-element.121), channel_id=1, source_target_pairs={{0,1},{1,0},{2,3},{3,2},{4,5},{5,4},{6,7},{7,6},{8,9},{9,8},{10,11... | collective-permute-start | bytes 196616 | tf_op jit(solution)/shard_map/ppermute | solution.py:104
  133.3 5.1 %collective-permute-start.34 = (f32[1,128,128]{2,1,0:T(8,128)S(1)}, f32[1,128,128]{2,1,0:T(8,128)S(1)}, u32[]{:S(2)}, u32[]{:S(2)}) collective-permute-start(f32[1,128,128]{2,1,0:T(8,128)S(1)} %get-tuple-element.122), channel_id=1, source_target_pairs={{0,2},{1,3},{2,0},{3,1},{4,6},{5,7},{6,4},{7,5},{8,10},{9,11},{10,... | collective-permute-start | bytes 196616 | tf_op jit(solution)/shard_map/ppermute | solution.py:104
  138.4 3.0 collective-permute-done.34
  152.7 4.9 %collective-permute-start.40 = (f32[1,512,128]{1,2,0:T(8,128)S(1)}, f32[1,512,128]{1,2,0:T(8,128)S(1)}, u32[]{:S(2)}, u32[]{:S(2)}) collective-permute-start(f32[1,512,128]{1,2,0:T(8,128)S(1)} %convolution_bitcast_fusion.2), channel_id=1, source_target_pairs={{0,1},{1,0},{2,3},{3,2},{4,5},{5,4},{6,7},{7,6},{8,9},{9,8},{10,11... | collective-permute-start | bytes 786440 | tf_op jit(solution)/shard_map/ppermute | solution.py:104
  157.6 4.4 %collective-permute-done.40 = f32[1,512,128]{1,2,0:T(8,128)S(1)} collective-permute-done((f32[1,512,128]{1,2,0:T(8,128)S(1)}, f32[1,512,128]{1,2,0:T(8,128)S(1)}, u32[]{:S(2)}, u32[]{:S(2)}) %collective-permute-start.40) | collective-permute-done | bytes 262176 | tf_op jit(solution)/shard_map/ppermute | solution.py:104
  162.0 5.7 %collective-permute-start.41 = (f32[1,512,128]{1,2,0:T(8,128)S(1)}, f32[1,512,128]{1,2,0:T(8,128)S(1)}, u32[]{:S(2)}, u32[]{:S(2)}) collective-permute-start(f32[1,512,128]{1,2,0:T(8,128)S(1)} %add.464), channel_id=1, source_target_pairs={{0,2},{1,3},{2,0},{3,1},{4,6},{5,7},{6,4},{7,5},{8,10},{9,11},{10,... | collective-permute-start | bytes 786440 | tf_op jit(solution)/shard_map/ppermute | solution.py:104
  167.7 5.1 %collective-permute-done.41 = f32[1,512,128]{1,2,0:T(8,128)S(1)} collective-permute-done((f32[1,512,128]{1,2,0:T(8,128)S(1)}, f32[1,512,128]{1,2,0:T(8,128)S(1)}, u32[]{:S(2)}, u32[]{:S(2)}) %collective-permute-start.41) | collective-permute-done | bytes 262176 | tf_op jit(solution)/shard_map/ppermute | solution.py:104
  180.3 2.9 collective-permute-done.44
  184.1 3.3 collective-permute-start.45
  208.0 3.8 %collective-permute-done.53 = f32[1,128,256]{1,2,0:T(8,128)S(1)} collective-permute-done((f32[1,128,256]{1,2,0:T(8,128)S(1)}, f32[1,128,256]{1,2,0:T(8,128)S(1)}, u32[]{:S(2)}, u32[]{:S(2)}) %collective-permute-start.53) | collective-permute-done | bytes 131104 | tf_op jit(solution)/shard_map/ppermute | solution.py:104
  215.4 3.0 collective-permute-done.57
  220.8 4.8 %collective-permute-done.55 = f32[1,128,256]{1,2,0:T(8,128)S(1)} collective-permute-done((f32[1,128,256]{1,2,0:T(8,128)S(1)}, f32[1,128,256]{1,2,0:T(8,128)S(1)}, u32[]{:S(2)}, u32[]{:S(2)}) %collective-permute-start.55) | collective-permute-done | bytes 131104 | tf_op jit(solution)/shard_map/ppermute | solution.py:104
  252.4 4.4 %collective-permute-done.64 = f32[1,128,256]{1,2,0:T(8,128)} collective-permute-done((f32[1,128,256]{1,2,0:T(8,128)}, f32[1,128,256]{1,2,0:T(8,128)}, u32[]{:S(2)}, u32[]{:S(2)}) %collective-permute-start.64) | collective-permute-done | bytes 131104 | tf_op jit(solution)/shard_map/ppermute | solution.py:104
  282.2 2.9 collective-permute-done.93
  285.1 8.7 %collective-permute-done.91 = f32[1,128,256]{1,2,0:T(8,128)S(1)} collective-permute-done((f32[1,128,256]{1,2,0:T(8,128)S(1)}, f32[1,128,256]{1,2,0:T(8,128)S(1)}, u32[]{:S(2)}, u32[]{:S(2)}) %collective-permute-start.91) | collective-permute-done | bytes 131104 | tf_op jit(solution)/shard_map/ppermute | solution.py:104
  301.4 3.3 collective-permute-done.94
  322.3 5.9 %collective-permute-done.100 = f32[1,128,256]{1,2,0:T(8,128)S(1)} collective-permute-done((f32[1,128,256]{1,2,0:T(8,128)S(1)}, f32[1,128,256]{1,2,0:T(8,128)S(1)}, u32[]{:S(2)}, u32[]{:S(2)}) %collective-permute-start.100) | collective-permute-done | bytes 131104 | tf_op jit(solution)/shard_map/ppermute | solution.py:104
  (301 shorter events, 192.2 us)
Async XLA Ops:
  2.2 14.9 %collective-permute-start.2 = (f32[2,128,256]{1,2,0:T(8,128)S(1)}, f32[2,128,256]{1,2,0:T(8,128)S(1)}, u32[]{:S(2)}, u32[]{:S(2)}) collective-permute-start(f32[2,128,256]{1,2,0:T(8,128)S(1)} %bitcast.366), channel_id=1, source_target_pairs={{0,8},{1,12},{2,0},{3,4},{4,9},{5,13},{6,1},{7,5},{8,10},{9,14},{1... | collective-permute-start | bytes 786440 | tf_op jit(solution)/shard_map/ppermute | solution.py:104
  6.3 12.4 %collective-permute-start.3 = (f32[2,128,256]{1,2,0:T(8,128)S(1)}, f32[2,128,256]{1,2,0:T(8,128)S(1)}, u32[]{:S(2)}, u32[]{:S(2)}) collective-permute-start(f32[2,128,256]{1,2,0:T(8,128)S(1)} %bitcast.367), channel_id=1, source_target_pairs={{0,12},{1,8},{2,4},{3,0},{4,13},{5,9},{6,5},{7,1},{8,14},{9,10},{1... | collective-permute-start | bytes 786440 | tf_op jit(solution)/shard_map/ppermute | solution.py:104
  9.6 13.5 %collective-permute-start.1 = (f32[2,128,256]{1,2,0:T(8,128)S(1)}, f32[2,128,256]{1,2,0:T(8,128)S(1)}, u32[]{:S(2)}, u32[]{:S(2)}) collective-permute-start(f32[2,128,256]{1,2,0:T(8,128)S(1)} %bitcast.368), channel_id=1, source_target_pairs={{0,4},{1,0},{2,12},{3,8},{4,5},{5,1},{6,13},{7,9},{8,6},{9,2},{10,... | collective-permute-start | bytes 786440 | tf_op jit(solution)/shard_map/ppermute | solution.py:104
  10.3 12.9 %collective-permute-start = (f32[2,128,256]{1,2,0:T(8,128)S(1)}, f32[2,128,256]{1,2,0:T(8,128)S(1)}, u32[]{:S(2)}, u32[]{:S(2)}) collective-permute-start(f32[2,128,256]{1,2,0:T(8,128)S(1)} %bitcast.369), channel_id=1, source_target_pairs={{1,4},{2,8},{3,12},{4,1},{6,9},{7,13},{8,2},{9,6},{11,14},{12,3},{... | collective-permute-start | bytes 786440 | tf_op jit(solution)/shard_map/ppermute | solution.py:104
  25.9 17.2 %collective-permute-start.6 = (f32[1,128,256]{1,2,0:T(8,128)S(1)}, f32[1,128,256]{1,2,0:T(8,128)S(1)}, u32[]{:S(2)}, u32[]{:S(2)}) collective-permute-start(f32[1,128,256]{1,2,0:T(8,128)S(1)} %get-tuple-element.105), channel_id=1, source_target_pairs={{0,1},{1,0},{2,3},{3,2},{4,5},{5,4},{6,7},{7,6},{8,9},{9,8},{10,11... | collective-permute-start | bytes 393224 | tf_op jit(solution)/shard_map/ppermute | solution.py:104
  30.4 14.5 %collective-permute-start.5 = (f32[1,128,256]{1,2,0:T(8,128)S(1)}, f32[1,128,256]{1,2,0:T(8,128)S(1)}, u32[]{:S(2)}, u32[]{:S(2)}) collective-permute-start(f32[1,128,256]{1,2,0:T(8,128)S(1)} %get-tuple-element.106), channel_id=1, source_target_pairs={{0,2},{1,3},{2,0},{3,1},{4,6},{5,7},{6,4},{7,5},{8,10},{9,11},{10,... | collective-permute-start | bytes 393224 | tf_op jit(solution)/shard_map/ppermute | solution.py:104
  40.9 13.3 %collective-permute-start.13 = (f32[1,128,256]{1,2,0:T(8,128)S(1)}, f32[1,128,256]{1,2,0:T(8,128)S(1)}, u32[]{:S(2)}, u32[]{:S(2)}) collective-permute-start(f32[1,128,256]{1,2,0:T(8,128)S(1)} %get-tuple-element.99), channel_id=1, source_target_pairs={{0,1},{1,0},{2,3},{3,2},{4,5},{5,4},{6,7},{7,6},{8,9},{9,8},{10,11... | collective-permute-start | bytes 393224 | tf_op jit(solution)/shard_map/ppermute | solution.py:104
  41.5 12.6 %collective-permute-start.12 = (f32[1,128,256]{1,2,0:T(8,128)S(1)}, f32[1,128,256]{1,2,0:T(8,128)S(1)}, u32[]{:S(2)}, u32[]{:S(2)}) collective-permute-start(f32[1,128,256]{1,2,0:T(8,128)S(1)} %get-tuple-element.100), channel_id=1, source_target_pairs={{0,2},{1,3},{2,0},{3,1},{4,6},{5,7},{6,4},{7,5},{8,10},{9,11},{10,... | collective-permute-start | bytes 393224 | tf_op jit(solution)/shard_map/ppermute | solution.py:104
  43.0 11.8 %collective-permute-start.11 = (f32[1,128,256]{1,2,0:T(8,128)S(1)}, f32[1,128,256]{1,2,0:T(8,128)S(1)}, u32[]{:S(2)}, u32[]{:S(2)}) collective-permute-start(f32[1,128,256]{1,2,0:T(8,128)S(1)} %get-tuple-element.98), channel_id=1, source_target_pairs={{0,3},{1,2},{2,1},{3,0},{4,7},{5,6},{6,5},{7,4},{8,11},{9,10},{10,... | collective-permute-start | bytes 393224 | tf_op jit(solution)/shard_map/ppermute | solution.py:104
  47.0 13.3 %collective-permute-start.9 = (f32[1,128,256]{1,2,0:T(8,128)S(1)}, f32[1,128,256]{1,2,0:T(8,128)S(1)}, u32[]{:S(2)}, u32[]{:S(2)}) collective-permute-start(f32[1,128,256]{1,2,0:T(8,128)S(1)} %fusion.75), channel_id=1, source_target_pairs={{0,8},{1,12},{2,0},{3,4},{4,9},{5,13},{6,1},{7,5},{8,10},{9,14},{1... | collective-permute-start | bytes 393224 | tf_op jit(solution)/shard_map/ppermute | solution.py:104
  48.9 14.0 %collective-permute-start.10 = (f32[1,128,256]{1,2,0:T(8,128)S(1)}, f32[1,128,256]{1,2,0:T(8,128)S(1)}, u32[]{:S(2)}, u32[]{:S(2)}) collective-permute-start(f32[1,128,256]{1,2,0:T(8,128)S(1)} %fusion.75), channel_id=1, source_target_pairs={{0,12},{1,8},{2,4},{3,0},{4,13},{5,9},{6,5},{7,1},{8,14},{9,10},{1... | collective-permute-start | bytes 393224 | tf_op jit(solution)/shard_map/ppermute | solution.py:104
  54.1 9.5 %collective-permute-start.7 = (f32[1,128,256]{1,2,0:T(8,128)S(1)}, f32[1,128,256]{1,2,0:T(8,128)S(1)}, u32[]{:S(2)}, u32[]{:S(2)}) collective-permute-start(f32[1,128,256]{1,2,0:T(8,128)S(1)} %fusion.75), channel_id=1, source_target_pairs={{1,4},{2,8},{3,12},{4,1},{6,9},{7,13},{8,2},{9,6},{11,14},{12,3},{... | collective-permute-start | bytes 393224 | tf_op jit(solution)/shard_map/ppermute | solution.py:104
  54.9 9.5 %collective-permute-start.16 = (f32[1,128,256]{1,2,0:T(8,128)S(1)}, f32[1,128,256]{1,2,0:T(8,128)S(1)}, u32[]{:S(2)}, u32[]{:S(2)}) collective-permute-start(f32[1,128,256]{1,2,0:T(8,128)S(1)} %fusion.73), channel_id=1, source_target_pairs={{0,8},{1,12},{2,0},{3,4},{4,9},{5,13},{6,1},{7,5},{8,10},{9,14},{1... | collective-permute-start | bytes 393224 | tf_op jit(solution)/shard_map/ppermute | solution.py:104
  69.2 15.0 %collective-permute-start.20 = (f32[1,128,256]{1,2,0:T(8,128)S(1)}, f32[1,128,256]{1,2,0:T(8,128)S(1)}, u32[]{:S(2)}, u32[]{:S(2)}) collective-permute-start(f32[1,128,256]{1,2,0:T(8,128)S(1)} %bitcast.370), channel_id=1, source_target_pairs={{0,1},{1,0},{2,3},{3,2},{4,5},{5,4},{6,7},{7,6},{8,9},{9,8},{10,11... | collective-permute-start | bytes 393224 | tf_op jit(solution)/shard_map/ppermute | solution.py:104
  74.1 10.1 %collective-permute-start.19 = (f32[1,128,256]{1,2,0:T(8,128)S(1)}, f32[1,128,256]{1,2,0:T(8,128)S(1)}, u32[]{:S(2)}, u32[]{:S(2)}) collective-permute-start(f32[1,128,256]{1,2,0:T(8,128)S(1)} %bitcast.371), channel_id=1, source_target_pairs={{0,2},{1,3},{2,0},{3,1},{4,6},{5,7},{6,4},{7,5},{8,10},{9,11},{10,... | collective-permute-start | bytes 393224 | tf_op jit(solution)/shard_map/ppermute | solution.py:104
  99.0 11.5 %collective-permute-start.27 = (f32[1,128,256]{1,2,0:T(8,128)S(1)}, f32[1,128,256]{1,2,0:T(8,128)S(1)}, u32[]{:S(2)}, u32[]{:S(2)}) collective-permute-start(f32[1,128,256]{1,2,0:T(8,128)S(1)} %get-tuple-element.86), channel_id=1, source_target_pairs={{0,1},{1,0},{2,3},{3,2},{4,5},{5,4},{6,7},{7,6},{8,9},{9,8},{10,11... | collective-permute-start | bytes 393224 | tf_op jit(solution)/shard_map/ppermute | solution.py:104
  103.4 12.8 %collective-permute-start.26 = (f32[1,128,256]{1,2,0:T(8,128)S(1)}, f32[1,128,256]{1,2,0:T(8,128)S(1)}, u32[]{:S(2)}, u32[]{:S(2)}) collective-permute-start(f32[1,128,256]{1,2,0:T(8,128)S(1)} %get-tuple-element.87), channel_id=1, source_target_pairs={{0,2},{1,3},{2,0},{3,1},{4,6},{5,7},{6,4},{7,5},{8,10},{9,11},{10,... | collective-permute-start | bytes 393224 | tf_op jit(solution)/shard_map/ppermute | solution.py:104
  129.2 9.2 %collective-permute-start.35 = (f32[1,128,128]{2,1,0:T(8,128)S(1)}, f32[1,128,128]{2,1,0:T(8,128)S(1)}, u32[]{:S(2)}, u32[]{:S(2)}) collective-permute-start(f32[1,128,128]{2,1,0:T(8,128)S(1)} %get-tuple-element.121), channel_id=1, source_target_pairs={{0,1},{1,0},{2,3},{3,2},{4,5},{5,4},{6,7},{7,6},{8,9},{9,8},{10,11... | collective-permute-start | bytes 196616 | tf_op jit(solution)/shard_map/ppermute | solution.py:104
  152.7 9.2 %collective-permute-start.40 = (f32[1,512,128]{1,2,0:T(8,128)S(1)}, f32[1,512,128]{1,2,0:T(8,128)S(1)}, u32[]{:S(2)}, u32[]{:S(2)}) collective-permute-start(f32[1,512,128]{1,2,0:T(8,128)S(1)} %convolution_bitcast_fusion.2), channel_id=1, source_target_pairs={{0,1},{1,0},{2,3},{3,2},{4,5},{5,4},{6,7},{7,6},{8,9},{9,8},{10,11... | collective-permute-start | bytes 786440 | tf_op jit(solution)/shard_map/ppermute | solution.py:104
  162.0 10.9 %collective-permute-start.41 = (f32[1,512,128]{1,2,0:T(8,128)S(1)}, f32[1,512,128]{1,2,0:T(8,128)S(1)}, u32[]{:S(2)}, u32[]{:S(2)}) collective-permute-start(f32[1,512,128]{1,2,0:T(8,128)S(1)} %add.464), channel_id=1, source_target_pairs={{0,2},{1,3},{2,0},{3,1},{4,6},{5,7},{6,4},{7,5},{8,10},{9,11},{10,... | collective-permute-start | bytes 786440 | tf_op jit(solution)/shard_map/ppermute | solution.py:104
  214.3 11.2 %collective-permute-start.55 = (f32[1,128,256]{1,2,0:T(8,128)S(1)}, f32[1,128,256]{1,2,0:T(8,128)S(1)}, u32[]{:S(2)}, u32[]{:S(2)}) collective-permute-start(f32[1,128,256]{1,2,0:T(8,128)S(1)} %get-tuple-element.73), channel_id=1, source_target_pairs={{0,8},{1,9},{2,10},{3,11},{4,12},{5,13},{6,14},{7,15},{8,0},{9,1},... | collective-permute-start | bytes 393224 | tf_op jit(solution)/shard_map/ppermute | solution.py:104
  246.4 10.3 %collective-permute-start.64 = (f32[1,128,256]{1,2,0:T(8,128)}, f32[1,128,256]{1,2,0:T(8,128)}, u32[]{:S(2)}, u32[]{:S(2)}) collective-permute-start(f32[1,128,256]{1,2,0:T(8,128)} %get-tuple-element.31), channel_id=1, source_target_pairs={{0,8},{1,9},{2,10},{3,11},{4,12},{5,13},{6,14},{7,15},{8,0},{9,1},... | collective-permute-start | bytes 393224 | tf_op jit(solution)/shard_map/ppermute | solution.py:104
  277.7 16.1 %collective-permute-start.91 = (f32[1,128,256]{1,2,0:T(8,128)S(1)}, f32[1,128,256]{1,2,0:T(8,128)S(1)}, u32[]{:S(2)}, u32[]{:S(2)}) collective-permute-start(f32[1,128,256]{1,2,0:T(8,128)S(1)} %get-tuple-element.28), channel_id=1, source_target_pairs={{0,8},{1,9},{2,10},{3,11},{4,12},{5,13},{6,14},{7,15},{8,0},{9,1},... | collective-permute-start | bytes 393224 | tf_op jit(solution)/shard_map/ppermute | solution.py:104
  279.9 15.5 %collective-permute-start.75 = (f32[1,128,256]{1,2,0:T(8,128)S(1)}, f32[1,128,256]{1,2,0:T(8,128)S(1)}, u32[]{:S(2)}, u32[]{:S(2)}) collective-permute-start(f32[1,128,256]{1,2,0:T(8,128)S(1)} %get-tuple-element.23), channel_id=1, source_target_pairs={{0,4},{1,5},{2,6},{3,7},{4,0},{5,1},{6,2},{7,3},{8,12},{9,13},{10,... | collective-permute-start | bytes 393224 | tf_op jit(solution)/shard_map/ppermute | solution.py:104
  280.8 16.6 %collective-permute-start.74 = (f32[1,128,256]{1,2,0:T(8,128)S(1)}, f32[1,128,256]{1,2,0:T(8,128)S(1)}, u32[]{:S(2)}, u32[]{:S(2)}) collective-permute-start(f32[1,128,256]{1,2,0:T(8,128)S(1)} %get-tuple-element.24), channel_id=1, source_target_pairs={{0,12},{1,13},{2,14},{3,15},{4,8},{5,9},{6,10},{7,11},{8,4},{9,5},... | collective-permute-start | bytes 393224 | tf_op jit(solution)/shard_map/ppermute | solution.py:104
  285.1 12.3 %collective-permute-start.73 = (f32[1,128,256]{1,2,0:T(8,128)S(1)}, f32[1,128,256]{1,2,0:T(8,128)S(1)}, u32[]{:S(2)}, u32[]{:S(2)}) collective-permute-start(f32[1,128,256]{1,2,0:T(8,128)S(1)} %get-tuple-element.22), channel_id=1, source_target_pairs={{0,8},{1,9},{2,10},{3,11},{4,12},{5,13},{6,14},{7,15},{8,0},{9,1},... | collective-permute-start | bytes 393224 | tf_op jit(solution)/shard_map/ppermute | solution.py:104
  297.7 11.3 %collective-permute-start.78 = (f32[1,128,256]{1,2,0:T(8,128)S(1)}, f32[1,128,256]{1,2,0:T(8,128)S(1)}, u32[]{:S(2)}, u32[]{:S(2)}) collective-permute-start(f32[1,128,256]{1,2,0:T(8,128)S(1)} %add_subtract_fusion.1), channel_id=1, source_target_pairs={{0,3},{1,2},{2,1},{3,0},{4,7},{5,6},{6,5},{7,4},{8,11},{9,10},{10,... | collective-permute-start | bytes 393224 | tf_op jit(solution)/shard_map/ppermute | solution.py:104
  300.2 9.9 %collective-permute-start.76 = (f32[1,128,256]{1,2,0:T(8,128)S(1)}, f32[1,128,256]{1,2,0:T(8,128)S(1)}, u32[]{:S(2)}, u32[]{:S(2)}) collective-permute-start(f32[1,128,256]{1,2,0:T(8,128)S(1)} %add_subtract_fusion.1), channel_id=1, source_target_pairs={{0,1},{1,0},{2,3},{3,2},{4,5},{5,4},{6,7},{7,6},{8,9},{9,8},{10,11... | collective-permute-start | bytes 393224 | tf_op jit(solution)/shard_map/ppermute | solution.py:104
  315.8 12.3 %collective-permute-start.100 = (f32[1,128,256]{1,2,0:T(8,128)S(1)}, f32[1,128,256]{1,2,0:T(8,128)S(1)}, u32[]{:S(2)}, u32[]{:S(2)}) collective-permute-start(f32[1,128,256]{1,2,0:T(8,128)S(1)} %get-tuple-element.25), channel_id=1, source_target_pairs={{0,8},{1,9},{2,10},{3,11},{4,12},{5,13},{6,14},{7,15},{8,0},{9,1},... | collective-permute-start | bytes 393224 | tf_op jit(solution)/shard_map/ppermute | solution.py:104
  318.0 12.7 %collective-permute-start.84 = (f32[1,128,256]{1,2,0:T(8,128)S(1)}, f32[1,128,256]{1,2,0:T(8,128)S(1)}, u32[]{:S(2)}, u32[]{:S(2)}) collective-permute-start(f32[1,128,256]{1,2,0:T(8,128)S(1)} %get-tuple-element.20), channel_id=1, source_target_pairs={{0,4},{1,5},{2,6},{3,7},{4,0},{5,1},{6,2},{7,3},{8,12},{9,13},{10,... | collective-permute-start | bytes 393224 | tf_op jit(solution)/shard_map/ppermute | solution.py:104
  319.1 12.7 %collective-permute-start.83 = (f32[1,128,256]{1,2,0:T(8,128)S(1)}, f32[1,128,256]{1,2,0:T(8,128)S(1)}, u32[]{:S(2)}, u32[]{:S(2)}) collective-permute-start(f32[1,128,256]{1,2,0:T(8,128)S(1)} %get-tuple-element.21), channel_id=1, source_target_pairs={{0,12},{1,13},{2,14},{3,15},{4,8},{5,9},{6,10},{7,11},{8,4},{9,5},... | collective-permute-start | bytes 393224 | tf_op jit(solution)/shard_map/ppermute | solution.py:104
  322.3 9.5 %collective-permute-start.82 = (f32[1,128,256]{1,2,0:T(8,128)S(1)}, f32[1,128,256]{1,2,0:T(8,128)S(1)}, u32[]{:S(2)}, u32[]{:S(2)}) collective-permute-start(f32[1,128,256]{1,2,0:T(8,128)S(1)} %get-tuple-element.19), channel_id=1, source_target_pairs={{0,8},{1,9},{2,10},{3,11},{4,12},{5,13},{6,14},{7,15},{8,0},{9,1},... | collective-permute-start | bytes 393224 | tf_op jit(solution)/shard_map/ppermute | solution.py:104
  (88 other events, 688.5 us)

commit v6 on v5

--- a/solution.py
+++ b/solution.py
@@ -104,6 +104,10 @@
     return lax.ppermute(value, GRID, pairs)
 
 
+def after(value, earlier):
+    return lax.optimization_barrier((value, earlier))[0]
+
+
 def swap_layers(value):
     return lax.ppermute(value, "layer", [(0, 1), (1, 0)])
 
@@ -194,8 +198,8 @@
     def both(value):
         return jnp.broadcast_to(value, (2,) + value.shape[1:])
 
-    from_root = dot_t(to_root, both(root_rows))
     mid_back = middle - reduce_columns(dot_t(mid_root, root_rows))
+    from_root = dot_t(to_root, both(after(root_rows, mid_back)))
     mid_rows = gather_rows(reduce_columns(dot_t(upper, gather_rows(mid_back))))
     solved = []
     for a in range(2):

time: 342 us -> 342 us (level)
  no operation moved by 1% of the time
where the time goes in v6:
time: 342 us
  starting transfers between devices  171 us (50%)
  waiting for transfers between devices  123 us (36%)
  matrix products  25.4 us (7%)
  other arithmetic  12.1 us (4%)
  local copies, waits for them, and re-layouts  8.62 us (3%)
    ppermute x104, starting transfers between devices, send(): return lax.ppermute(value, GRID, pairs)  171 us
    ppermute x104, waiting for transfers between devices, send(): return lax.ppermute(value, GRID, pairs)  119 us
    dot_general x3, matrix products, blocks(): return coupling[0, first:last] * jnp.einsum('nru,uc->nrc', rows, col_pick)  8.97 us
    dot_general x8, matrix products, dot_t(): jnp.einsum('nij,nik->njk', matrices, vectors, precision=lax.Precision.HIGH)  8.35 us
    dot_general x9, matrix products, dot(): jnp.einsum('nij,njk->nik', matrices, vectors, precision=lax.Precision.HIGH)  8.1 us
  transfers between devices with their start and end apart: 106, of which 61 were waited for; matrix products, arithmetic and copies ran while one was open for 6% of the time, Pallas kernels for 0%

profile of v6, /device:TPU:0, one launch (start us, length us, event | category | flops | bytes accessed | tf_op | source)
XLA Modules:
  0.0 341.5 jit_solution(9758149323660903098)
XLA Ops:
  2.2 4.1 %collective-permute-start.2 = (f32[2,128,256]{1,2,0:T(8,128)S(1)}, f32[2,128,256]{1,2,0:T(8,128)S(1)}, u32[]{:S(2)}, u32[]{:S(2)}) collective-permute-start(f32[2,128,256]{1,2,0:T(8,128)S(1)} %bitcast.369), channel_id=1, source_target_pairs={{0,8},{1,12},{2,0},{3,4},{4,9},{5,13},{6,1},{7,5},{8,10},{9,14},{1... | collective-permute-start | bytes 786440 | tf_op jit(solution)/shard_map/ppermute | solution.py:104
  6.3 3.3 collective-permute-start.3
  11.2 3.6 %bitcast_multiply_fusion = f32[2,512,512]{2,1,0:T(8,128)} fusion(f32[1,5,512,512]{3,2,1,0:T(8,128)} %param.8, s32[512]{0:T(512)S(1)} %get-tuple-element.128, s32[1,5,16,16]{3,2,1,0:T(8,128)} %param.9, s32[512]{0:T(512)S(1)} %get-tuple-element.127), kind=kOutput, calls=%fused_computation | convolution fusion | flops 17842688 | bytes 4214784 | tf_op jit(solution)/shard_map/nru,uc->nrc/dot_general | solution.py:166
  18.7 4.5 %collective-permute-done.1 = f32[2,128,256]{1,2,0:T(8,128)S(1)} collective-permute-done((f32[2,128,256]{1,2,0:T(8,128)S(1)}, f32[2,128,256]{1,2,0:T(8,128)S(1)}, u32[]{:S(2)}, u32[]{:S(2)}) %collective-permute-start.1) | collective-permute-done | bytes 262176 | tf_op jit(solution)/shard_map/ppermute | solution.py:104
  25.9 4.5 %collective-permute-start.6 = (f32[1,128,256]{1,2,0:T(8,128)S(1)}, f32[1,128,256]{1,2,0:T(8,128)S(1)}, u32[]{:S(2)}, u32[]{:S(2)}) collective-permute-start(f32[1,128,256]{1,2,0:T(8,128)S(1)} %get-tuple-element.109), channel_id=1, source_target_pairs={{0,1},{1,0},{2,3},{3,2},{4,5},{5,4},{6,7},{7,6},{8,9},{9,8},{10,11... | collective-permute-start | bytes 393224 | tf_op jit(solution)/shard_map/ppermute | solution.py:104
  30.4 8.4 %collective-permute-start.5 = (f32[1,128,256]{1,2,0:T(8,128)S(1)}, f32[1,128,256]{1,2,0:T(8,128)S(1)}, u32[]{:S(2)}, u32[]{:S(2)}) collective-permute-start(f32[1,128,256]{1,2,0:T(8,128)S(1)} %get-tuple-element.110), channel_id=1, source_target_pairs={{0,2},{1,3},{2,0},{3,1},{4,6},{5,7},{6,4},{7,5},{8,10},{9,11},{10,... | collective-permute-start | bytes 393224 | tf_op jit(solution)/shard_map/ppermute | solution.py:104
  48.9 5.2 %collective-permute-start.10 = (f32[1,128,256]{1,2,0:T(8,128)S(1)}, f32[1,128,256]{1,2,0:T(8,128)S(1)}, u32[]{:S(2)}, u32[]{:S(2)}) collective-permute-start(f32[1,128,256]{1,2,0:T(8,128)S(1)} %fusion.75), channel_id=1, source_target_pairs={{0,12},{1,8},{2,4},{3,0},{4,13},{5,9},{6,5},{7,1},{8,14},{9,10},{1... | collective-permute-start | bytes 393224 | tf_op jit(solution)/shard_map/ppermute | solution.py:104
  54.9 5.4 %collective-permute-start.16 = (f32[1,128,256]{1,2,0:T(8,128)S(1)}, f32[1,128,256]{1,2,0:T(8,128)S(1)}, u32[]{:S(2)}, u32[]{:S(2)}) collective-permute-start(f32[1,128,256]{1,2,0:T(8,128)S(1)} %fusion.73), channel_id=1, source_target_pairs={{0,8},{1,12},{2,0},{3,4},{4,9},{5,13},{6,1},{7,5},{8,10},{9,14},{1... | collective-permute-start | bytes 393224 | tf_op jit(solution)/shard_map/ppermute | solution.py:104
  69.2 4.8 %collective-permute-start.20 = (f32[1,128,256]{1,2,0:T(8,128)S(1)}, f32[1,128,256]{1,2,0:T(8,128)S(1)}, u32[]{:S(2)}, u32[]{:S(2)}) collective-permute-start(f32[1,128,256]{1,2,0:T(8,128)S(1)} %bitcast.373), channel_id=1, source_target_pairs={{0,1},{1,0},{2,3},{3,2},{4,5},{5,4},{6,7},{7,6},{8,9},{9,8},{10,11... | collective-permute-start | bytes 393224 | tf_op jit(solution)/shard_map/ppermute | solution.py:104
  74.1 5.5 %collective-permute-start.19 = (f32[1,128,256]{1,2,0:T(8,128)S(1)}, f32[1,128,256]{1,2,0:T(8,128)S(1)}, u32[]{:S(2)}, u32[]{:S(2)}) collective-permute-start(f32[1,128,256]{1,2,0:T(8,128)S(1)} %bitcast.374), channel_id=1, source_target_pairs={{0,2},{1,3},{2,0},{3,1},{4,6},{5,7},{6,4},{7,5},{8,10},{9,11},{10,... | collective-permute-start | bytes 393224 | tf_op jit(solution)/shard_map/ppermute | solution.py:104
  80.3 3.7 %bitcast_multiply_fusion.1 = f32[2,512,512]{2,1,0:T(8,128)} fusion(f32[1,5,512,512]{3,2,1,0:T(8,128)} %param.8, s32[512]{0:T(512)S(1)} %get-tuple-element.128, s32[512]{0:T(512)S(1)} %get-tuple-element.127, s32[1,5,16,16]{3,2,1,0:T(8,128)} %param.9), kind=kOutput, calls=%fused_computation.1 | convolution fusion | flops 17842688 | bytes 4214784 | tf_op jit(solution)/shard_map/nru,uc->nrc/dot_general | solution.py:166
  89.1 2.7 collective-permute-start.22
  99.0 4.4 %collective-permute-start.27 = (f32[1,128,256]{1,2,0:T(8,128)S(1)}, f32[1,128,256]{1,2,0:T(8,128)S(1)}, u32[]{:S(2)}, u32[]{:S(2)}) collective-permute-start(f32[1,128,256]{1,2,0:T(8,128)S(1)} %get-tuple-element.90), channel_id=1, source_target_pairs={{0,1},{1,0},{2,3},{3,2},{4,5},{5,4},{6,7},{7,6},{8,9},{9,8},{10,11... | collective-permute-start | bytes 393224 | tf_op jit(solution)/shard_map/ppermute | solution.py:104
  103.4 6.5 %collective-permute-start.26 = (f32[1,128,256]{1,2,0:T(8,128)S(1)}, f32[1,128,256]{1,2,0:T(8,128)S(1)}, u32[]{:S(2)}, u32[]{:S(2)}) collective-permute-start(f32[1,128,256]{1,2,0:T(8,128)S(1)} %get-tuple-element.91), channel_id=1, source_target_pairs={{0,2},{1,3},{2,0},{3,1},{4,6},{5,7},{6,4},{7,5},{8,10},{9,11},{10,... | collective-permute-start | bytes 393224 | tf_op jit(solution)/shard_map/ppermute | solution.py:104
  110.5 5.7 %collective-permute-done.26 = f32[1,128,256]{1,2,0:T(8,128)S(1)} collective-permute-done((f32[1,128,256]{1,2,0:T(8,128)S(1)}, f32[1,128,256]{1,2,0:T(8,128)S(1)}, u32[]{:S(2)}, u32[]{:S(2)}) %collective-permute-start.26) | collective-permute-done | bytes 131104 | tf_op jit(solution)/shard_map/ppermute | solution.py:104
  129.2 4.1 %collective-permute-start.35 = (f32[1,128,128]{2,1,0:T(8,128)S(1)}, f32[1,128,128]{2,1,0:T(8,128)S(1)}, u32[]{:S(2)}, u32[]{:S(2)}) collective-permute-start(f32[1,128,128]{2,1,0:T(8,128)S(1)} %get-tuple-element.125), channel_id=1, source_target_pairs={{0,1},{1,0},{2,3},{3,2},{4,5},{5,4},{6,7},{7,6},{8,9},{9,8},{10,11... | collective-permute-start | bytes 196616 | tf_op jit(solution)/shard_map/ppermute | solution.py:104
  133.3 5.1 %collective-permute-start.34 = (f32[1,128,128]{2,1,0:T(8,128)S(1)}, f32[1,128,128]{2,1,0:T(8,128)S(1)}, u32[]{:S(2)}, u32[]{:S(2)}) collective-permute-start(f32[1,128,128]{2,1,0:T(8,128)S(1)} %get-tuple-element.126), channel_id=1, source_target_pairs={{0,2},{1,3},{2,0},{3,1},{4,6},{5,7},{6,4},{7,5},{8,10},{9,11},{10,... | collective-permute-start | bytes 196616 | tf_op jit(solution)/shard_map/ppermute | solution.py:104
  138.4 3.0 collective-permute-done.34
  152.7 4.9 %collective-permute-start.40 = (f32[1,512,128]{1,2,0:T(8,128)S(1)}, f32[1,512,128]{1,2,0:T(8,128)S(1)}, u32[]{:S(2)}, u32[]{:S(2)}) collective-permute-start(f32[1,512,128]{1,2,0:T(8,128)S(1)} %convolution_bitcast_fusion.2), channel_id=1, source_target_pairs={{0,1},{1,0},{2,3},{3,2},{4,5},{5,4},{6,7},{7,6},{8,9},{9,8},{10,11... | collective-permute-start | bytes 786440 | tf_op jit(solution)/shard_map/ppermute | solution.py:104
  157.6 4.4 %collective-permute-done.40 = f32[1,512,128]{1,2,0:T(8,128)S(1)} collective-permute-done((f32[1,512,128]{1,2,0:T(8,128)S(1)}, f32[1,512,128]{1,2,0:T(8,128)S(1)}, u32[]{:S(2)}, u32[]{:S(2)}) %collective-permute-start.40) | collective-permute-done | bytes 262176 | tf_op jit(solution)/shard_map/ppermute | solution.py:104
  162.0 5.7 %collective-permute-start.41 = (f32[1,512,128]{1,2,0:T(8,128)S(1)}, f32[1,512,128]{1,2,0:T(8,128)S(1)}, u32[]{:S(2)}, u32[]{:S(2)}) collective-permute-start(f32[1,512,128]{1,2,0:T(8,128)S(1)} %add.464), channel_id=1, source_target_pairs={{0,2},{1,3},{2,0},{3,1},{4,6},{5,7},{6,4},{7,5},{8,10},{9,11},{10,... | collective-permute-start | bytes 786440 | tf_op jit(solution)/shard_map/ppermute | solution.py:104
  167.7 5.1 %collective-permute-done.41 = f32[1,512,128]{1,2,0:T(8,128)S(1)} collective-permute-done((f32[1,512,128]{1,2,0:T(8,128)S(1)}, f32[1,512,128]{1,2,0:T(8,128)S(1)}, u32[]{:S(2)}, u32[]{:S(2)}) %collective-permute-start.41) | collective-permute-done | bytes 262176 | tf_op jit(solution)/shard_map/ppermute | solution.py:104
  180.3 2.9 collective-permute-done.44
  184.1 3.3 collective-permute-start.45
  208.0 3.8 %collective-permute-done.53 = f32[1,128,256]{1,2,0:T(8,128)S(1)} collective-permute-done((f32[1,128,256]{1,2,0:T(8,128)S(1)}, f32[1,128,256]{1,2,0:T(8,128)S(1)}, u32[]{:S(2)}, u32[]{:S(2)}) %collective-permute-start.53) | collective-permute-done | bytes 131104 | tf_op jit(solution)/shard_map/ppermute | solution.py:104
  215.4 3.0 collective-permute-done.57
  220.8 4.8 %collective-permute-done.55 = f32[1,128,256]{1,2,0:T(8,128)S(1)} collective-permute-done((f32[1,128,256]{1,2,0:T(8,128)S(1)}, f32[1,128,256]{1,2,0:T(8,128)S(1)}, u32[]{:S(2)}, u32[]{:S(2)}) %collective-permute-start.55) | collective-permute-done | bytes 131104 | tf_op jit(solution)/shard_map/ppermute | solution.py:104
  252.4 4.4 %collective-permute-done.64 = f32[1,128,256]{1,2,0:T(8,128)} collective-permute-done((f32[1,128,256]{1,2,0:T(8,128)}, f32[1,128,256]{1,2,0:T(8,128)}, u32[]{:S(2)}, u32[]{:S(2)}) %collective-permute-start.64) | collective-permute-done | bytes 131104 | tf_op jit(solution)/shard_map/ppermute | solution.py:104
  282.2 2.9 collective-permute-done.93
  285.1 8.7 %collective-permute-done.91 = f32[1,128,256]{1,2,0:T(8,128)S(1)} collective-permute-done((f32[1,128,256]{1,2,0:T(8,128)S(1)}, f32[1,128,256]{1,2,0:T(8,128)S(1)}, u32[]{:S(2)}, u32[]{:S(2)}) %collective-permute-start.91) | collective-permute-done | bytes 131104 | tf_op jit(solution)/shard_map/ppermute | solution.py:104
  301.3 3.3 collective-permute-done.94
  322.3 5.9 %collective-permute-done.100 = f32[1,128,256]{1,2,0:T(8,128)S(1)} collective-permute-done((f32[1,128,256]{1,2,0:T(8,128)S(1)}, f32[1,128,256]{1,2,0:T(8,128)S(1)}, u32[]{:S(2)}, u32[]{:S(2)}) %collective-permute-start.100) | collective-permute-done | bytes 131104 | tf_op jit(solution)/shard_map/ppermute | solution.py:104
  (300 shorter events, 192.3 us)
Async XLA Ops:
  2.2 14.9 %collective-permute-start.2 = (f32[2,128,256]{1,2,0:T(8,128)S(1)}, f32[2,128,256]{1,2,0:T(8,128)S(1)}, u32[]{:S(2)}, u32[]{:S(2)}) collective-permute-start(f32[2,128,256]{1,2,0:T(8,128)S(1)} %bitcast.369), channel_id=1, source_target_pairs={{0,8},{1,12},{2,0},{3,4},{4,9},{5,13},{6,1},{7,5},{8,10},{9,14},{1... | collective-permute-start | bytes 786440 | tf_op jit(solution)/shard_map/ppermute | solution.py:104
  6.3 12.4 %collective-permute-start.3 = (f32[2,128,256]{1,2,0:T(8,128)S(1)}, f32[2,128,256]{1,2,0:T(8,128)S(1)}, u32[]{:S(2)}, u32[]{:S(2)}) collective-permute-start(f32[2,128,256]{1,2,0:T(8,128)S(1)} %bitcast.370), channel_id=1, source_target_pairs={{0,12},{1,8},{2,4},{3,0},{4,13},{5,9},{6,5},{7,1},{8,14},{9,10},{1... | collective-permute-start | bytes 786440 | tf_op jit(solution)/shard_map/ppermute | solution.py:104
  9.6 13.5 %collective-permute-start.1 = (f32[2,128,256]{1,2,0:T(8,128)S(1)}, f32[2,128,256]{1,2,0:T(8,128)S(1)}, u32[]{:S(2)}, u32[]{:S(2)}) collective-permute-start(f32[2,128,256]{1,2,0:T(8,128)S(1)} %bitcast.371), channel_id=1, source_target_pairs={{0,4},{1,0},{2,12},{3,8},{4,5},{5,1},{6,13},{7,9},{8,6},{9,2},{10,... | collective-permute-start | bytes 786440 | tf_op jit(solution)/shard_map/ppermute | solution.py:104
  10.3 12.9 %collective-permute-start = (f32[2,128,256]{1,2,0:T(8,128)S(1)}, f32[2,128,256]{1,2,0:T(8,128)S(1)}, u32[]{:S(2)}, u32[]{:S(2)}) collective-permute-start(f32[2,128,256]{1,2,0:T(8,128)S(1)} %bitcast.372), channel_id=1, source_target_pairs={{1,4},{2,8},{3,12},{4,1},{6,9},{7,13},{8,2},{9,6},{11,14},{12,3},{... | collective-permute-start | bytes 786440 | tf_op jit(solution)/shard_map/ppermute | solution.py:104
  25.9 17.2 %collective-permute-start.6 = (f32[1,128,256]{1,2,0:T(8,128)S(1)}, f32[1,128,256]{1,2,0:T(8,128)S(1)}, u32[]{:S(2)}, u32[]{:S(2)}) collective-permute-start(f32[1,128,256]{1,2,0:T(8,128)S(1)} %get-tuple-element.109), channel_id=1, source_target_pairs={{0,1},{1,0},{2,3},{3,2},{4,5},{5,4},{6,7},{7,6},{8,9},{9,8},{10,11... | collective-permute-start | bytes 393224 | tf_op jit(solution)/shard_map/ppermute | solution.py:104
  30.4 14.5 %collective-permute-start.5 = (f32[1,128,256]{1,2,0:T(8,128)S(1)}, f32[1,128,256]{1,2,0:T(8,128)S(1)}, u32[]{:S(2)}, u32[]{:S(2)}) collective-permute-start(f32[1,128,256]{1,2,0:T(8,128)S(1)} %get-tuple-element.110), channel_id=1, source_target_pairs={{0,2},{1,3},{2,0},{3,1},{4,6},{5,7},{6,4},{7,5},{8,10},{9,11},{10,... | collective-permute-start | bytes 393224 | tf_op jit(solution)/shard_map/ppermute | solution.py:104
  40.9 13.3 %collective-permute-start.13 = (f32[1,128,256]{1,2,0:T(8,128)S(1)}, f32[1,128,256]{1,2,0:T(8,128)S(1)}, u32[]{:S(2)}, u32[]{:S(2)}) collective-permute-start(f32[1,128,256]{1,2,0:T(8,128)S(1)} %get-tuple-element.103), channel_id=1, source_target_pairs={{0,1},{1,0},{2,3},{3,2},{4,5},{5,4},{6,7},{7,6},{8,9},{9,8},{10,11... | collective-permute-start | bytes 393224 | tf_op jit(solution)/shard_map/ppermute | solution.py:104
  41.5 12.6 %collective-permute-start.12 = (f32[1,128,256]{1,2,0:T(8,128)S(1)}, f32[1,128,256]{1,2,0:T(8,128)S(1)}, u32[]{:S(2)}, u32[]{:S(2)}) collective-permute-start(f32[1,128,256]{1,2,0:T(8,128)S(1)} %get-tuple-element.104), channel_id=1, source_target_pairs={{0,2},{1,3},{2,0},{3,1},{4,6},{5,7},{6,4},{7,5},{8,10},{9,11},{10,... | collective-permute-start | bytes 393224 | tf_op jit(solution)/shard_map/ppermute | solution.py:104
  43.0 11.8 %collective-permute-start.11 = (f32[1,128,256]{1,2,0:T(8,128)S(1)}, f32[1,128,256]{1,2,0:T(8,128)S(1)}, u32[]{:S(2)}, u32[]{:S(2)}) collective-permute-start(f32[1,128,256]{1,2,0:T(8,128)S(1)} %get-tuple-element.102), channel_id=1, source_target_pairs={{0,3},{1,2},{2,1},{3,0},{4,7},{5,6},{6,5},{7,4},{8,11},{9,10},{10,... | collective-permute-start | bytes 393224 | tf_op jit(solution)/shard_map/ppermute | solution.py:104
  47.0 13.3 %collective-permute-start.9 = (f32[1,128,256]{1,2,0:T(8,128)S(1)}, f32[1,128,256]{1,2,0:T(8,128)S(1)}, u32[]{:S(2)}, u32[]{:S(2)}) collective-permute-start(f32[1,128,256]{1,2,0:T(8,128)S(1)} %fusion.75), channel_id=1, source_target_pairs={{0,8},{1,12},{2,0},{3,4},{4,9},{5,13},{6,1},{7,5},{8,10},{9,14},{1... | collective-permute-start | bytes 393224 | tf_op jit(solution)/shard_map/ppermute | solution.py:104
  48.9 14.0 %collective-permute-start.10 = (f32[1,128,256]{1,2,0:T(8,128)S(1)}, f32[1,128,256]{1,2,0:T(8,128)S(1)}, u32[]{:S(2)}, u32[]{:S(2)}) collective-permute-start(f32[1,128,256]{1,2,0:T(8,128)S(1)} %fusion.75), channel_id=1, source_target_pairs={{0,12},{1,8},{2,4},{3,0},{4,13},{5,9},{6,5},{7,1},{8,14},{9,10},{1... | collective-permute-start | bytes 393224 | tf_op jit(solution)/shard_map/ppermute | solution.py:104
  54.1 9.5 %collective-permute-start.7 = (f32[1,128,256]{1,2,0:T(8,128)S(1)}, f32[1,128,256]{1,2,0:T(8,128)S(1)}, u32[]{:S(2)}, u32[]{:S(2)}) collective-permute-start(f32[1,128,256]{1,2,0:T(8,128)S(1)} %fusion.75), channel_id=1, source_target_pairs={{1,4},{2,8},{3,12},{4,1},{6,9},{7,13},{8,2},{9,6},{11,14},{12,3},{... | collective-permute-start | bytes 393224 | tf_op jit(solution)/shard_map/ppermute | solution.py:104
  54.9 9.5 %collective-permute-start.16 = (f32[1,128,256]{1,2,0:T(8,128)S(1)}, f32[1,128,256]{1,2,0:T(8,128)S(1)}, u32[]{:S(2)}, u32[]{:S(2)}) collective-permute-start(f32[1,128,256]{1,2,0:T(8,128)S(1)} %fusion.73), channel_id=1, source_target_pairs={{0,8},{1,12},{2,0},{3,4},{4,9},{5,13},{6,1},{7,5},{8,10},{9,14},{1... | collective-permute-start | bytes 393224 | tf_op jit(solution)/shard_map/ppermute | solution.py:104
  69.2 15.0 %collective-permute-start.20 = (f32[1,128,256]{1,2,0:T(8,128)S(1)}, f32[1,128,256]{1,2,0:T(8,128)S(1)}, u32[]{:S(2)}, u32[]{:S(2)}) collective-permute-start(f32[1,128,256]{1,2,0:T(8,128)S(1)} %bitcast.373), channel_id=1, source_target_pairs={{0,1},{1,0},{2,3},{3,2},{4,5},{5,4},{6,7},{7,6},{8,9},{9,8},{10,11... | collective-permute-start | bytes 393224 | tf_op jit(solution)/shard_map/ppermute | solution.py:104
  74.1 10.1 %collective-permute-start.19 = (f32[1,128,256]{1,2,0:T(8,128)S(1)}, f32[1,128,256]{1,2,0:T(8,128)S(1)}, u32[]{:S(2)}, u32[]{:S(2)}) collective-permute-start(f32[1,128,256]{1,2,0:T(8,128)S(1)} %bitcast.374), channel_id=1, source_target_pairs={{0,2},{1,3},{2,0},{3,1},{4,6},{5,7},{6,4},{7,5},{8,10},{9,11},{10,... | collective-permute-start | bytes 393224 | tf_op jit(solution)/shard_map/ppermute | solution.py:104
  99.0 11.5 %collective-permute-start.27 = (f32[1,128,256]{1,2,0:T(8,128)S(1)}, f32[1,128,256]{1,2,0:T(8,128)S(1)}, u32[]{:S(2)}, u32[]{:S(2)}) collective-permute-start(f32[1,128,256]{1,2,0:T(8,128)S(1)} %get-tuple-element.90), channel_id=1, source_target_pairs={{0,1},{1,0},{2,3},{3,2},{4,5},{5,4},{6,7},{7,6},{8,9},{9,8},{10,11... | collective-permute-start | bytes 393224 | tf_op jit(solution)/shard_map/ppermute | solution.py:104
  103.4 12.8 %collective-permute-start.26 = (f32[1,128,256]{1,2,0:T(8,128)S(1)}, f32[1,128,256]{1,2,0:T(8,128)S(1)}, u32[]{:S(2)}, u32[]{:S(2)}) collective-permute-start(f32[1,128,256]{1,2,0:T(8,128)S(1)} %get-tuple-element.91), channel_id=1, source_target_pairs={{0,2},{1,3},{2,0},{3,1},{4,6},{5,7},{6,4},{7,5},{8,10},{9,11},{10,... | collective-permute-start | bytes 393224 | tf_op jit(solution)/shard_map/ppermute | solution.py:104
  129.2 9.2 %collective-permute-start.35 = (f32[1,128,128]{2,1,0:T(8,128)S(1)}, f32[1,128,128]{2,1,0:T(8,128)S(1)}, u32[]{:S(2)}, u32[]{:S(2)}) collective-permute-start(f32[1,128,128]{2,1,0:T(8,128)S(1)} %get-tuple-element.125), channel_id=1, source_target_pairs={{0,1},{1,0},{2,3},{3,2},{4,5},{5,4},{6,7},{7,6},{8,9},{9,8},{10,11... | collective-permute-start | bytes 196616 | tf_op jit(solution)/shard_map/ppermute | solution.py:104
  152.7 9.2 %collective-permute-start.40 = (f32[1,512,128]{1,2,0:T(8,128)S(1)}, f32[1,512,128]{1,2,0:T(8,128)S(1)}, u32[]{:S(2)}, u32[]{:S(2)}) collective-permute-start(f32[1,512,128]{1,2,0:T(8,128)S(1)} %convolution_bitcast_fusion.2), channel_id=1, source_target_pairs={{0,1},{1,0},{2,3},{3,2},{4,5},{5,4},{6,7},{7,6},{8,9},{9,8},{10,11... | collective-permute-start | bytes 786440 | tf_op jit(solution)/shard_map/ppermute | solution.py:104
  162.0 10.9 %collective-permute-start.41 = (f32[1,512,128]{1,2,0:T(8,128)S(1)}, f32[1,512,128]{1,2,0:T(8,128)S(1)}, u32[]{:S(2)}, u32[]{:S(2)}) collective-permute-start(f32[1,512,128]{1,2,0:T(8,128)S(1)} %add.464), channel_id=1, source_target_pairs={{0,2},{1,3},{2,0},{3,1},{4,6},{5,7},{6,4},{7,5},{8,10},{9,11},{10,... | collective-permute-start | bytes 786440 | tf_op jit(solution)/shard_map/ppermute | solution.py:104
  214.3 11.2 %collective-permute-start.55 = (f32[1,128,256]{1,2,0:T(8,128)S(1)}, f32[1,128,256]{1,2,0:T(8,128)S(1)}, u32[]{:S(2)}, u32[]{:S(2)}) collective-permute-start(f32[1,128,256]{1,2,0:T(8,128)S(1)} %get-tuple-element.77), channel_id=1, source_target_pairs={{0,8},{1,9},{2,10},{3,11},{4,12},{5,13},{6,14},{7,15},{8,0},{9,1},... | collective-permute-start | bytes 393224 | tf_op jit(solution)/shard_map/ppermute | solution.py:104
  246.4 10.3 %collective-permute-start.64 = (f32[1,128,256]{1,2,0:T(8,128)}, f32[1,128,256]{1,2,0:T(8,128)}, u32[]{:S(2)}, u32[]{:S(2)}) collective-permute-start(f32[1,128,256]{1,2,0:T(8,128)} %get-tuple-element.33), channel_id=1, source_target_pairs={{0,8},{1,9},{2,10},{3,11},{4,12},{5,13},{6,14},{7,15},{8,0},{9,1},... | collective-permute-start | bytes 393224 | tf_op jit(solution)/shard_map/ppermute | solution.py:104
  277.7 16.1 %collective-permute-start.91 = (f32[1,128,256]{1,2,0:T(8,128)S(1)}, f32[1,128,256]{1,2,0:T(8,128)S(1)}, u32[]{:S(2)}, u32[]{:S(2)}) collective-permute-start(f32[1,128,256]{1,2,0:T(8,128)S(1)} %get-tuple-element.30), channel_id=1, source_target_pairs={{0,8},{1,9},{2,10},{3,11},{4,12},{5,13},{6,14},{7,15},{8,0},{9,1},... | collective-permute-start | bytes 393224 | tf_op jit(solution)/shard_map/ppermute | solution.py:104
  279.9 15.5 %collective-permute-start.75 = (f32[1,128,256]{1,2,0:T(8,128)S(1)}, f32[1,128,256]{1,2,0:T(8,128)S(1)}, u32[]{:S(2)}, u32[]{:S(2)}) collective-permute-start(f32[1,128,256]{1,2,0:T(8,128)S(1)} %get-tuple-element.25), channel_id=1, source_target_pairs={{0,4},{1,5},{2,6},{3,7},{4,0},{5,1},{6,2},{7,3},{8,12},{9,13},{10,... | collective-permute-start | bytes 393224 | tf_op jit(solution)/shard_map/ppermute | solution.py:104
  280.8 16.6 %collective-permute-start.74 = (f32[1,128,256]{1,2,0:T(8,128)S(1)}, f32[1,128,256]{1,2,0:T(8,128)S(1)}, u32[]{:S(2)}, u32[]{:S(2)}) collective-permute-start(f32[1,128,256]{1,2,0:T(8,128)S(1)} %get-tuple-element.26), channel_id=1, source_target_pairs={{0,12},{1,13},{2,14},{3,15},{4,8},{5,9},{6,10},{7,11},{8,4},{9,5},... | collective-permute-start | bytes 393224 | tf_op jit(solution)/shard_map/ppermute | solution.py:104
  285.1 12.3 %collective-permute-start.73 = (f32[1,128,256]{1,2,0:T(8,128)S(1)}, f32[1,128,256]{1,2,0:T(8,128)S(1)}, u32[]{:S(2)}, u32[]{:S(2)}) collective-permute-start(f32[1,128,256]{1,2,0:T(8,128)S(1)} %get-tuple-element.24), channel_id=1, source_target_pairs={{0,8},{1,9},{2,10},{3,11},{4,12},{5,13},{6,14},{7,15},{8,0},{9,1},... | collective-permute-start | bytes 393224 | tf_op jit(solution)/shard_map/ppermute | solution.py:104
  297.7 11.3 %collective-permute-start.78 = (f32[1,128,256]{1,2,0:T(8,128)S(1)}, f32[1,128,256]{1,2,0:T(8,128)S(1)}, u32[]{:S(2)}, u32[]{:S(2)}) collective-permute-start(f32[1,128,256]{1,2,0:T(8,128)S(1)} %add_subtract_fusion.1), channel_id=1, source_target_pairs={{0,3},{1,2},{2,1},{3,0},{4,7},{5,6},{6,5},{7,4},{8,11},{9,10},{10,... | collective-permute-start | bytes 393224 | tf_op jit(solution)/shard_map/ppermute | solution.py:104
  300.2 9.9 %collective-permute-start.76 = (f32[1,128,256]{1,2,0:T(8,128)S(1)}, f32[1,128,256]{1,2,0:T(8,128)S(1)}, u32[]{:S(2)}, u32[]{:S(2)}) collective-permute-start(f32[1,128,256]{1,2,0:T(8,128)S(1)} %add_subtract_fusion.1), channel_id=1, source_target_pairs={{0,1},{1,0},{2,3},{3,2},{4,5},{5,4},{6,7},{7,6},{8,9},{9,8},{10,11... | collective-permute-start | bytes 393224 | tf_op jit(solution)/shard_map/ppermute | solution.py:104
  315.8 12.3 %collective-permute-start.100 = (f32[1,128,256]{1,2,0:T(8,128)S(1)}, f32[1,128,256]{1,2,0:T(8,128)S(1)}, u32[]{:S(2)}, u32[]{:S(2)}) collective-permute-start(f32[1,128,256]{1,2,0:T(8,128)S(1)} %get-tuple-element.27), channel_id=1, source_target_pairs={{0,8},{1,9},{2,10},{3,11},{4,12},{5,13},{6,14},{7,15},{8,0},{9,1},... | collective-permute-start | bytes 393224 | tf_op jit(solution)/shard_map/ppermute | solution.py:104
  318.0 12.7 %collective-permute-start.84 = (f32[1,128,256]{1,2,0:T(8,128)S(1)}, f32[1,128,256]{1,2,0:T(8,128)S(1)}, u32[]{:S(2)}, u32[]{:S(2)}) collective-permute-start(f32[1,128,256]{1,2,0:T(8,128)S(1)} %get-tuple-element.22), channel_id=1, source_target_pairs={{0,4},{1,5},{2,6},{3,7},{4,0},{5,1},{6,2},{7,3},{8,12},{9,13},{10,... | collective-permute-start | bytes 393224 | tf_op jit(solution)/shard_map/ppermute | solution.py:104
  319.1 12.7 %collective-permute-start.83 = (f32[1,128,256]{1,2,0:T(8,128)S(1)}, f32[1,128,256]{1,2,0:T(8,128)S(1)}, u32[]{:S(2)}, u32[]{:S(2)}) collective-permute-start(f32[1,128,256]{1,2,0:T(8,128)S(1)} %get-tuple-element.23), channel_id=1, source_target_pairs={{0,12},{1,13},{2,14},{3,15},{4,8},{5,9},{6,10},{7,11},{8,4},{9,5},... | collective-permute-start | bytes 393224 | tf_op jit(solution)/shard_map/ppermute | solution.py:104
  322.3 9.5 %collective-permute-start.82 = (f32[1,128,256]{1,2,0:T(8,128)S(1)}, f32[1,128,256]{1,2,0:T(8,128)S(1)}, u32[]{:S(2)}, u32[]{:S(2)}) collective-permute-start(f32[1,128,256]{1,2,0:T(8,128)S(1)} %get-tuple-element.21), channel_id=1, source_target_pairs={{0,8},{1,9},{2,10},{3,11},{4,12},{5,13},{6,14},{7,15},{8,0},{9,1},... | collective-permute-start | bytes 393224 | tf_op jit(solution)/shard_map/ppermute | solution.py:104
  (87 other events, 674.9 us)
